TPU v7x, 32 devices: a whole 2x2x4 slice. The times are simulated.
32 devices in a mesh: dp: 8 (over y, x, core), mp: 4 (over z).
Axes of the slice: x: 2, y: 2, z: 4, core: 2. Of those that a mesh axis runs over, the one named last changes fastest.
Arguments:
- tokens: bfloat16 [2048, 2048], P('dp'), may hold values from -6 to 6
- lengths: int32 [8, 4], P('dp'), may hold values from 0 to 256, as said below
- ln_gain: float32 [2048], replicated, may hold values from 0.5 to 1.5
- ln_bias: float32 [2048], replicated, may hold values from -3 to 3
- w_query: bfloat16 [2048, 2048], P(None, 'mp'), may hold values from -0.125 to 0.125
- b_query: float32 [2048], P('mp'), may hold values from -3 to 3
- w_key: bfloat16 [2048, 2048], P(None, 'mp'), may hold values from -0.125 to 0.125
- b_key: float32 [2048], P('mp'), may hold values from -3 to 3
- w_value: bfloat16 [2048, 2048], P(None, 'mp'), may hold values from -0.125 to 0.125
- b_value: float32 [2048], P('mp'), may hold values from -3 to 3
- w_out: bfloat16 [2048, 2048], P('mp'), may hold values from -0.375 to 0.375
- w_up: bfloat16 [2048, 8192], P(None, 'mp'), may hold values from -0.125 to 0.125
- b_up: float32 [8192], P('mp'), may hold values from -3 to 3
- w_down: bfloat16 [8192, 2048], P('mp'), may hold values from -0.0625 to 0.0625
- out_bias: float32 [2048], replicated, may hold values from -3 to 3
- cotangent: bfloat16 [2048, 2048], P('dp'), may hold values from -6 to 6
Outputs:
- mixed: bfloat16 [2048, 2048], P('dp')
- grad_tokens: bfloat16 [2048, 2048], P('dp')
- grad_ln_gain: float32 [2048], P('dp')
- grad_ln_bias: float32 [2048], P('dp')
- grad_w_query: float32 [2048, 2048], P('dp', 'mp')
- grad_b_query: float32 [2048], P('mp')
- grad_w_key: float32 [2048, 2048], P('dp', 'mp')
- grad_b_key: float32 [2048], P('mp')
- grad_w_value: float32 [2048, 2048], P('dp', 'mp')
- grad_b_value: float32 [2048], P('mp')
- grad_w_out: float32 [2048, 2048], P('mp', 'dp')
- grad_w_up: float32 [2048, 8192], P('dp', 'mp')
- grad_b_up: float32 [8192], P('mp')
- grad_w_down: float32 [8192, 2048], P('mp', 'dp')
- grad_out_bias: float32 [2048], P('dp')
Inputs may be any that keep to these rules, and one draw needn't show every extreme that they name: `lengths`: row g lists the sequences that the group g of 256 slots packs, used slots first, each used length at least 64, unused slots 0; a row sums to 256 or less; some row holds a single sequence of 256.
All inputs are finite; a program needn't handle non-finite values.
Results may differ from a plain program's by a relative error of at most 0.015.
Values may be sent and summed in bfloat16 or wider, within the bound.
A program may use at most 192 MiB of HBM per device.

v0:
```python
import jax
import jax.numpy as jnp
from jax import lax
from jax.sharding import PartitionSpec as P

HD = 64
ROT = 32


EPSILON = 1e-05


def layer_norm(inputs, gain_vec, shift_vec):
    center = inputs - jnp.mean(inputs, axis=-1, keepdims=True)
    spread = jnp.mean(center * center, axis=-1, keepdims=True)
    return center * lax.rsqrt(spread + EPSILON) * gain_vec + shift_vec


def gelu_tanh(inputs):
    return jax.nn.gelu(inputs, approximate=True)


def token_layout(lens_row, tok_count):
    ends = jnp.cumsum(lens_row)
    starts_at = ends - lens_row
    places = jnp.arange(tok_count, dtype=jnp.int32)
    inside = (places[:, None] >= starts_at[None, :]) & (places[:, None] < ends[None, :])
    inside_int = inside.astype(jnp.int32)
    numbers = jnp.arange(1, lens_row.shape[0] + 1, dtype=jnp.int32)
    segment = jnp.sum(inside_int * numbers[None, :], axis=1) - 1
    offset = places - jnp.sum(inside_int * starts_at[None, :], axis=1)
    return (segment, offset, segment >= 0)


def rotary_tables(offset):
    freq = 10000.0 ** (-jnp.arange(0, ROT, 2, dtype=jnp.float32) / ROT)
    angle = offset.astype(jnp.float32)[:, None] * freq[None, :]
    return (jnp.cos(angle)[:, None, :], jnp.sin(angle)[:, None, :])


def rotate(field, cosine, sine):
    half = cosine.shape[-1]
    first = field[..., :half]
    second = field[..., half : 2 * half]
    return jnp.concatenate(
        [first * cosine - second * sine, second * cosine + first * sine, field[..., 2 * half :]],
        axis=-1,
    )


def masked_scores(query_low, key_low, segment, first_row, block_rows):
    scores = (
        jnp.einsum("qhd,khd->hqk", query_low, key_low, preferred_element_type=jnp.float32) * 0.125
    )
    place_rows = first_row + jnp.arange(block_rows, dtype=jnp.int32)
    place_cols = jnp.arange(key_low.shape[0], dtype=jnp.int32)
    allowed = (segment[:, None] == segment[None, :]) & (place_cols[None, :] <= place_rows[:, None])
    return jnp.where(allowed[None], scores, -1e30)


def contract_rows(left, right):
    return lax.dot_general(
        left, right, (((0,), (0,)), ((), ())), preferred_element_type=jnp.float32
    )


def contract_cols(left, right):
    return lax.dot_general(
        left, right, (((1,), (1,)), ((), ())), preferred_element_type=jnp.float32
    )


def body(
    tokens,
    lengths,
    ln_gain,
    ln_bias,
    w_query,
    b_query,
    w_key,
    b_key,
    w_value,
    b_value,
    w_out,
    w_up,
    b_up,
    w_down,
    out_bias,
    cotangent,
):
    tok_count = tokens.shape[0]
    local_width = w_query.shape[1]
    head_count = local_width // HD
    segment, offset, is_valid = token_layout(lengths[0], tok_count)
    cosine, sine = rotary_tables(offset)
    tokens_f = tokens.astype(jnp.float32)
    normed, norm_back = jax.vjp(layer_norm, tokens_f, ln_gain, ln_bias)
    normed_low = normed.astype(jnp.bfloat16)

    def project(weight, offset_vec):
        return jnp.dot(normed_low, weight, preferred_element_type=jnp.float32) + offset_vec

    queries = project(w_query, b_query).reshape(tok_count, head_count, HD)
    key_rows = project(w_key, b_key).reshape(tok_count, head_count, HD)
    turned_q, turn_q_back = jax.vjp(lambda field: rotate(field, cosine, sine), queries)
    turned_k, turn_k_back = jax.vjp(lambda field: rotate(field, cosine, sine), key_rows)
    query_low = turned_q.astype(jnp.bfloat16)
    key_low = turned_k.astype(jnp.bfloat16)
    value_low = project(w_value, b_value).reshape(tok_count, head_count, HD).astype(jnp.bfloat16)
    block_rows = min(512, tok_count)
    firsts = list(range(0, tok_count, block_rows))
    pieces = []
    log_sums = []
    for first_row in firsts:
        masked = masked_scores(query_low, key_low, segment, first_row, block_rows)
        row_top = jnp.max(masked, axis=-1, keepdims=True)
        expo = jnp.exp(masked - row_top)
        totals = jnp.sum(expo, axis=-1, keepdims=True)
        probs = (expo / totals).astype(jnp.bfloat16)
        pieces.append(
            jnp.einsum("hqk,khd->qhd", probs, value_low, preferred_element_type=jnp.float32)
        )
        log_sums.append(row_top + jnp.log(totals))
    attended_low = pieces[0].reshape(tok_count, local_width).astype(jnp.bfloat16)
    partial_out = jnp.dot(attended_low, w_out, preferred_element_type=jnp.float32)
    upward = project(w_up, b_up)
    activated, act_back = jax.vjp(gelu_tanh, upward)
    activated_low = activated.astype(jnp.bfloat16)
    partial_out = partial_out + jnp.dot(activated_low, w_down, preferred_element_type=jnp.float32)
    total = lax.psum(partial_out, "mp")
    mixed = (tokens_f + jnp.where(is_valid[:, None], total + out_bias, 0.0)).astype(jnp.bfloat16)
    grad_low = jnp.where(is_valid[:, None], cotangent, jnp.zeros_like(cotangent))
    grad_bias_out = jnp.sum(grad_low.astype(jnp.float32), axis=0)
    grad_down = contract_rows(activated_low, grad_low)
    act_grad = contract_cols(grad_low, w_down)
    up_grad = act_back(act_grad)[0].astype(jnp.bfloat16)
    grad_bias_up = jnp.sum(up_grad.astype(jnp.float32), axis=0)
    grad_up = contract_rows(normed_low, up_grad)
    normed_grad = contract_cols(up_grad, w_up)
    grad_outproj = contract_rows(attended_low, grad_low)
    att_grad = (
        contract_cols(grad_low, w_out).astype(jnp.bfloat16).reshape(tok_count, head_count, HD)
    )
    query_parts = []
    key_grad = jnp.zeros((tok_count, head_count, HD), jnp.float32)
    value_grad = jnp.zeros((tok_count, head_count, HD), jnp.float32)
    for index_block, first_row in enumerate(firsts):
        masked = masked_scores(query_low, key_low, segment, first_row, block_rows)
        probs_f = jnp.exp(masked - log_sums[index_block])
        probs_low = probs_f.astype(jnp.bfloat16)
        prob_grad = jnp.einsum(
            "qhd,khd->hqk", att_grad, value_low, preferred_element_type=jnp.float32
        )
        row_delta = jnp.sum(probs_f * prob_grad, axis=-1, keepdims=True)
        score_grad = (probs_f * (prob_grad - row_delta)).astype(jnp.bfloat16)
        query_parts.append(
            jnp.einsum("hqk,khd->qhd", score_grad, key_low, preferred_element_type=jnp.float32)
            * 0.125
        )
        key_grad = (
            jnp.einsum("hqk,qhd->khd", score_grad, query_low, preferred_element_type=jnp.float32)
            * 0.125
        )
        value_grad = jnp.einsum(
            "hqk,qhd->khd", probs_low, att_grad, preferred_element_type=jnp.float32
        )
    query_grad = turn_q_back(query_parts[0])[0].reshape(tok_count, local_width).astype(jnp.bfloat16)
    key_grad_low = turn_k_back(key_grad)[0].reshape(tok_count, local_width).astype(jnp.bfloat16)
    value_grad_low = value_grad.reshape(tok_count, local_width).astype(jnp.bfloat16)
    grad_query = contract_rows(normed_low, query_grad)
    grad_key = contract_rows(normed_low, key_grad_low)
    grad_value = contract_rows(normed_low, value_grad_low)
    normed_grad = (
        normed_grad
        + contract_cols(query_grad, w_query)
        + contract_cols(key_grad_low, w_key)
        + contract_cols(value_grad_low, w_value)
    )
    normed_grad = lax.psum(normed_grad, "mp")
    input_grad, grad_gain, grad_shift = norm_back(normed_grad)
    grad_tokens = (cotangent.astype(jnp.float32) + input_grad).astype(jnp.bfloat16)
    bias_q, bias_k, bias_v, bias_up = lax.psum(
        (
            jnp.sum(query_grad.astype(jnp.float32), axis=0),
            jnp.sum(key_grad_low.astype(jnp.float32), axis=0),
            jnp.sum(value_grad_low.astype(jnp.float32), axis=0),
            grad_bias_up,
        ),
        "dp",
    )
    sent_q, sent_k, sent_v, sent_out, sent_up, sent_down, sent_gain, sent_shift, sent_bias = (
        lax.psum_scatter(grad_query, "dp", scatter_dimension=0, tiled=True),
        lax.psum_scatter(grad_key, "dp", scatter_dimension=0, tiled=True),
        lax.psum_scatter(grad_value, "dp", scatter_dimension=0, tiled=True),
        lax.psum_scatter(grad_outproj, "dp", scatter_dimension=1, tiled=True),
        lax.psum_scatter(grad_up, "dp", scatter_dimension=0, tiled=True),
        lax.psum_scatter(grad_down, "dp", scatter_dimension=1, tiled=True),
        lax.psum_scatter(grad_gain, "dp", scatter_dimension=0, tiled=True),
        lax.psum_scatter(grad_shift, "dp", scatter_dimension=0, tiled=True),
        lax.psum_scatter(grad_bias_out, "dp", scatter_dimension=0, tiled=True),
    )
    return (
        mixed,
        grad_tokens,
        sent_gain,
        sent_shift,
        sent_q,
        bias_q,
        sent_k,
        bias_k,
        sent_v,
        bias_v,
        sent_out,
        sent_up,
        bias_up,
        sent_down,
        sent_bias,
    )


def solution(mesh):
    in_specs = (
        P("dp", None),
        P("dp", None),
        P(),
        P(),
        P(None, "mp"),
        P("mp"),
        P(None, "mp"),
        P("mp"),
        P(None, "mp"),
        P("mp"),
        P("mp", None),
        P(None, "mp"),
        P("mp"),
        P("mp", None),
        P(),
        P("dp", None),
    )
    out_specs = (
        P("dp", None),
        P("dp", None),
        P("dp"),
        P("dp"),
        P("dp", "mp"),
        P("mp"),
        P("dp", "mp"),
        P("mp"),
        P("dp", "mp"),
        P("mp"),
        P("mp", "dp"),
        P("dp", "mp"),
        P("mp"),
        P("mp", "dp"),
        P("dp"),
    )
    return jax.shard_map(body, mesh=mesh, in_specs=in_specs, out_specs=out_specs, check_vma=False)
```

profile of v0, /device:TPU:0, one launch (start us, length us, event | category | flops | bytes accessed | tf_op | source)
XLA Modules:
  0.0 541.5 jit_solution(5144197644415522230)
XLA Ops:
  8.1 0.5 multiply_power_fusion
  8.7 0.8 reduce-window.4
  9.5 0.7 fusion.29
  10.3 0.6 subtract_convert_fusion.2
  10.8 1.4 convert_reduce_fusion
  12.3 1.6 fusion.16
  13.9 0.6 copy-done.34
  14.5 0.7 fusion.26
  15.2 3.1 fusion.23
  18.3 1.1 copy.61
  19.4 3.5 convolution_convert_fusion.1
  22.9 1.8 copy.65
  24.7 3.2 convolution_add_fusion.5
  27.9 2.0 copy.63
  29.9 1.0 slice.42
  30.9 2.3 convolution_add_fusion.6
  33.1 2.0 copy.62
  35.2 1.0 slice.43
  36.1 0.8 multiply_cosine_fusion
  37.0 1.2 subtract_convert_fusion.1
  38.2 1.4 fusion.51
  39.9 0.5 convolution_convert_fusion.2
  40.4 0.4 copy-done.11
  40.8 1.1 convert_reduce_fusion.3
  42.0 0.6 multiply_reduce_fusion
  42.6 0.5 multiply_convert_fusion
  43.0 0.4 fusion.21
  43.5 0.3 fusion.22
  44.1 1.8 slice-done.5
  46.0 2.5 convolution_add_fusion.4
  48.8 3.8 convert_reduce_fusion.2
  52.6 2.6 fusion.34
  55.2 5.8 %fusion.52 = f32[256,2048]{1,0:T(8,128)S(1)} fusion(bf16[256,2048]{1,0:T(8,128)(2,1)S(1)} %get-tuple-element.58, bf16[2048,2048]{1,0:T(8,128)(2,1)} %param.27), kind=kOutput, calls=%fused_computation.108 | convolution fusion | flops 2147483648 | bytes 11534336 | tf_op jit(solution)/shard_map/dot_general | solution.py:68
  61.2 0.8 convolution_add_fusion.2
  62.4 0.6 copy-done.12
  63.0 0.8 convolution_add_fusion.1
  63.8 0.8 copy-done.13
  64.6 2.1 convolution_add_fusion
  66.7 2.0 convolution_add_fusion.3
  68.8 1.1 copy-done.5
  70.0 2.7 fusion.36
  72.8 0.6 copy-done.29
  73.5 2.8 fusion.40
  76.4 0.9 copy-done.10
  77.3 2.9 fusion.42
  80.2 0.9 copy-done.8
  81.1 3.0 fusion.44
  84.4 10.3 %fusion.33 = f32[2048,2048]{1,0:T(8,128)} fusion(f32[256,2048]{1,0:T(8,128)} %copy-done.18, bf16[256,2048]{1,0:T(8,128)(2,1)S(1)} %copy-done.5, pred[256]{0:T(512)(128)(4,1)S(1)} %copy-done.38), kind=kOutput, calls=%fused_computation.97 | convolution fusion | flops 2152726528 | bytes 19923200 | tf_op jit(solution)/shard_map/dot_general | solution.py:62
  94.7 1.1 copy-done.21
  95.9 8.3 %fusion.38 = f32[2048,2048]{1,0:T(8,128)} fusion(bf16[256,2048]{1,0:T(8,128)(2,1)S(1)} %copy-done.21, bf16[256,2048]{1,0:T(8,128)(2,1)S(1)} %copy-done.2, f32[2048]{0:T(1024)S(1)} %copy-done.26, f32[2048]{0:T(1024)S(1)} %copy-done.19, f32[256]{0:T(256)S(1)} %copy-done.32, f32[256]{0:T(256)S(1)} %copy-done.29), kind=kOutput, calls=%fused_computation.102 | convolution fusion | flops 2150629376 | bytes 18892800 | tf_op jit(solution)/shard_map/dot_general | solution.py:62
  104.2 0.6 copy-done.33
  105.1 0.6 dynamic-slice
  106.3 120.6 %all-reduce.13.cloned.1.call-done = (f32[256,2048]{1,0:T(8,128)}, f32[256,2048]{1,0:T(8,128)}) async-done(((f32[256,2048]{1,0:T(8,128)}, f32[256,2048]{1,0:T(8,128)}), (f32[256,2048]{1,0:T(8,128)}, f32[256,2048]{1,0:T(8,128)})) %all-reduce.13.cloned.1.call-update) | async-done | bytes 4194320 | tf_op jit(solution)/shard_map/psum | solution.py:130
  227.0 2.3 fusion.50
  229.3 1.0 fusion.8
  230.5 0.7 copy-done.15
  231.2 2.5 convert_reduce_fusion.1
  233.7 25.2 %all-reduce.9 = (f32[2048]{0:T(1024)S(1)}, f32[2048]{0:T(1024)S(1)}, f32[512]{0:T(512)}, f32[512]{0:T(512)}, f32[512]{0:T(512)}, /*index=5*/f32[2048]{0:T(1024)}, f32[2048]{0:T(1024)S(1)}) all-reduce(f32[2048]{0:T(1024)S(1)} %get-tuple-element.15, f32[2048]{0:T(1024)S(1)} %get-tuple-element.17, ...), channel_id=2, replica_groups=mesh['dp'=8,'mp'=4] {'dp'}, use_global_device_ids=true, to_apply=%region_13.14.clone | all-reduce | flops 9728 | bytes 77824
  258.8 0.6 dynamic-slice.1
  259.5 0.6 dynamic-slice.3
  260.1 0.6 dynamic-slice.5
  260.7 32.5 %reduce-scatter.7.cloned.1.call-done = f32[256,512]{1,0:T(8,128)} async-done(((f32[2048,512]{1,0:T(8,128)}), f32[256,512]{1,0:T(8,128)}) %reduce-scatter.7.cloned.1.call-update) | async-done | bytes 524304 | tf_op jit(solution)/shard_map/reduce_scatter | solution.py:192
  293.2 120.4 %reduce-scatter.17.cloned.1.call-done = f32[2048,256]{1,0:T(8,128)} async-done(((f32[2048,2048]{1,0:T(8,128)}), f32[2048,256]{1,0:T(8,128)}) %reduce-scatter.17.cloned.1.call-update) | async-done | bytes 2097168 | tf_op jit(solution)/shard_map/reduce_scatter | solution.py:197
  413.6 120.4 %reduce-scatter.15.cloned.1.call-done = f32[256,2048]{1,0:T(8,128)} async-done(((f32[2048,2048]{1,0:T(8,128)}), f32[256,2048]{1,0:T(8,128)}) %reduce-scatter.15.cloned.1.call-update) | async-done | bytes 2097168 | tf_op jit(solution)/shard_map/reduce_scatter | solution.py:196
  (120 shorter events, 2.8 us)
Async XLA Ops:
  8.0 22.9 %copy-start = (bf16[2048,512]{1,0:T(8,128)(2,1)S(1)}, bf16[2048,512]{1,0:T(8,128)(2,1)}, u32[]{:S(2)}) copy-start(bf16[2048,512]{1,0:T(8,128)(2,1)} %param.20) | copy-start | bytes 6291460
  8.0 7.2 %copy-start.2 = (bf16[256,2048]{1,0:T(8,128)(2,1)S(1)}, bf16[256,2048]{1,0:T(8,128)(2,1)}, u32[]{:S(2)}) copy-start(bf16[256,2048]{1,0:T(8,128)(2,1)} %param.16) | copy-start | bytes 3145732
  8.0 7.2 %copy-start.19 = (f32[2048]{0:T(1024)S(1)}, f32[2048]{0:T(1024)}, u32[]{:S(2)}) copy-start(f32[2048]{0:T(1024)} %param.18) | copy-start | bytes 24580
  8.1 7.2 %copy-start.26 = (f32[2048]{0:T(1024)S(1)}, f32[2048]{0:T(1024)}, u32[]{:S(2)}) copy-start(f32[2048]{0:T(1024)} %param.19) | copy-start | bytes 24580
  8.1 7.2 %copy-start.40 = (f32[512]{0:T(512)S(1)}, f32[512]{0:T(512)}, u32[]{:S(2)}) copy-start(f32[512]{0:T(512)} %param.25) | copy-start | bytes 6148
  8.1 218.9 %all-reduce.13.cloned.1.call-start = ((), (), s32[]{:S(2)}) async-start(), calls=%async_computation.12 | async-start | bytes 8388608 | tf_op jit(solution)/shard_map/psum | solution.py:130
  10.2 9.2 %copy-start.37 = (pred[256]{0:T(512)(128)(4,1)}, pred[256]{0:T(512)(128)(4,1)S(1)}, u32[]{:S(2)}) copy-start(pred[256]{0:T(512)(128)(4,1)S(1)} %broadcast_compare_fusion) | copy-start | bytes 772
  12.3 12.4 %copy-start.27 = (f32[256]{0:T(256)}, f32[256]{0:T(256)S(1)}, u32[]{:S(2)}) copy-start(f32[256]{0:T(256)S(1)} %broadcast_multiply_fusion) | copy-start | bytes 3076
  13.9 0.6 copy-start.34
  14.5 10.2 %copy-start.30 = (f32[256]{0:T(256)}, f32[256]{0:T(256)S(1)}, u32[]{:S(2)}) copy-start(f32[256]{0:T(256)S(1)} %fusion.28) | copy-start | bytes 3076
  19.4 20.4 %copy-start.24 = (bf16[256,512]{0,1:T(8,128)(2,1)}, bf16[256,512]{0,1:T(8,128)(2,1)S(1)}, u32[]{:S(2)}) copy-start(bf16[256,512]{0,1:T(8,128)(2,1)S(1)} %copy.61) | copy-start | bytes 786436
  19.4 5.3 copy-start.41
  39.9 1.0 copy-start.11
  40.4 26.4 %copy-start.22 = (bf16[8,64,256]{2,1,0:T(8,128)(2,1)}, bf16[8,64,256]{2,1,0:T(8,128)(2,1)S(1)}, u32[]{:S(2)}) copy-start(bf16[8,64,256]{2,1,0:T(8,128)(2,1)S(1)} %convolution_convert_fusion.2) | copy-start | bytes 786436
  40.4 1.6 copy-start.25
  41.9 2.2 slice-start.4
  42.5 3.4 slice-start.5
  43.5 5.0 copy-start.16
  43.5 2.5 copy-start.28
  43.5 2.5 copy-start.31
  43.5 2.5 copy-start.39
  43.8 4.7 copy-start.17
  43.8 4.7 slice-start.2
  46.0 2.6 copy-start.4
  46.0 2.6 copy-start.38
  46.0 2.8 slice-start.3
  48.8 3.8 copy-start.18
  52.6 2.6 copy-start.20
  55.2 5.8 %slice-start.1 = ((f32[256,8,64]{0,2,1:T(8,128)}), f32[256,8,32]{0,2,1:T(8,128)S(1)}, s32[]{:S(2)}) async-start(f32[256,8,64]{0,2,1:T(8,128)} %copy-done.17), calls=%async_computation.14 | async-start | bytes 524288 | tf_op jit(solution)/shard_map/transpose(jvp())/split | solution.py:45
  61.2 0.8 copy-start.7
  61.2 1.0 slice-start
  61.2 1.8 copy-start.12
  62.4 1.4 copy-start.9
  63.0 1.6 copy-start.13
  64.6 2.1 copy-start.14
  68.8 1.2 copy-start.5
  68.8 1.3 copy-start.23
  68.8 191.9 %reduce-scatter.13.cloned.1.call-start = ((), (), s32[]{:S(2)}) async-start(), calls=%async_computation.9 | async-start | bytes 4718592 | tf_op jit(solution)/shard_map/reduce_scatter | solution.py:195
  72.8 0.7 copy-start.29
  72.8 0.7 copy-start.32
  72.8 187.9 %reduce-scatter.11.cloned.1.call-start = ((), (), s32[]{:S(2)}) async-start(), calls=%async_computation.8 | async-start | bytes 4718592 | tf_op jit(solution)/shard_map/reduce_scatter | solution.py:194
  76.3 1.0 copy-start.10
  76.3 184.4 %reduce-scatter.9.cloned.1.call-start = ((), (), s32[]{:S(2)}) async-start(), calls=%async_computation.7 | async-start | bytes 4718592 | tf_op jit(solution)/shard_map/reduce_scatter | solution.py:193
  80.2 0.9 copy-start.8
  80.2 213.0 %reduce-scatter.7.cloned.1.call-start = ((), (), s32[]{:S(2)}) async-start(), calls=%async_computation.6 | async-start | bytes 4718592 | tf_op jit(solution)/shard_map/reduce_scatter | solution.py:192
  84.1 329.6 %reduce-scatter.17.cloned.1.call-start = ((), (), s32[]{:S(2)}) async-start(), calls=%async_computation.11 | async-start | bytes 18874368 | tf_op jit(solution)/shard_map/reduce_scatter | solution.py:197
  94.6 1.2 copy-start.21
  94.7 439.4 %reduce-scatter.15.cloned.1.call-start = ((), (), s32[]{:S(2)}) async-start(), calls=%async_computation.10 | async-start | bytes 18874368 | tf_op jit(solution)/shard_map/reduce_scatter | solution.py:196
  104.2 0.7 copy-start.33
  104.2 0.9 copy-start.42
  104.2 125.1 %copy-start.35 = (f32[256]{0:T(256)S(1)}, f32[256]{0:T(256)}, u32[]{:S(2)}) copy-start(f32[256]{0:T(256)} %copy-done.34) | copy-start | bytes 3076
  227.0 2.3 copy-start.3
  229.2 1.2 copy-start.6
  229.2 1.9 copy-start.15
  229.3 1.9 copy-start.36
  231.2 302.9 %copy-start.1 = (bf16[2048,512]{1,0:T(8,128)(2,1)S(1)}, bf16[2048,512]{1,0:T(8,128)(2,1)}, u32[]{:S(2)}) copy-start(bf16[2048,512]{1,0:T(8,128)(2,1)} %param.20) | copy-start | bytes 6291460
Sparse Core Ops, SparseCore 0:
  68.9 158.0 all-reduce.12
Sparse Core Ops, SparseCore 1:
  73.6 53.8 reduce-scatter.12
  131.3 51.2 reduce-scatter.10
  186.7 51.1 reduce-scatter.8
  241.9 51.3 reduce-scatter.6
  297.8 115.8 reduce-scatter.16
  418.2 115.8 reduce-scatter.14
where the time goes:
time: 542 us
  waiting for transfers between devices  394 us (73%)
  matrix products  66.6 us (12%)
  blocking collectives  25.2 us (5%)
  local copies, waits for them, and re-layouts  22.9 us (4%)
  between operations  16.8 us (3%)
  other arithmetic  15.4 us (3%)
    psum x1, waiting for transfers between devices, body(): total = lax.psum(partial_out, 'mp')  121 us
    reduce_scatter x1, waiting for transfers between devices, body(): lax.psum_scatter(grad_down, 'dp', scatter_dimension=1, tiled=True)  120 us
    reduce_scatter x1, waiting for transfers between devices, body(): lax.psum_scatter(grad_up, 'dp', scatter_dimension=0, tiled=True)  120 us
    reduce_scatter x1, waiting for transfers between devices, body(): lax.psum_scatter(grad_query, 'dp', scatter_dimension=0, tiled=True)  32.5 us
    dot_general x6, matrix products, contract_rows(): lax.dot_general(left, right, (((0,), (0,)), ((), ())), preferred_element_...  30 us
    unnamed x1, blocking collectives  25.2 us
    dot_general x6, matrix products, contract_cols(): lax.dot_general(left, right, (((1,), (1,)), ((), ())), preferred_element_...  16.7 us
    unnamed x98, local copies, waits for them, and re-layouts  13.6 us
  transfers between devices with their start and end apart: 7, of which 4 were waited for; matrix products, arithmetic and copies ran while one was open for 7% of the time, Pallas kernels for 0%

commit v1 on v0

v1 whole, which is shorter than its diff:
```python
import jax
import jax.numpy as jnp
from jax import lax
from jax.sharding import PartitionSpec as P

HD = 64
ROT = 32
EPSILON = 1e-05


def token_layout(lens_row, tok_count):
    ends = jnp.cumsum(lens_row)
    starts_at = ends - lens_row
    places = jnp.arange(tok_count, dtype=jnp.int32)
    inside = (places[:, None] >= starts_at[None, :]) & (places[:, None] < ends[None, :])
    inside_int = inside.astype(jnp.int32)
    numbers = jnp.arange(1, lens_row.shape[0] + 1, dtype=jnp.int32)
    segment = jnp.sum(inside_int * numbers[None, :], axis=1) - 1
    offset = places - jnp.sum(inside_int * starts_at[None, :], axis=1)
    return (segment, offset, segment >= 0)


def rotary_tables(offset):
    freq = 10000.0 ** (-jnp.arange(0, ROT, 2, dtype=jnp.float32) / ROT)
    angle = offset.astype(jnp.float32)[:, None] * freq[None, :]
    return (jnp.cos(angle)[:, None, :], jnp.sin(angle)[:, None, :])


def rotate(field, cosine, sine):
    half = cosine.shape[-1]
    first = field[..., :half]
    second = field[..., half : 2 * half]
    return jnp.concatenate(
        [first * cosine - second * sine, second * cosine + first * sine, field[..., 2 * half :]],
        axis=-1,
    )


def dot(left, right, dims):
    return lax.dot_general(left, right, (dims, ((), ())), preferred_element_type=jnp.float32)


def span(bits):
    out = [0]
    for bit in bits:
        out = out + [value | bit for value in out]
    return out


def make_body(n_dp, n_mp):
    low_bits = [1 << i for i in range(n_dp.bit_length() - 1)]
    rest = low_bits[1:]
    half = len(rest) // 2
    first_bits, second_bits = rest[:half], rest[half:]
    core_bits = low_bits[:1]

    def swap(value, mask):
        return lax.ppermute(value, "dp", [(i, i ^ mask) for i in range(n_dp)])

    def gather(value, bits):
        pieces = [value]
        for bit in bits:
            pieces = pieces + [swap(piece, bit) for piece in pieces]
        return pieces

    def to_others(blocks):
        me = lax.axis_index("mp")
        received = []
        for delta in range(1, n_mp):
            block = lax.dynamic_index_in_dim(blocks, lax.rem(me + delta, n_mp), 0, keepdims=False)
            received.append(
                lax.ppermute(block, "mp", [(i, (i + delta) % n_mp) for i in range(n_mp)])
            )
        own = lax.dynamic_index_in_dim(blocks, me, 0, keepdims=False)
        return own, received

    def share_rows(block):
        me = lax.axis_index("mp")
        out = jnp.zeros((n_mp,) + block.shape, block.dtype)
        out = lax.dynamic_update_index_in_dim(out, block, me, 0)
        for delta in range(1, n_mp):
            other = lax.ppermute(block, "mp", [(i, (i + delta) % n_mp) for i in range(n_mp)])
            out = lax.dynamic_update_index_in_dim(out, other, lax.rem(me - delta + n_mp, n_mp), 0)
        return out.reshape((-1,) + block.shape[1:])

    def body(
        tokens,
        lengths,
        ln_gain,
        ln_bias,
        w_query,
        b_query,
        w_key,
        b_key,
        w_value,
        b_value,
        w_out,
        w_up,
        b_up,
        w_down,
        out_bias,
        cotangent,
    ):
        tok_count, width = tokens.shape
        local_width = w_query.shape[1]
        head_count = local_width // HD
        me = lax.axis_index("dp")
        zed = lax.axis_index("mp")
        own_cols = width // n_dp
        segment, offset, is_valid = token_layout(lengths[0], tok_count)
        cosine, sine = rotary_tables(offset)
        tokens_f = tokens.astype(jnp.float32)
        center = tokens_f - jnp.mean(tokens_f, axis=-1, keepdims=True)
        spread = jnp.mean(center * center, axis=-1, keepdims=True)
        inv_dev = lax.rsqrt(spread + EPSILON)
        standard = center * inv_dev
        normed_low = (standard * ln_gain + ln_bias).astype(jnp.bfloat16)
        grad_low = jnp.where(is_valid[:, None], cotangent, jnp.zeros_like(cotangent))

        def columns_for(value, owner):
            return lax.dynamic_slice_in_dim(value, owner * own_cols, own_cols, 1)

        def exchange_side(value, gather_bits, reduce_bits):
            pieces = []
            for offset_j in span(gather_bits):
                block = jnp.concatenate(
                    [columns_for(value, me ^ (offset_j ^ m)) for m in span(reduce_bits)], axis=1
                )
                pieces.append(swap(block, offset_j) if offset_j else block)
            return jnp.concatenate(pieces, axis=0)

        bits_n = (first_bits + core_bits, second_bits)
        bits_g = (second_bits + core_bits, first_bits)
        side_g = exchange_side(grad_low, *bits_g)
        side_n = exchange_side(normed_low, *bits_n)

        def weight_grad(pieces, side, reduce_bits, rows_first):
            many = jnp.concatenate(pieces, axis=0)
            total = None
            for at, m in enumerate(span(reduce_bits)):
                part = side[:, at * own_cols : (at + 1) * own_cols]
                if rows_first:
                    product = dot(part, many, ((0,), (0,)))
                else:
                    product = dot(many, part, ((0,), (0,)))
                if m == 0:
                    total = product
                else:
                    total = total + swap(product.astype(jnp.bfloat16), m).astype(jnp.float32)
            return total

        upward = dot(normed_low, w_up, ((1,), (0,))) + b_up
        activated, act_back = jax.vjp(lambda u: jax.nn.gelu(u, approximate=True), upward)
        activated_low = activated.astype(jnp.bfloat16)
        many_act = gather(activated_low, bits_g[0])
        act_grad = dot(grad_low, w_down, ((1,), (1,)))
        up_grad = act_back(act_grad)[0].astype(jnp.bfloat16)
        many_up = gather(up_grad, bits_n[0])
        grad_down = weight_grad(many_act, side_g, bits_g[1], False)
        grad_up = weight_grad(many_up, side_n, bits_n[1], True)

        def project(weight, offset_vec):
            return dot(normed_low, weight, ((1,), (0,))) + offset_vec

        queries = project(w_query, b_query).reshape(tok_count, head_count, HD)
        key_rows = project(w_key, b_key).reshape(tok_count, head_count, HD)
        turned_q, turn_q_back = jax.vjp(lambda field: rotate(field, cosine, sine), queries)
        turned_k, turn_k_back = jax.vjp(lambda field: rotate(field, cosine, sine), key_rows)
        query_low = turned_q.astype(jnp.bfloat16)
        key_low = turned_k.astype(jnp.bfloat16)
        value_low = (
            project(w_value, b_value).reshape(tok_count, head_count, HD).astype(jnp.bfloat16)
        )
        scores = (
            jnp.einsum("qhd,khd->hqk", query_low, key_low, preferred_element_type=jnp.float32)
            * 0.125
        )
        places = jnp.arange(tok_count, dtype=jnp.int32)
        allowed = (segment[:, None] == segment[None, :]) & (places[None, :] <= places[:, None])
        masked = jnp.where(allowed[None], scores, -1e30)
        row_top = jnp.max(masked, axis=-1, keepdims=True)
        expo = jnp.exp(masked - row_top)
        totals = jnp.sum(expo, axis=-1, keepdims=True)
        probs_f = expo / totals
        probs = probs_f.astype(jnp.bfloat16)
        attended_low = (
            jnp.einsum("hqk,khd->qhd", probs, value_low, preferred_element_type=jnp.float32)
            .reshape(tok_count, local_width)
            .astype(jnp.bfloat16)
        )
        many_att = gather(attended_low, bits_g[0])
        partial_out = dot(attended_low, w_out, ((1,), (0,))) + dot(
            activated_low, w_down, ((1,), (0,))
        )
        att_grad = (
            dot(grad_low, w_out, ((1,), (1,)))
            .astype(jnp.bfloat16)
            .reshape(tok_count, head_count, HD)
        )
        prob_grad = jnp.einsum(
            "qhd,khd->hqk", att_grad, value_low, preferred_element_type=jnp.float32
        )
        row_delta = jnp.sum(probs_f * prob_grad, axis=-1, keepdims=True)
        score_grad = (probs_f * (prob_grad - row_delta)).astype(jnp.bfloat16)
        q_grad = (
            jnp.einsum("hqk,khd->qhd", score_grad, key_low, preferred_element_type=jnp.float32)
            * 0.125
        )
        k_grad = (
            jnp.einsum("hqk,qhd->khd", score_grad, query_low, preferred_element_type=jnp.float32)
            * 0.125
        )
        v_grad = jnp.einsum("hqk,qhd->khd", probs, att_grad, preferred_element_type=jnp.float32)
        query_grad = turn_q_back(q_grad)[0].reshape(tok_count, local_width).astype(jnp.bfloat16)
        key_grad = turn_k_back(k_grad)[0].reshape(tok_count, local_width).astype(jnp.bfloat16)
        value_grad = v_grad.reshape(tok_count, local_width).astype(jnp.bfloat16)
        qkv_grad = jnp.concatenate([query_grad, key_grad, value_grad], axis=1)
        many_qkv = gather(qkv_grad, bits_n[0])
        grad_qkv = weight_grad(many_qkv, side_n, bits_n[1], True)
        grad_outproj = weight_grad(many_att, side_g, bits_g[1], False)
        normed_grad = (
            dot(up_grad, w_up, ((1,), (1,)))
            + dot(query_grad, w_query, ((1,), (1,)))
            + dot(key_grad, w_key, ((1,), (1,)))
            + dot(value_grad, w_value, ((1,), (1,)))
        )

        rows = tok_count // n_mp

        def my_rows(value):
            return lax.dynamic_slice_in_dim(value, zed * rows, rows, 0)

        def sum_rows(value):
            own = my_rows(value)
            blocks = value.astype(jnp.bfloat16).reshape(n_mp, rows, width)
            for other in to_others(blocks)[1]:
                own = own + other.astype(jnp.float32)
            return own

        total = sum_rows(partial_out)
        mixed_rows = (
            my_rows(tokens_f) + jnp.where(my_rows(is_valid)[:, None], total + out_bias, 0.0)
        ).astype(jnp.bfloat16)
        mixed = share_rows(mixed_rows)

        grads = sum_rows(normed_grad) * ln_gain
        xhat = my_rows(standard)
        back = my_rows(inv_dev) * (
            grads
            - jnp.mean(grads, axis=-1, keepdims=True)
            - xhat * jnp.mean(grads * xhat, axis=-1, keepdims=True)
        )
        grad_tokens = share_rows(
            (my_rows(cotangent).astype(jnp.float32) + back).astype(jnp.bfloat16)
        )

        def sum_over_dp(value):
            for bit in low_bits:
                value = value + swap(value, bit)
            return value

        vectors = jnp.concatenate(
            [
                jnp.sum(normed_grad * standard, axis=0),
                jnp.sum(normed_grad, axis=0),
                jnp.sum(grad_low.astype(jnp.float32), axis=0),
                jnp.sum(up_grad.astype(jnp.float32), axis=0),
                jnp.sum(qkv_grad.astype(jnp.float32), axis=0),
            ]
        )
        vectors = sum_over_dp(vectors)
        norms = vectors[: 2 * width]
        for bit in [1 << i for i in range(n_mp.bit_length() - 1)]:
            norms = norms + lax.ppermute(norms, "mp", [(i, i ^ bit) for i in range(n_mp)])

        def shard(value):
            return lax.dynamic_slice_in_dim(value, me * own_cols, own_cols, 0)

        sent_gain = shard(norms[:width])
        sent_shift = shard(norms[width:])
        sent_bias = shard(vectors[2 * width : 3 * width])
        hidden = w_up.shape[1]
        bias_up = vectors[3 * width : 3 * width + hidden]
        bias_q, bias_k, bias_v = jnp.split(vectors[3 * width + hidden :], 3)
        sent_q, sent_k, sent_v = jnp.split(grad_qkv, 3, axis=1)
        return (
            mixed,
            grad_tokens,
            sent_gain,
            sent_shift,
            sent_q,
            bias_q,
            sent_k,
            bias_k,
            sent_v,
            bias_v,
            grad_outproj,
            grad_up,
            bias_up,
            grad_down,
            sent_bias,
        )

    return body


def solution(mesh):
    in_specs = (
        P("dp", None),
        P("dp", None),
        P(),
        P(),
        P(None, "mp"),
        P("mp"),
        P(None, "mp"),
        P("mp"),
        P(None, "mp"),
        P("mp"),
        P("mp", None),
        P(None, "mp"),
        P("mp"),
        P("mp", None),
        P(),
        P("dp", None),
    )
    out_specs = (
        P("dp", None),
        P("dp", None),
        P("dp"),
        P("dp"),
        P("dp", "mp"),
        P("mp"),
        P("dp", "mp"),
        P("mp"),
        P("dp", "mp"),
        P("mp"),
        P("mp", "dp"),
        P("dp", "mp"),
        P("mp"),
        P("mp", "dp"),
        P("dp"),
    )
    body = make_body(mesh.shape["dp"], mesh.shape["mp"])
    return jax.shard_map(body, mesh=mesh, in_specs=in_specs, out_specs=out_specs, check_vma=False)
```

time: 542 us -> 265 us (0.49)
  the two profiles are of different devices: /device:TPU:0 before, /device:TPU:18 now
where the time goes in v1:
time: 265 us; the launch traced here: 264 us
  waiting for transfers between devices  105 us (40%)
  matrix products  56.3 us (21%)
  starting transfers between devices  46.9 us (18%)
  local copies, waits for them, and re-layouts  29.2 us (11%)
  other arithmetic  24.6 us (9%)
    ppermute x25, waiting for transfers between devices, swap(): return lax.ppermute(value, 'dp', [(i, i ^ mask) for i in range(n_dp)])  65.6 us
    dot_general x20, matrix products, dot(): lax.dot_general(left, right, (dims, ((), ())), preferred_element_type=jnp...  47.1 us
    ppermute x6, waiting for transfers between devices, share_rows(): lax.ppermute(block, 'mp', [(i, (i + delta) % n_mp) for i in range(n_mp)])  36.4 us
    ppermute x25, starting transfers between devices, swap(): return lax.ppermute(value, 'dp', [(i, i ^ mask) for i in range(n_dp)])  16.3 us
    ppermute x6, starting transfers between devices, share_rows(): lax.ppermute(block, 'mp', [(i, (i + delta) % n_mp) for i in range(n_mp)])  13 us
    ppermute x6, starting transfers between devices, to_others(): lax.ppermute(block, 'mp', [(i, (i + delta) % n_mp) for i in range(n_mp)])  12.9 us
    unnamed x128, local copies, waits for them, and re-layouts  9.07 us
  transfers between devices with their start and end apart: 39, of which 15 were waited for; matrix products, arithmetic and copies ran while one was open for 17% of the time, Pallas kernels for 0%

profile of v1, /device:TPU:18, one launch (start us, length us, event | category | flops | bytes accessed | tf_op | source)
XLA Modules:
  0.0 263.9 jit_solution(10477713479457460351)
XLA Ops:
  2.5 1.6 convert_reduce_fusion.3
  4.1 1.6 multiply_reduce_fusion.2
  7.2 1.5 convolution_add_fusion.10
  8.8 2.0 copy.54
  10.8 3.4 %convolution_add_fusion.9 = f32[256,512]{1,0:T(8,128)} fusion(bf16[256,2048]{1,0:T(8,128)(2,1)} %copy-done.4, bf16[2048,512]{1,0:T(8,128)(2,1)} %param.22, f32[512]{0:T(512)S(1)} %copy-done.56), kind=kOutput, calls=%fused_computation.43 | convolution fusion | flops 537001984 | bytes 3672064 | tf_op jit(solution)/shard_map/dot_general | solution.py:40
  14.2 2.0 copy.55
  18.9 2.6 fusion.11
  21.6 1.8 copy.53
  23.4 2.3 convert_reduce_fusion.1
  26.6 1.5 convolution_convert_fusion.5
  28.1 1.8 copy.57
  30.6 1.8 subtract_convert_fusion.1
  32.4 3.7 %fusion.45 = (f32[8,256]{1,0:T(8,128)}, f32[8,256,256]{1,2,0:T(8,128)}) fusion(pred[256,256]{0,1:T(8,128)(4,1)} %fusion.25, bf16[256,8,32]{0,2,1:T(8,128)(2,1)S(1)} %slice.112, bf16[256,8,16]{0,2,1:T(8,128)(2,1)} %get-tuple-element.75, bf16[256,8,16]{0,2,1:T(8,128)(2,1)} %get-tuple-element.76, bf16[256,8,32]{0,2,1:T(8,128)(2,1)S(1)} %slice.113, ...), kind=kOutput, calls=%fused_computation.165 | convolution fusion | flops 70779136 | bytes 2695168 | tf_op jit(solution)/shard_map/sub | solution.py:182
  36.1 2.4 multiply_reduce_fusion.1
  41.5 1.3 slice-done.5
  42.9 2.4 fusion.48
  45.9 5.0 %convert_reduce_fusion = (f32[2048]{0:T(1024)S(1)}, bf16[256,2048]{1,0:T(8,128)(2,1)S(1)}, bf16[256,2048]{1,0:T(8,128)(2,1)}) fusion(f32[256,2048]{1,0:T(8,128)S(1)} %fusion.48, f32[2048]{0:T(1024)S(1)} %copy-done.54, bf16[256,2048]{1,0:T(8,128)(2,1)S(1)} %copy-done.5, bf16[2048,2048]{1,0:T(8,128)(2,1)S(1)} %bitcast.117), kind=kOutput, calls=%fused_computation.24 | convolution fusion | flops 2160588800 | bytes 13647872 | tf_op jit(solution)/shard_map/dot_general | solution.py:40
  50.9 2.4 fusion.49
  56.9 3.5 %fusion.38 = (f32[2048]{0:T(1024)S(1)}, f32[2048]{0:T(1024)S(1)}, bf16[256,2048]{1,0:T(8,128)(2,1)}, f32[256,2048]{1,0:T(8,128)}, f32[256,2048]{1,0:T(8,128)}) fusion(f32[256]{0:T(256)S(1)} %copy-done.42, f32[256]{0:T(256)S(1)} %copy-done.40, bf16[256,2048]{1,0:T(8,128)(2,1)S(1)} %copy-done.2, f32[256,2048]{1,0:T(8,128)S(1)} %convolution_add_fusion.2, ...), kind=kOutput, calls=%fused_computation.159 | convolution fusion | flops 541061120 | bytes 10766336 | tf_op jit(solution)/shard_map/dot_general | solution.py:40
  63.4 2.0 dynamic-slice_bitcast_fusion.2
  65.4 1.6 collective-permute-start.6
  67.3 1.4 collective-permute-start.8
  68.7 2.0 convolution_convert_fusion.6
  70.7 5.9 %fusion.47 = f32[256,2048]{1,0:T(8,128)S(1)} fusion(bf16[256,2048]{1,0:T(8,128)(2,1)S(1)} %copy-done.52, bf16[2048,2048]{1,0:T(8,128)(2,1)} %param.29), kind=kOutput, calls=%fused_computation.167 | convolution fusion | flops 2147483648 | bytes 11534336 | tf_op jit(solution)/shard_map/dot_general | solution.py:40
  76.6 2.1 fusion.46
  86.8 2.7 %collective-permute-done.13 = f32[9728]{0:T(1024)S(1)} collective-permute-done((f32[9728]{0:T(1024)S(1)}, f32[9728]{0:T(1024)S(1)}, u32[]{:S(2)}, u32[]{:S(2)}) %collective-permute-start.13) | collective-permute-done | bytes 38944 | tf_op jit(solution)/shard_map/ppermute | solution.py:58
  90.2 1.6 collective-permute-start.14
  93.1 1.6 convert_element_type.133
  95.5 3.4 %collective-permute-start.15 = (f32[4096]{0:T(1024)S(1)}, f32[4096]{0:T(1024)S(1)}, u32[]{:S(2)}, u32[]{:S(2)}) collective-permute-start(f32[4096]{0:T(1024)S(1)} %slice.76), channel_id=1, source_target_pairs={{0,1},{1,0},{2,3},{3,2},{4,5},{5,4},{6,7},{7,6},{8,9},{9,8},{10,11... | collective-permute-start | bytes 49160 | tf_op jit(solution)/shard_map/ppermute | solution.py:274
  99.5 1.1 collective-permute-done.15
  100.6 1.3 collective-permute-start.16
  103.1 2.1 collective-permute-done.16
  105.3 4.4 %collective-permute-start.1 = (bf16[64,2048]{1,0:T(8,128)(2,1)}, bf16[64,2048]{1,0:T(8,128)(2,1)S(1)}, u32[]{:S(2)}, u32[]{:S(2)}) collective-permute-start(bf16[64,2048]{1,0:T(8,128)(2,1)} %get-tuple-element.59), channel_id=1, source_target_pairs={{0,2},{1,3},{2,0},{3,1},{4,6},{5,7},{6,4},{7,5},{8,10},{9,11},{10,... | collective-permute-start | bytes 786440 | tf_op jit(solution)/shard_map/ppermute | solution.py:72
  109.7 4.6 %collective-permute-start.2 = (bf16[64,2048]{1,0:T(8,128)(2,1)}, bf16[64,2048]{1,0:T(8,128)(2,1)S(1)}, u32[]{:S(2)}, u32[]{:S(2)}) collective-permute-start(bf16[64,2048]{1,0:T(8,128)(2,1)} %get-tuple-element.58), channel_id=1, source_target_pairs={{0,3},{1,0},{2,1},{3,2},{4,7},{5,4},{6,5},{7,6},{8,11},{9,8},{10,9... | collective-permute-start | bytes 786440 | tf_op jit(solution)/shard_map/ppermute | solution.py:72
  116.6 1.6 fusion.39
  118.2 1.2 collective-permute-start.29
  119.3 3.4 %collective-permute-start.17 = (bf16[256,512]{1,0:T(8,128)(2,1)}, bf16[256,512]{1,0:T(8,128)(2,1)S(1)}, u32[]{:S(2)}, u32[]{:S(2)}) collective-permute-start(bf16[256,512]{1,0:T(8,128)(2,1)} %pad_maximum_fusion.13), channel_id=1, source_target_pairs={{0,8},{4,12},{8,0},{12,4},{16,24},{20,28},{24,16},{28,20},{1,9},{5... | collective-permute-start | bytes 786440 | tf_op jit(solution)/shard_map/ppermute | solution.py:58
  122.9 1.6 bitcast_dynamic-update-slice_fusion.7
  125.6 1.2 bitcast_dynamic-update-slice_fusion.3
  127.1 3.1 %collective-permute-start.9 = (bf16[64,2048]{1,0:T(8,128)(2,1)S(1)}, bf16[64,2048]{1,0:T(8,128)(2,1)S(1)}, u32[]{:S(2)}, u32[]{:S(2)}) collective-permute-start(bf16[64,2048]{1,0:T(8,128)(2,1)S(1)} %get-tuple-element.28), channel_id=1, source_target_pairs={{0,1},{1,2},{2,3},{3,0},{4,5},{5,6},{6,7},{7,4},{8,9},{9,10},{10,1... | collective-permute-start | bytes 786440 | tf_op jit(solution)/shard_map/ppermute | solution.py:82
  130.3 1.7 collective-permute-start.24
  132.0 2.4 collective-permute-done.19
  134.4 1.4 collective-permute-start.20
  136.1 3.3 %collective-permute-start.10 = (bf16[64,2048]{1,0:T(8,128)(2,1)S(1)}, bf16[64,2048]{1,0:T(8,128)(2,1)S(1)}, u32[]{:S(2)}, u32[]{:S(2)}) collective-permute-start(bf16[64,2048]{1,0:T(8,128)(2,1)S(1)} %get-tuple-element.28), channel_id=1, source_target_pairs={{0,2},{1,3},{2,0},{3,1},{4,6},{5,7},{6,4},{7,5},{8,10},{9,11},{10,... | collective-permute-start | bytes 786440 | tf_op jit(solution)/shard_map/ppermute | solution.py:82
  139.4 10.3 %collective-permute-done.10 = bf16[64,2048]{1,0:T(8,128)(2,1)S(1)} collective-permute-done((bf16[64,2048]{1,0:T(8,128)(2,1)S(1)}, bf16[64,2048]{1,0:T(8,128)(2,1)S(1)}, u32[]{:S(2)}, u32[]{:S(2)}) %collective-permute-start.10) | collective-permute-done | bytes 262176 | tf_op jit(solution)/shard_map/ppermute | solution.py:82
  149.7 1.4 collective-permute-start.11
  151.1 8.4 %collective-permute-done.11 = bf16[64,2048]{1,0:T(8,128)(2,1)S(1)} collective-permute-done((bf16[64,2048]{1,0:T(8,128)(2,1)S(1)}, bf16[64,2048]{1,0:T(8,128)(2,1)S(1)}, u32[]{:S(2)}, u32[]{:S(2)}) %collective-permute-start.11) | collective-permute-done | bytes 262176 | tf_op jit(solution)/shard_map/ppermute | solution.py:82
  159.5 3.7 %collective-permute-start.3 = (bf16[64,2048]{1,0:T(8,128)(2,1)S(1)}, bf16[64,2048]{1,0:T(8,128)(2,1)S(1)}, u32[]{:S(2)}, u32[]{:S(2)}) collective-permute-start(bf16[64,2048]{1,0:T(8,128)(2,1)S(1)} %get-tuple-element.31), channel_id=1, source_target_pairs={{0,1},{1,2},{2,3},{3,0},{4,5},{5,6},{6,7},{7,4},{8,9},{9,10},{10,1... | collective-permute-start | bytes 786440 | tf_op jit(solution)/shard_map/ppermute | solution.py:82
  163.3 1.4 collective-permute-start.5
  164.7 15.2 %collective-permute-done.3 = bf16[64,2048]{1,0:T(8,128)(2,1)S(1)} collective-permute-done((bf16[64,2048]{1,0:T(8,128)(2,1)S(1)}, bf16[64,2048]{1,0:T(8,128)(2,1)S(1)}, u32[]{:S(2)}, u32[]{:S(2)}) %collective-permute-start.3) | collective-permute-done | bytes 262176 | tf_op jit(solution)/shard_map/ppermute | solution.py:82
  180.0 1.5 collective-permute-done.26
  182.1 2.4 collective-permute-done.5
  185.3 27.0 %collective-permute-done.30 = bf16[512,256]{1,0:T(8,128)(2,1)S(1)} collective-permute-done((bf16[512,256]{1,0:T(8,128)(2,1)S(1)}, bf16[512,256]{1,0:T(8,128)(2,1)S(1)}, u32[]{:S(2)}, u32[]{:S(2)}) %collective-permute-start.30) | collective-permute-done | bytes 262176 | tf_op jit(solution)/shard_map/ppermute | solution.py:58
  212.9 1.3 convolution_add_fusion.8
  214.7 4.7 %convolution_convert_fusion.2 = bf16[256,1536]{1,0:T(8,128)(2,1)S(1)} fusion(bf16[1024,512]{1,0:T(8,128)(2,1)S(1)} %pad_maximum_fusion.3, bf16[256,1536]{0,1:T(8,128)(2,1)S(1)} %collective-permute-done.22, bf16[256,1536]{0,1:T(8,128)(2,1)S(1)} %collective-permute-done.21, bf16[256,1536]{0,1:T(8,128)(2,1)S(1)} %collective-permute-done.20, ...), kind=kOutput, calls=%fused_computation.16 | convolution fusion | flops 824573952 | bytes 4456448 | tf_op jit(solution)/shard_map/dot_general | solution.py:40
  219.4 1.2 collective-permute-start.23
  220.6 1.5 convolution_convert_fusion
  222.6 1.5 convolution_convert_fusion.1
  225.0 14.9 %collective-permute-done.23 = bf16[256,1536]{1,0:T(8,128)(2,1)S(1)} collective-permute-done((bf16[256,1536]{1,0:T(8,128)(2,1)S(1)}, bf16[256,1536]{1,0:T(8,128)(2,1)S(1)}, u32[]{:S(2)}, u32[]{:S(2)}) %collective-permute-start.23) | collective-permute-done | bytes 786464 | tf_op jit(solution)/shard_map/ppermute | solution.py:58
  240.9 1.2 fusion.41
  242.1 5.0 %collective-permute-done.38 = bf16[2048,256]{1,0:T(8,128)(2,1)S(1)} collective-permute-done((bf16[2048,256]{1,0:T(8,128)(2,1)S(1)}, bf16[2048,256]{1,0:T(8,128)(2,1)S(1)}, u32[]{:S(2)}, u32[]{:S(2)}) %collective-permute-start.38) | collective-permute-done | bytes 1048608 | tf_op jit(solution)/shard_map/ppermute | solution.py:58
  247.1 2.5 convolution_add_fusion.5
  249.6 11.9 %collective-permute-done.34 = bf16[256,2048]{1,0:T(8,128)(2,1)S(1)} collective-permute-done((bf16[256,2048]{1,0:T(8,128)(2,1)S(1)}, bf16[256,2048]{1,0:T(8,128)(2,1)S(1)}, u32[]{:S(2)}, u32[]{:S(2)}) %collective-permute-start.34) | collective-permute-done | bytes 1048608 | tf_op jit(solution)/shard_map/ppermute | solution.py:58
  261.5 2.5 convolution_add_fusion.6
  (243 shorter events, 40.0 us)
Async XLA Ops:
  0.6 18.3 %copy-start = (bf16[2048,512]{1,0:T(8,128)(2,1)S(1)}, bf16[2048,512]{1,0:T(8,128)(2,1)}, u32[]{:S(2)}) copy-start(bf16[2048,512]{1,0:T(8,128)(2,1)} %param.24) | copy-start | bytes 6291460
  0.7 5.1 %copy-start.2 = (bf16[256,2048]{1,0:T(8,128)(2,1)S(1)}, bf16[256,2048]{1,0:T(8,128)(2,1)}, u32[]{:S(2)}) copy-start(bf16[256,2048]{1,0:T(8,128)(2,1)} %param.16) | copy-start | bytes 3145732
  0.7 5.1 %copy-start.36 = (f32[2048]{0:T(1024)S(1)}, f32[2048]{0:T(1024)}, u32[]{:S(2)}) copy-start(f32[2048]{0:T(1024)} %param.18) | copy-start | bytes 24580
  0.7 5.1 %copy-start.43 = (f32[2048]{0:T(1024)S(1)}, f32[2048]{0:T(1024)}, u32[]{:S(2)}) copy-start(f32[2048]{0:T(1024)} %param.19) | copy-start | bytes 24580
  2.5 20.9 %copy-start.47 = (pred[256]{0:T(512)(128)(4,1)}, pred[256]{0:T(512)(128)(4,1)S(1)}, u32[]{:S(2)}) copy-start(pred[256]{0:T(512)(128)(4,1)S(1)} %broadcast_compare_fusion) | copy-start | bytes 772
  2.5 4.8 %copy-start.12 = (bf16[2048,512]{1,0:T(8,128)(2,1)S(1)}, bf16[2048,512]{1,0:T(8,128)(2,1)}, u32[]{:S(2)}) copy-start(bf16[2048,512]{1,0:T(8,128)(2,1)} %param.20) | copy-start | bytes 6291460
  2.5 4.8 %copy-start.55 = (f32[512]{0:T(512)S(1)}, f32[512]{0:T(512)}, u32[]{:S(2)}) copy-start(f32[512]{0:T(512)} %param.21) | copy-start | bytes 6148
  10.8 8.1 %copy-start.57 = (f32[512]{0:T(512)S(1)}, f32[512]{0:T(512)}, u32[]{:S(2)}) copy-start(f32[512]{0:T(512)} %param.25) | copy-start | bytes 6148
  42.9 14.0 %copy-start.22 = (bf16[8,64,256]{2,1,0:T(8,128)(2,1)}, bf16[8,64,256]{2,1,0:T(8,128)(2,1)S(1)}, u32[]{:S(2)}) copy-start(bf16[8,64,256]{2,1,0:T(8,128)(2,1)S(1)} %convolution_convert_fusion.4) | copy-start | bytes 786436
  56.9 4.7 %copy-start.38 = (f32[2048]{0:T(1024)S(1)}, f32[2048]{0:T(1024)}, u32[]{:S(2)}) copy-start(f32[2048]{0:T(1024)} %get-tuple-element.25) | copy-start | bytes 24580
  56.9 11.8 %copy-start.46 = (f32[8,256]{1,0:T(8,128)S(1)}, f32[8,256]{1,0:T(8,128)}, u32[]{:S(2)}) copy-start(f32[8,256]{1,0:T(8,128)} %get-tuple-element.81) | copy-start | bytes 24580
  63.4 21.4 %collective-permute-start.12 = (f32[9728]{0:T(1024)}, f32[9728]{0:T(1024)}, u32[]{:S(2)}, u32[]{:S(2)}) collective-permute-start(f32[9728]{0:T(1024)} %constant_dynamic-update-slice_fusion), channel_id=1, source_target_pairs={{0,4},{4,0},{8,12},{12,8},{16,20},{20,16},{24,28},{28,24},{1,5},{5... | collective-permute-start | bytes 116744 | tf_op jit(solution)/shard_map/ppermute | solution.py:58
  65.4 44.3 %collective-permute-start.6 = (bf16[64,2048]{1,0:T(8,128)(2,1)}, bf16[64,2048]{1,0:T(8,128)(2,1)}, u32[]{:S(2)}, u32[]{:S(2)}) collective-permute-start(bf16[64,2048]{1,0:T(8,128)(2,1)} %get-tuple-element.54), channel_id=1, source_target_pairs={{0,1},{1,2},{2,3},{3,0},{4,5},{5,6},{6,7},{7,4},{8,9},{9,10},{10,1... | collective-permute-start | bytes 786440 | tf_op jit(solution)/shard_map/ppermute | solution.py:72
  67.0 48.5 %collective-permute-start.7 = (bf16[64,2048]{1,0:T(8,128)(2,1)}, bf16[64,2048]{1,0:T(8,128)(2,1)}, u32[]{:S(2)}, u32[]{:S(2)}) collective-permute-start(bf16[64,2048]{1,0:T(8,128)(2,1)} %get-tuple-element.56), channel_id=1, source_target_pairs={{0,2},{1,3},{2,0},{3,1},{4,6},{5,7},{6,4},{7,5},{8,10},{9,11},{10,... | collective-permute-start | bytes 786440 | tf_op jit(solution)/shard_map/ppermute | solution.py:72
  67.3 49.3 %collective-permute-start.8 = (bf16[64,2048]{1,0:T(8,128)(2,1)}, bf16[64,2048]{1,0:T(8,128)(2,1)}, u32[]{:S(2)}, u32[]{:S(2)}) collective-permute-start(bf16[64,2048]{1,0:T(8,128)(2,1)} %get-tuple-element.55), channel_id=1, source_target_pairs={{0,3},{1,0},{2,1},{3,2},{4,7},{5,4},{6,5},{7,6},{8,11},{9,8},{10,9... | collective-permute-start | bytes 786440 | tf_op jit(solution)/shard_map/ppermute | solution.py:72
  70.7 5.9 %copy-start.32 = (bf16[8,64,256]{2,1,0:T(8,128)(2,1)}, bf16[8,64,256]{2,1,0:T(8,128)(2,1)S(1)}, u32[]{:S(2)}) copy-start(bf16[8,64,256]{2,1,0:T(8,128)(2,1)S(1)} %convolution_convert_fusion.6) | copy-start | bytes 786436
  70.7 5.9 %copy-start.19 = (bf16[512,2048]{1,0:T(8,128)(2,1)S(1)}, bf16[512,2048]{1,0:T(8,128)(2,1)}, u32[]{:S(2)}) copy-start(bf16[512,2048]{1,0:T(8,128)(2,1)} %param.26) | copy-start | bytes 6291460
  79.6 38.6 %collective-permute-start = (bf16[64,2048]{1,0:T(8,128)(2,1)}, bf16[64,2048]{1,0:T(8,128)(2,1)}, u32[]{:S(2)}, u32[]{:S(2)}) collective-permute-start(bf16[64,2048]{1,0:T(8,128)(2,1)} %get-tuple-element.57), channel_id=1, source_target_pairs={{0,1},{1,2},{2,3},{3,0},{4,5},{5,6},{6,7},{7,4},{8,9},{9,10},{10,1... | collective-permute-start | bytes 786440 | tf_op jit(solution)/shard_map/ppermute | solution.py:72
  81.8 11.2 %copy-start.48 = (pred[256]{0:T(512)(128)(4,1)S(1)}, pred[256]{0:T(512)(128)(4,1)}, u32[]{:S(2)}) copy-start(pred[256]{0:T(512)(128)(4,1)} %copy-done.47) | copy-start | bytes 772
  85.5 4.0 %collective-permute-start.13 = (f32[9728]{0:T(1024)S(1)}, f32[9728]{0:T(1024)S(1)}, u32[]{:S(2)}, u32[]{:S(2)}) collective-permute-start(f32[9728]{0:T(1024)S(1)} %add.305), channel_id=1, source_target_pairs={{0,8},{4,12},{8,0},{12,4},{16,24},{20,28},{24,16},{28,20},{1,9},{5... | collective-permute-start | bytes 116744 | tf_op jit(solution)/shard_map/ppermute | solution.py:58
  86.8 29.7 %copy-start.3 = (f32[256,2048]{1,0:T(8,128)S(1)}, f32[256,2048]{1,0:T(8,128)}, u32[]{:S(2)}) copy-start(f32[256,2048]{1,0:T(8,128)} %get-tuple-element.37) | copy-start | bytes 6291460
  86.8 29.7 %copy-start.37 = (f32[2048]{0:T(1024)S(1)}, f32[2048]{0:T(1024)}, u32[]{:S(2)}) copy-start(f32[2048]{0:T(1024)} %param.18) | copy-start | bytes 24580
  90.2 4.5 %collective-permute-start.14 = (f32[9728]{0:T(1024)}, f32[9728]{0:T(1024)}, u32[]{:S(2)}, u32[]{:S(2)}) collective-permute-start(f32[9728]{0:T(1024)} %add.306), channel_id=1, source_target_pairs={{0,16},{4,20},{8,24},{12,28},{16,0},{20,4},{24,8},{28,12},{1,17},{... | collective-permute-start | bytes 116744 | tf_op jit(solution)/shard_map/ppermute | solution.py:58
  94.7 28.2 %copy-start.44 = (f32[2048]{0:T(1024)S(1)}, f32[2048]{0:T(1024)}, u32[]{:S(2)}) copy-start(f32[2048]{0:T(1024)} %param.30) | copy-start | bytes 24580
  95.5 5.1 %collective-permute-start.15 = (f32[4096]{0:T(1024)S(1)}, f32[4096]{0:T(1024)S(1)}, u32[]{:S(2)}, u32[]{:S(2)}) collective-permute-start(f32[4096]{0:T(1024)S(1)} %slice.76), channel_id=1, source_target_pairs={{0,1},{1,0},{2,3},{3,2},{4,5},{5,4},{6,7},{7,6},{8,9},{9,8},{10,11... | collective-permute-start | bytes 49160 | tf_op jit(solution)/shard_map/ppermute | solution.py:274
  100.6 4.6 %collective-permute-start.16 = (f32[4096]{0:T(1024)S(1)}, f32[4096]{0:T(1024)S(1)}, u32[]{:S(2)}, u32[]{:S(2)}) collective-permute-start(f32[4096]{0:T(1024)S(1)} %slice_add_fusion), channel_id=1, source_target_pairs={{0,2},{1,3},{2,0},{3,1},{4,6},{5,7},{6,4},{7,5},{8,10},{9,11},{10,... | collective-permute-start | bytes 49160 | tf_op jit(solution)/shard_map/ppermute | solution.py:274
  105.3 14.1 %collective-permute-start.1 = (bf16[64,2048]{1,0:T(8,128)(2,1)}, bf16[64,2048]{1,0:T(8,128)(2,1)S(1)}, u32[]{:S(2)}, u32[]{:S(2)}) collective-permute-start(bf16[64,2048]{1,0:T(8,128)(2,1)} %get-tuple-element.59), channel_id=1, source_target_pairs={{0,2},{1,3},{2,0},{3,1},{4,6},{5,7},{6,4},{7,5},{8,10},{9,11},{10,... | collective-permute-start | bytes 786440 | tf_op jit(solution)/shard_map/ppermute | solution.py:72
  109.7 13.0 %collective-permute-start.2 = (bf16[64,2048]{1,0:T(8,128)(2,1)}, bf16[64,2048]{1,0:T(8,128)(2,1)S(1)}, u32[]{:S(2)}, u32[]{:S(2)}) collective-permute-start(bf16[64,2048]{1,0:T(8,128)(2,1)} %get-tuple-element.58), channel_id=1, source_target_pairs={{0,3},{1,0},{2,1},{3,2},{4,7},{5,4},{6,5},{7,6},{8,11},{9,8},{10,9... | collective-permute-start | bytes 786440 | tf_op jit(solution)/shard_map/ppermute | solution.py:72
  115.5 8.9 %collective-permute-start.27 = (bf16[256,512]{1,0:T(8,128)(2,1)}, bf16[256,512]{1,0:T(8,128)(2,1)S(1)}, u32[]{:S(2)}, u32[]{:S(2)}) collective-permute-start(bf16[256,512]{1,0:T(8,128)(2,1)} %pad_maximum_fusion.16), channel_id=1, source_target_pairs={{0,16},{4,20},{8,24},{12,28},{16,0},{20,4},{24,8},{28,12},{1,17},{... | collective-permute-start | bytes 786440 | tf_op jit(solution)/shard_map/ppermute | solution.py:58
  116.6 10.3 %collective-permute-start.28 = (bf16[256,512]{1,0:T(8,128)(2,1)}, bf16[256,512]{1,0:T(8,128)(2,1)S(1)}, u32[]{:S(2)}, u32[]{:S(2)}) collective-permute-start(bf16[256,512]{1,0:T(8,128)(2,1)} %pad_maximum_fusion.17), channel_id=1, source_target_pairs={{0,4},{4,0},{8,12},{12,8},{16,20},{20,16},{24,28},{28,24},{1,5},{5... | collective-permute-start | bytes 786440 | tf_op jit(solution)/shard_map/ppermute | solution.py:58
  118.2 6.3 %copy-start.30 = (bf16[256,512]{1,0:T(8,128)(2,1)S(1)}, bf16[256,512]{1,0:T(8,128)(2,1)}, u32[]{:S(2)}) copy-start(bf16[256,512]{1,0:T(8,128)(2,1)} %pad_maximum_fusion.15) | copy-start | bytes 786436
  118.2 8.9 %collective-permute-start.29 = (bf16[256,512]{1,0:T(8,128)(2,1)}, bf16[256,512]{1,0:T(8,128)(2,1)S(1)}, u32[]{:S(2)}, u32[]{:S(2)}) collective-permute-start(bf16[256,512]{1,0:T(8,128)(2,1)} %pad_maximum_fusion.18), channel_id=1, source_target_pairs={{0,20},{4,16},{8,28},{12,24},{16,4},{20,0},{24,12},{28,8},{1,21},{... | collective-permute-start | bytes 786440 | tf_op jit(solution)/shard_map/ppermute | solution.py:58
  119.3 11.0 %collective-permute-start.17 = (bf16[256,512]{1,0:T(8,128)(2,1)}, bf16[256,512]{1,0:T(8,128)(2,1)S(1)}, u32[]{:S(2)}, u32[]{:S(2)}) collective-permute-start(bf16[256,512]{1,0:T(8,128)(2,1)} %pad_maximum_fusion.13), channel_id=1, source_target_pairs={{0,8},{4,12},{8,0},{12,4},{16,24},{20,28},{24,16},{28,20},{1,9},{5... | collective-permute-start | bytes 786440 | tf_op jit(solution)/shard_map/ppermute | solution.py:58
  122.7 9.3 %collective-permute-start.18 = (bf16[256,512]{1,0:T(8,128)(2,1)}, bf16[256,512]{1,0:T(8,128)(2,1)S(1)}, u32[]{:S(2)}, u32[]{:S(2)}) collective-permute-start(bf16[256,512]{1,0:T(8,128)(2,1)} %pad_maximum_fusion.14), channel_id=1, source_target_pairs={{0,4},{4,0},{8,12},{12,8},{16,20},{20,16},{24,28},{28,24},{1,5},{5... | collective-permute-start | bytes 786440 | tf_op jit(solution)/shard_map/ppermute | solution.py:58
  122.9 7.4 %copy-start.26 = (bf16[256,256]{1,0:T(8,128)(2,1)S(1)}, bf16[256,256]{1,0:T(8,128)(2,1)}, u32[]{:S(2)}) copy-start(bf16[256,256]{1,0:T(8,128)(2,1)} %get-tuple-element.38) | copy-start | bytes 393220
  122.9 7.4 %copy-start.27 = (bf16[256,256]{1,0:T(8,128)(2,1)S(1)}, bf16[256,256]{1,0:T(8,128)(2,1)}, u32[]{:S(2)}) copy-start(bf16[256,256]{1,0:T(8,128)(2,1)} %get-tuple-element.44) | copy-start | bytes 393220
  124.5 9.9 %collective-permute-start.19 = (bf16[256,512]{1,0:T(8,128)(2,1)S(1)}, bf16[256,512]{1,0:T(8,128)(2,1)S(1)}, u32[]{:S(2)}, u32[]{:S(2)}) collective-permute-start(bf16[256,512]{1,0:T(8,128)(2,1)S(1)} %copy-done.30), channel_id=1, source_target_pairs={{0,12},{4,8},{8,4},{12,0},{16,28},{20,24},{24,20},{28,16},{1,13},{... | collective-permute-start | bytes 786440 | tf_op jit(solution)/shard_map/ppermute | solution.py:58
  125.6 4.8 %copy-start.33 = (bf16[8,64,256]{2,1,0:T(8,128)(2,1)S(1)}, bf16[8,64,256]{2,1,0:T(8,128)(2,1)}, u32[]{:S(2)}) copy-start(bf16[8,64,256]{2,1,0:T(8,128)(2,1)} %copy-done.32) | copy-start | bytes 786436
  125.6 8.8 %copy-start.24 = (bf16[256,1536]{0,1:T(8,128)(2,1)S(1)}, bf16[256,1536]{0,1:T(8,128)(2,1)}, u32[]{:S(2)}) copy-start(bf16[256,1536]{0,1:T(8,128)(2,1)} %get-tuple-element.22) | copy-start | bytes 2359300
  125.6 10.3 %copy-start.25 = (bf16[256,256]{1,0:T(8,128)(2,1)S(1)}, bf16[256,256]{1,0:T(8,128)(2,1)}, u32[]{:S(2)}) copy-start(bf16[256,256]{1,0:T(8,128)(2,1)} %get-tuple-element.53) | copy-start | bytes 393220
  126.9 85.4 %collective-permute-start.35 = (bf16[256,2048]{1,0:T(8,128)(2,1)S(1)}, bf16[256,2048]{1,0:T(8,128)(2,1)S(1)}, u32[]{:S(2)}, u32[]{:S(2)}) collective-permute-start(bf16[256,2048]{1,0:T(8,128)(2,1)S(1)} %copy-done.53), channel_id=1, source_target_pairs={{0,16},{4,20},{8,24},{12,28},{16,0},{20,4},{24,8},{28,12},{1,17},{... | collective-permute-start | bytes 3145736 | tf_op jit(solution)/shard_map/ppermute | solution.py:58
  127.1 8.9 %collective-permute-start.9 = (bf16[64,2048]{1,0:T(8,128)(2,1)S(1)}, bf16[64,2048]{1,0:T(8,128)(2,1)S(1)}, u32[]{:S(2)}, u32[]{:S(2)}) collective-permute-start(bf16[64,2048]{1,0:T(8,128)(2,1)S(1)} %get-tuple-element.28), channel_id=1, source_target_pairs={{0,1},{1,2},{2,3},{3,0},{4,5},{5,6},{6,7},{7,4},{8,9},{9,10},{10,1... | collective-permute-start | bytes 786440 | tf_op jit(solution)/shard_map/ppermute | solution.py:82
  130.3 32.9 %collective-permute-start.24 = (bf16[256,512]{0,1:T(8,128)(2,1)S(1)}, bf16[256,512]{0,1:T(8,128)(2,1)S(1)}, u32[]{:S(2)}, u32[]{:S(2)}) collective-permute-start(bf16[256,512]{0,1:T(8,128)(2,1)S(1)} %bitcast.111), channel_id=1, source_target_pairs={{0,16},{4,20},{8,24},{12,28},{16,0},{20,4},{24,8},{28,12},{1,17},{... | collective-permute-start | bytes 786440 | tf_op jit(solution)/shard_map/ppermute | solution.py:58
  132.0 31.2 %collective-permute-start.25 = (bf16[256,512]{0,1:T(8,128)(2,1)S(1)}, bf16[256,512]{0,1:T(8,128)(2,1)S(1)}, u32[]{:S(2)}, u32[]{:S(2)}) collective-permute-start(bf16[256,512]{0,1:T(8,128)(2,1)S(1)} %bitcast.112), channel_id=1, source_target_pairs={{0,4},{4,0},{8,12},{12,8},{16,20},{20,16},{24,28},{28,24},{1,5},{5... | collective-permute-start | bytes 786440 | tf_op jit(solution)/shard_map/ppermute | solution.py:58
  134.4 50.9 %collective-permute-start.20 = (bf16[256,1536]{0,1:T(8,128)(2,1)S(1)}, bf16[256,1536]{0,1:T(8,128)(2,1)S(1)}, u32[]{:S(2)}, u32[]{:S(2)}) collective-permute-start(bf16[256,1536]{0,1:T(8,128)(2,1)S(1)} %copy-done.24), channel_id=1, source_target_pairs={{0,8},{4,12},{8,0},{12,4},{16,24},{20,28},{24,16},{28,20},{1,9},{5... | collective-permute-start | bytes 2359304 | tf_op jit(solution)/shard_map/ppermute | solution.py:58
  135.8 45.6 %copy-start.51 = (bf16[256,2048]{1,0:T(8,128)(2,1)S(1)}, bf16[256,2048]{1,0:T(8,128)(2,1)}, u32[]{:S(2)}) copy-start(bf16[256,2048]{1,0:T(8,128)(2,1)} %copy-done.50) | copy-start | bytes 3145732
  136.1 13.6 %collective-permute-start.10 = (bf16[64,2048]{1,0:T(8,128)(2,1)S(1)}, bf16[64,2048]{1,0:T(8,128)(2,1)S(1)}, u32[]{:S(2)}, u32[]{:S(2)}) collective-permute-start(bf16[64,2048]{1,0:T(8,128)(2,1)S(1)} %get-tuple-element.28), channel_id=1, source_target_pairs={{0,2},{1,3},{2,0},{3,1},{4,6},{5,7},{6,4},{7,5},{8,10},{9,11},{10,... | collective-permute-start | bytes 786440 | tf_op jit(solution)/shard_map/ppermute | solution.py:82
  149.7 9.8 %collective-permute-start.11 = (bf16[64,2048]{1,0:T(8,128)(2,1)S(1)}, bf16[64,2048]{1,0:T(8,128)(2,1)S(1)}, u32[]{:S(2)}, u32[]{:S(2)}) collective-permute-start(bf16[64,2048]{1,0:T(8,128)(2,1)S(1)} %get-tuple-element.28), channel_id=1, source_target_pairs={{0,3},{1,0},{2,1},{3,2},{4,7},{5,4},{6,5},{7,6},{8,11},{9,8},{10,9... | collective-permute-start | bytes 786440 | tf_op jit(solution)/shard_map/ppermute | solution.py:82
  159.5 20.5 %collective-permute-start.3 = (bf16[64,2048]{1,0:T(8,128)(2,1)S(1)}, bf16[64,2048]{1,0:T(8,128)(2,1)S(1)}, u32[]{:S(2)}, u32[]{:S(2)}) collective-permute-start(bf16[64,2048]{1,0:T(8,128)(2,1)S(1)} %get-tuple-element.31), channel_id=1, source_target_pairs={{0,1},{1,2},{2,3},{3,0},{4,5},{5,6},{6,7},{7,4},{8,9},{9,10},{10,1... | collective-permute-start | bytes 786440 | tf_op jit(solution)/shard_map/ppermute | solution.py:82
  163.2 18.7 %copy-start.20 = (bf16[4,64,2048]{2,1,0:T(8,128)(2,1)}, bf16[4,64,2048]{2,1,0:T(8,128)(2,1)S(1)}, u32[]{:S(2)}) copy-start(bf16[4,64,2048]{2,1,0:T(8,128)(2,1)S(1)} %bitcast_dynamic-update-slice_fusion) | copy-start | bytes 3145732
  163.2 18.7 %collective-permute-start.4 = (bf16[64,2048]{1,0:T(8,128)(2,1)S(1)}, bf16[64,2048]{1,0:T(8,128)(2,1)S(1)}, u32[]{:S(2)}, u32[]{:S(2)}) collective-permute-start(bf16[64,2048]{1,0:T(8,128)(2,1)S(1)} %get-tuple-element.31), channel_id=1, source_target_pairs={{0,2},{1,3},{2,0},{3,1},{4,6},{5,7},{6,4},{7,5},{8,10},{9,11},{10,... | collective-permute-start | bytes 786440 | tf_op jit(solution)/shard_map/ppermute | solution.py:82
  163.3 21.2 %collective-permute-start.5 = (bf16[64,2048]{1,0:T(8,128)(2,1)S(1)}, bf16[64,2048]{1,0:T(8,128)(2,1)S(1)}, u32[]{:S(2)}, u32[]{:S(2)}) collective-permute-start(bf16[64,2048]{1,0:T(8,128)(2,1)S(1)} %get-tuple-element.31), channel_id=1, source_target_pairs={{0,3},{1,0},{2,1},{3,2},{4,7},{5,4},{6,5},{7,6},{8,11},{9,8},{10,9... | collective-permute-start | bytes 786440 | tf_op jit(solution)/shard_map/ppermute | solution.py:82
  179.9 1.5 collective-permute-start.26
  181.5 32.7 %collective-permute-start.31 = (bf16[256,2048]{1,0:T(8,128)(2,1)S(1)}, bf16[256,2048]{1,0:T(8,128)(2,1)S(1)}, u32[]{:S(2)}, u32[]{:S(2)}) collective-permute-start(bf16[256,2048]{1,0:T(8,128)(2,1)S(1)} %copy-done.51), channel_id=1, source_target_pairs={{0,8},{4,12},{8,0},{12,4},{16,24},{20,28},{24,16},{28,20},{1,9},{5... | collective-permute-start | bytes 3145736 | tf_op jit(solution)/shard_map/ppermute | solution.py:58
  181.9 32.2 %collective-permute-start.21 = (bf16[256,1536]{0,1:T(8,128)(2,1)S(1)}, bf16[256,1536]{0,1:T(8,128)(2,1)S(1)}, u32[]{:S(2)}, u32[]{:S(2)}) collective-permute-start(bf16[256,1536]{0,1:T(8,128)(2,1)S(1)} %copy-done.24), channel_id=1, source_target_pairs={{0,4},{4,0},{8,12},{12,8},{16,20},{20,16},{24,28},{28,24},{1,5},{5... | collective-permute-start | bytes 2359304 | tf_op jit(solution)/shard_map/ppermute | solution.py:58
  184.5 27.8 %collective-permute-start.30 = (bf16[512,256]{1,0:T(8,128)(2,1)S(1)}, bf16[512,256]{1,0:T(8,128)(2,1)S(1)}, u32[]{:S(2)}, u32[]{:S(2)}) collective-permute-start(bf16[512,256]{1,0:T(8,128)(2,1)S(1)} %convolution_convert_fusion.3), channel_id=1, source_target_pairs={{0,8},{4,12},{8,0},{12,4},{16,24},{20,28},{24,16},{28,20},{1,9},{5... | collective-permute-start | bytes 786440 | tf_op jit(solution)/shard_map/ppermute | solution.py:58
  185.3 29.3 %collective-permute-start.22 = (bf16[256,1536]{0,1:T(8,128)(2,1)S(1)}, bf16[256,1536]{0,1:T(8,128)(2,1)S(1)}, u32[]{:S(2)}, u32[]{:S(2)}) collective-permute-start(bf16[256,1536]{0,1:T(8,128)(2,1)S(1)} %collective-permute-done.20), channel_id=1, source_target_pairs={{0,4},{4,0},{8,12},{12,8},{16,20},{20,16},{24,28},{28,24},{1,5},{5... | collective-permute-start | bytes 2359304 | tf_op jit(solution)/shard_map/ppermute | solution.py:58
  212.3 8.3 %collective-permute-start.36 = (bf16[256,2048]{1,0:T(8,128)(2,1)S(1)}, bf16[256,2048]{1,0:T(8,128)(2,1)S(1)}, u32[]{:S(2)}, u32[]{:S(2)}) collective-permute-start(bf16[256,2048]{1,0:T(8,128)(2,1)S(1)} %copy-done.53), channel_id=1, source_target_pairs={{0,4},{4,0},{8,12},{12,8},{16,20},{20,16},{24,28},{28,24},{1,5},{5... | collective-permute-start | bytes 3145736 | tf_op jit(solution)/shard_map/ppermute | solution.py:58
  212.3 8.3 %collective-permute-start.37 = (bf16[256,2048]{1,0:T(8,128)(2,1)S(1)}, bf16[256,2048]{1,0:T(8,128)(2,1)S(1)}, u32[]{:S(2)}, u32[]{:S(2)}) collective-permute-start(bf16[256,2048]{1,0:T(8,128)(2,1)S(1)} %collective-permute-done.35), channel_id=1, source_target_pairs={{0,4},{4,0},{8,12},{12,8},{16,20},{20,16},{24,28},{28,24},{1,5},{5... | collective-permute-start | bytes 3145736 | tf_op jit(solution)/shard_map/ppermute | solution.py:58
  214.1 8.5 %collective-permute-start.32 = (bf16[256,2048]{1,0:T(8,128)(2,1)S(1)}, bf16[256,2048]{1,0:T(8,128)(2,1)S(1)}, u32[]{:S(2)}, u32[]{:S(2)}) collective-permute-start(bf16[256,2048]{1,0:T(8,128)(2,1)S(1)} %copy-done.51), channel_id=1, source_target_pairs={{0,4},{4,0},{8,12},{12,8},{16,20},{20,16},{24,28},{28,24},{1,5},{5... | collective-permute-start | bytes 3145736 | tf_op jit(solution)/shard_map/ppermute | solution.py:58
  214.1 8.5 %collective-permute-start.33 = (bf16[256,2048]{1,0:T(8,128)(2,1)S(1)}, bf16[256,2048]{1,0:T(8,128)(2,1)S(1)}, u32[]{:S(2)}, u32[]{:S(2)}) collective-permute-start(bf16[256,2048]{1,0:T(8,128)(2,1)S(1)} %collective-permute-done.31), channel_id=1, source_target_pairs={{0,4},{4,0},{8,12},{12,8},{16,20},{20,16},{24,28},{28,24},{1,5},{5... | collective-permute-start | bytes 3145736 | tf_op jit(solution)/shard_map/ppermute | solution.py:58
  219.4 20.5 %collective-permute-start.23 = (bf16[256,1536]{1,0:T(8,128)(2,1)S(1)}, bf16[256,1536]{1,0:T(8,128)(2,1)S(1)}, u32[]{:S(2)}, u32[]{:S(2)}) collective-permute-start(bf16[256,1536]{1,0:T(8,128)(2,1)S(1)} %convolution_convert_fusion.2), channel_id=1, source_target_pairs={{0,16},{4,20},{8,24},{12,28},{16,0},{20,4},{24,8},{28,12},{1,17},{... | collective-permute-start | bytes 2359304 | tf_op jit(solution)/shard_map/ppermute | solution.py:58
  222.2 24.9 %collective-permute-start.38 = (bf16[2048,256]{1,0:T(8,128)(2,1)S(1)}, bf16[2048,256]{1,0:T(8,128)(2,1)S(1)}, u32[]{:S(2)}, u32[]{:S(2)}) collective-permute-start(bf16[2048,256]{1,0:T(8,128)(2,1)S(1)} %convolution_convert_fusion), channel_id=1, source_target_pairs={{0,8},{4,12},{8,0},{12,4},{16,24},{20,28},{24,16},{28,20},{1,9},{5... | collective-permute-start | bytes 3145736 | tf_op jit(solution)/shard_map/ppermute | solution.py:58
  224.1 37.3 %collective-permute-start.34 = (bf16[256,2048]{1,0:T(8,128)(2,1)S(1)}, bf16[256,2048]{1,0:T(8,128)(2,1)S(1)}, u32[]{:S(2)}, u32[]{:S(2)}) collective-permute-start(bf16[256,2048]{1,0:T(8,128)(2,1)S(1)} %convolution_convert_fusion.1), channel_id=1, source_target_pairs={{0,16},{4,20},{8,24},{12,28},{16,0},{20,4},{24,8},{28,12},{1,17},{... | collective-permute-start | bytes 3145736 | tf_op jit(solution)/shard_map/ppermute | solution.py:58
  (39 other events, 85.5 us)

commit v2 on v0

v2 whole, which is shorter than its diff:
```python
import functools
import math

import jax
import jax.numpy as jnp
from jax import lax
from jax.experimental import pallas as pl
from jax.experimental.pallas import tpu as pltpu
from jax.sharding import PartitionSpec as P

HD = 64
ROT = 32
EPSILON = 1e-05
GROUP = 8
CORE, XBIT, YBIT = 1, 2, 4
BLK = 256
F32 = jnp.float32
BF16 = jnp.bfloat16
MESH = pl.DeviceIdType.MESH
GELU_A = math.sqrt(2.0 / math.pi)
GELU_B = 0.044715


def nn(left, right):
    return lax.dot_general(left, right, (((1,), (0,)), ((), ())), preferred_element_type=F32)


def nt(left, right):
    return lax.dot_general(left, right, (((1,), (1,)), ((), ())), preferred_element_type=F32)


def tn(left, right):
    return lax.dot_general(left, right, (((0,), (0,)), ((), ())), preferred_element_type=F32)


def flip(index, mask):
    for bit in (1, 2, 4):
        if mask & bit:
            index = index + bit * (1 - 2 * ((index // bit) % 2))
    return index


def mult(value, by):
    return pl.multiple_of(value, by)


N_JS = (0, XBIT, CORE, XBIT | CORE)
N_MS = (0, YBIT)
G_JS = (0, YBIT, CORE, YBIT | CORE)
G_MS = (0, XBIT)


def layer_kernel(
    n_chunks,
    g_chunks,
    lens,
    tok_h,
    cot_h,
    gain,
    shift,
    bq,
    bk,
    bv,
    bup,
    obias,
    wq_h,
    wk_h,
    wv_h,
    wo_h,
    wu_h,
    wd_h,
    mixed_h,
    gtok_h,
    gradn_h,
    gradg_h,
    vec_o,
    tok,
    gout,
    normed,
    turned_n,
    wq,
    wk,
    wv,
    wo,
    wu,
    wd,
    bn,
    bg,
    side_n,
    side_g,
    rsn_s,
    rsn_r,
    rsg_s,
    rsg_r,
    act,
    dact,
    gqkv,
    att,
    q_s,
    k_s,
    v_s,
    ga_s,
    amask,
    rot_c,
    rot_a,
    rot_b,
    stat_m,
    stat_i,
    stage_n,
    stage_g,
    zpart,
    zr1,
    zr2,
    zs2,
    zout,
    vz,
    vzr,
    vd,
    vdr,
    gsum,
    bsum,
    bsum_r,
    cot_rows,
    in_sem,
    wu_sem,
    wd_sem,
    sn_ss,
    sn_rs,
    sg_ss,
    sg_rs,
    bn_ss,
    bn_rs,
    bg_ss,
    bg_rs,
    rn_ss,
    rn_rs,
    rg_ss,
    rg_rs,
    z_ss,
    z_rs,
    vz_ss,
    vz_rs,
    vd_ss,
    vd_rs,
    bs_ss,
    bs_rs,
    on_sem,
    og_sem,
    oz_sem,
):
    toks, width = tok.shape
    hidden = wu.shape[1]
    heads_w = wq.shape[1]
    n_qkv = 3 * heads_w // BLK
    n_att = heads_w // BLK
    n_hid = hidden // BLK
    n_own = width // BLK
    dp = lax.axis_index("dp")
    zed = lax.axis_index("mp")
    inner = lax.rem(dp, GROUP)
    outer = dp - inner
    half = toks // 2
    quarter = toks // 4

    def peer(mask):
        return (outer + flip(inner, mask), zed)

    def zpeer(mask):
        return (dp, zed + mask * (1 - 2 * ((zed // mask) % 2)))

    def remote(src, dst, ssem, rsem, where):
        return pltpu.make_async_remote_copy(
            src_ref=src,
            dst_ref=dst,
            send_sem=ssem,
            recv_sem=rsem,
            device_id=where,
            device_id_type=MESH,
        )

    loads = [
        pltpu.make_async_copy(src, dst, in_sem.at[i])
        for i, (src, dst) in enumerate(
            ((cot_h, gout), (tok_h, tok), (wq_h, wq), (wk_h, wk), (wv_h, wv), (wo_h, wo))
        )
    ]
    for load in loads:
        load.start()

    def wu_load(c):
        cols = pl.ds(mult(c * BLK, BLK), BLK)
        return pltpu.make_async_copy(wu_h.at[:, cols], wu.at[:, cols], wu_sem.at[c])

    def wd_load(c):
        rows = pl.ds(mult(c * BLK, BLK), BLK)
        return pltpu.make_async_copy(wd_h.at[rows, :], wd.at[rows, :], wd_sem.at[c])

    @pl.loop(0, n_hid)
    def _(c):
        wu_load(c).start()

    @pl.loop(0, n_hid)
    def _(c):
        wd_load(c).start()

    b0 = lax.rem(zed, 2)
    b1 = (zed // 2) % 2
    keep_half = mult(b0 * half, half)
    send_half = mult((1 - b0) * half, half)
    keep_q = mult(b1 * quarter, quarter)
    send_q = mult((1 - b1) * quarter, quarter)
    my_rows = mult(b0 * half + b1 * quarter, quarter)
    cot_load = pltpu.make_async_copy(cot_h.at[pl.ds(my_rows, quarter), :], cot_rows, in_sem.at[6])
    cot_load.start()

    barrier = pltpu.get_barrier_semaphore()
    for mask in range(1, GROUP):
        pl.semaphore_signal(barrier, inc=1, device_id=peer(mask), device_id_type=MESH)
    for mask in (1, 2):
        pl.semaphore_signal(barrier, inc=1, device_id=zpeer(mask), device_id_type=MESH)

    ends = []
    total_len = 0
    for j in range(lens.shape[1]):
        total_len = total_len + lens[0, j]
        ends.append(total_len)

    def segment_of(place):
        number = jnp.zeros_like(place)
        start_of = jnp.zeros_like(place)
        for j, end in enumerate(ends):
            start = end - lens[0, j]
            inside = ((place >= start) & (place < end)).astype(jnp.int32)
            number = number + inside * (j + 1)
            start_of = start_of + inside * start
        return number, start_of

    place_r = lax.broadcasted_iota(jnp.int32, (toks, toks), 0)
    place_c = lax.broadcasted_iota(jnp.int32, (toks, toks), 1)
    seg_r, _ = segment_of(place_r)
    seg_c, _ = segment_of(place_c)
    allowed = (seg_r == seg_c) & (place_c <= place_r)
    amask[...] = jnp.where(allowed, 0.0, -1e30)

    loads[0].wait()
    gsum[...] = jnp.zeros_like(gsum)
    step_rows = 32

    @pl.loop(0, toks // step_rows)
    def _(r):
        first = r * step_rows
        rows = pl.ds(mult(first, step_rows), step_rows)
        place = first + lax.broadcasted_iota(jnp.int32, (step_rows, width), 0)
        value = jnp.where(place < total_len, gout[rows, :].astype(F32), 0.0)
        gout[rows, :] = value.astype(BF16)
        gsum[0:1, :] = gsum[0:1, :] + jnp.sum(value, axis=0, keepdims=True)

    pl.semaphore_wait(barrier, GROUP + 1)

    def side_g_copy(i, m):
        owner = flip(inner, G_JS[i] ^ G_MS[m])
        return remote(
            gout.at[:, pl.ds(mult(owner * BLK, BLK), BLK)],
            side_g.at[m, pl.ds(i * toks, toks), :],
            sg_ss.at[i - 1, m],
            sg_rs.at[i - 1, m],
            peer(G_JS[i]),
        )

    def side_n_copy(i, m):
        owner = flip(inner, N_JS[i] ^ N_MS[m])
        return remote(
            turned_n.at[owner],
            side_n.at[m, :, pl.ds(i * toks, toks)],
            sn_ss.at[i - 1, m],
            sn_rs.at[i - 1, m],
            peer(N_JS[i]),
        )

    for i in (1, 3, 2):
        for m in (0, 1):
            side_g_copy(i, m).start()

    loads[1].wait()

    @pl.loop(0, toks // step_rows)
    def _(r):
        rows = pl.ds(mult(r * step_rows, step_rows), step_rows)
        value = tok[rows, :].astype(F32)
        mean = jnp.sum(value, axis=1, keepdims=True) * (1.0 / width)
        center = value - mean
        spread = jnp.sum(center * center, axis=1, keepdims=True) * (1.0 / width)
        inv = lax.rsqrt(spread + EPSILON)
        normed[rows, :] = (center * inv * gain[...] + shift[...]).astype(BF16)
        stat_m[rows, :] = jnp.broadcast_to(mean, (step_rows, 128))
        stat_i[rows, :] = jnp.broadcast_to(inv, (step_rows, 128))

    @pl.loop(0, n_own)
    def _(o):
        turned_n[o] = normed[:, pl.ds(mult(o * BLK, BLK), BLK)].T

    for i in (1, 3, 2):
        for m in (0, 1):
            side_n_copy(i, m).start()
    for m in (0, 1):
        owner_g = mult(flip(inner, G_MS[m]) * BLK, BLK)
        side_g[m, 0:toks, :] = gout[:, pl.ds(owner_g, BLK)]
        side_n[m, :, 0:toks] = turned_n[flip(inner, N_MS[m])]

    lane = lax.broadcasted_iota(jnp.int32, (toks, 128), 1)
    slot = lax.broadcasted_iota(jnp.int32, (toks, 128), 0)
    _, start_of = segment_of(slot)
    in_head = lane % HD
    order = (in_head % (ROT // 2)).astype(F32)
    freq = jnp.exp(order * (-2.0 / ROT * math.log(10000.0)))
    angle = (slot - start_of).astype(F32) * freq
    cosine, sine = jnp.cos(angle), jnp.sin(angle)
    rot_c[...] = jnp.where(in_head < ROT, cosine, 1.0)
    rot_a[...] = jnp.where(in_head < ROT // 2, -sine, 0.0)
    rot_b[...] = jnp.where((in_head >= ROT // 2) & (in_head < ROT), sine, 0.0)

    def rotate(value, sign):
        left = pltpu.roll(value, 128 - ROT // 2, 1)
        right = pltpu.roll(value, ROT // 2, 1)
        return value * rot_c[...] + sign * (left * rot_a[...] + right * rot_b[...])

    for load in loads[2:6]:
        load.wait()

    @pl.loop(0, heads_w // BLK)
    def _(n):
        cols = pl.ds(mult(n * BLK, BLK), BLK)
        query = nn(normed[...], wq[:, cols]) + bq[:, cols]
        keys = nn(normed[...], wk[:, cols]) + bk[:, cols]
        for part in range(BLK // 128):
            at = pl.ds(mult(n * BLK + part * 128, 128), 128)
            lanes = slice(part * 128, part * 128 + 128)
            q_s[:, at] = (rotate(query[:, lanes], 1.0) * 0.125).astype(BF16)
            k_s[:, at] = rotate(keys[:, lanes], 1.0).astype(BF16)
        v_s[:, cols] = (nn(normed[...], wv[:, cols]) + bv[:, cols]).astype(BF16)
        ga_s[:, cols] = nt(gout[...], wo[cols, :]).astype(BF16)

    def bn_copy(s, k):
        src = bn.at[s, pl.ds(toks if k == 2 else 0, toks), :]
        slot_at = (1, 2, 3)[k]
        return remote(
            src,
            bn.at[s, pl.ds(slot_at * toks, toks), :],
            bn_ss.at[s, k],
            bn_rs.at[s, k],
            peer((XBIT, CORE, CORE)[k]),
        )

    def bg_copy(s, k):
        src = bg.at[s, :, pl.ds(toks if k == 2 else 0, toks)]
        slot_at = (1, 2, 3)[k]
        return remote(
            src,
            bg.at[s, :, pl.ds(slot_at * toks, toks)],
            bg_ss.at[s, k],
            bg_rs.at[s, k],
            peer((YBIT, CORE, CORE)[k]),
        )

    low_lane = lax.broadcasted_iota(jnp.int32, (1, 128), 1) < HD
    head_mask = (jnp.where(low_lane, 1.0, 0.0).astype(BF16), jnp.where(low_lane, 0.0, 1.0).astype(BF16))
    low_full = lax.broadcasted_iota(jnp.int32, (toks, 128), 1) < HD

    @pl.loop(0, n_att)
    def _(n):
        for part in range(BLK // 128):
            at = pl.ds(mult(n * BLK + part * 128, 128), 128)
            lanes = slice(part * 128, part * 128 + 128)
            qp, kp, vp, gp = q_s[:, at], k_s[:, at], v_s[:, at], ga_s[:, at]
            results = []
            for h in range(2):
                scores = nt(qp * head_mask[h], kp) + amask[...]
                top = jnp.max(scores, axis=1, keepdims=True)
                expo = jnp.exp(scores - top)
                probs = expo * (1.0 / jnp.sum(expo, axis=1, keepdims=True))
                probs_low = probs.astype(BF16)
                out = nn(probs_low, vp)
                prob_grad = nt(gp * head_mask[h], vp)
                delta = jnp.sum(probs * prob_grad, axis=1, keepdims=True)
                score_grad = (probs * (prob_grad - delta)).astype(BF16)
                results.append(
                    (out, nn(score_grad, kp), tn(score_grad, qp), tn(probs_low, gp))
                )
            out, dq, dk, dv = (
                jnp.where(low_full, first, second) for first, second in zip(*results)
            )
            att[:, at] = out.astype(BF16)
            bg[n, lanes, 0:toks] = out.astype(BF16).T
            dq = rotate(dq * 0.125, -1.0).astype(BF16)
            dk = rotate(dk, -1.0).astype(BF16)
            dv = dv.astype(BF16)
            for kind, value in enumerate((dq, dk, dv)):
                bn[n + kind * n_att, 0:toks, lanes] = value
                gqkv[:, pl.ds(mult(kind * heads_w + n * BLK + part * 128, 128), 128)] = value
        for k in (0, 1):
            bg_copy(n, k).start()
            for kind in range(3):
                bn_copy(n + kind * n_att, k).start()

    @pl.loop(0, n_hid)
    def _(c):
        cols = pl.ds(mult(c * BLK, BLK), BLK)
        wu_load(c).wait()
        up = nn(normed[...], wu[:, cols]) + bup[:, cols]
        square = up * up
        tanh = jnp.tanh(GELU_A * up * (1.0 + GELU_B * square))
        active = (0.5 * up * (1.0 + tanh)).astype(BF16)
        act[:, cols] = active
        dact[:, cols] = (
            0.5 * (1.0 + tanh)
            + 0.5 * up * (1.0 - tanh * tanh) * (GELU_A * (1.0 + 3.0 * GELU_B * square))
        ).astype(BF16)
        bg[n_att + c, :, 0:toks] = active.T
        for k in (0, 1):
            bg_copy(n_att + c, k).start()

    def z_copy(t, which):
        if which == 0:
            return remote(
                zpart.at[t, pl.ds(send_half, half), :],
                zr1.at[t],
                z_ss.at[t, 0],
                z_rs.at[t, 0],
                zpeer(1),
            )
        if which == 1:
            return remote(zs2.at[t], zr2.at[t], z_ss.at[t, 1], z_rs.at[t, 1], zpeer(2))
        if which == 2:
            rows = pl.ds(my_rows, quarter)
            where = zpeer(2)
        else:
            rows = pl.ds(keep_half, half)
            where = zpeer(1)
        return remote(
            zout.at[t, rows, :], zout.at[t, rows, :], z_ss.at[t, which], z_rs.at[t, which], where
        )

    def z_second(t):
        z_copy(t, 0).wait_recv()

        @pl.loop(0, quarter // 16)
        def _(r):
            at = r * 16
            mine = zpart[t, pl.ds(mult(keep_half + send_q + at, 16), 16), :].astype(F32)
            other = zr1[t, pl.ds(mult(send_q + at, 16), 16), :].astype(F32)
            zs2[t, pl.ds(mult(at, 16), 16), :] = (mine + other).astype(BF16)

        z_copy(t, 1).start()

    def z_sum(t, at):
        mine = zpart[t, pl.ds(mult(my_rows + at, 16), 16), :].astype(F32)
        other = zr1[t, pl.ds(mult(keep_q + at, 16), 16), :].astype(F32)
        far = zr2[t, pl.ds(mult(at, 16), 16), :].astype(F32)
        return mine + other + far

    @pl.loop(0, n_hid)
    def _(c):
        wd_load(c).wait()

    @pl.loop(0, n_own)
    def _(n):
        cols = pl.ds(mult(n * BLK, BLK), BLK)
        zpart[0, :, cols] = (nn(act[...], wd[:, cols]) + nn(att[...], wo[:, cols])).astype(BF16)

    z_copy(0, 0).start()

    @pl.loop(0, n_hid)
    def _(c):
        cols = pl.ds(mult(c * BLK, BLK), BLK)
        grad = (nt(gout[...], wd[cols, :]) * dact[:, cols].astype(F32)).astype(BF16)
        dact[:, cols] = grad
        bn[n_qkv + c, 0:toks, :] = grad
        for k in (0, 1):
            bn_copy(n_qkv + c, k).start()

    vz[...] = jnp.zeros_like(vz)

    @pl.loop(0, n_own)
    def _(n):
        cols = pl.ds(mult(n * BLK, BLK), BLK)
        grad = nt(dact[...], wu[cols, :])
        for kind, weight in enumerate((wq, wk, wv)):
            grad = grad + nt(gqkv[:, kind * heads_w : (kind + 1) * heads_w], weight[cols, :])
        zpart[1, :, cols] = grad.astype(BF16)
        for part in range(BLK // 128):
            lanes = slice(part * 128, part * 128 + 128)
            at = pl.ds(mult(n * BLK + part * 128, 128), 128)
            piece = grad[:, lanes]
            standard = (tok[:, at].astype(F32) - stat_m[...]) * stat_i[...]
            vz[0, n, 0:1, lanes] = jnp.sum(piece * standard, axis=0, keepdims=True)
            vz[0, n, 1:2, lanes] = jnp.sum(piece, axis=0, keepdims=True)

    z_copy(1, 0).start()

    def vz_copy(t):
        return remote(vz.at[t], vzr.at[t], vz_ss.at[t], vz_rs.at[t], zpeer((1, 2)[t]))

    def vd_copy(mask):
        return remote(
            vd.at[flip(inner, mask)],
            vdr.at[mask],
            vd_ss.at[mask],
            vd_rs.at[mask],
            peer(mask),
        )

    bs_copy = remote(bsum, bsum_r, bs_ss, bs_rs, peer(YBIT))
    vz_copy(0).start()

    def rn_copy(s):
        return remote(rsn_s.at[s], rsn_r.at[s], rn_ss.at[s], rn_rs.at[s], peer(YBIT))

    def rg_copy(s):
        return remote(rsg_s.at[s], rsg_r.at[s], rg_ss.at[s], rg_rs.at[s], peer(XBIT))

    for i in (1, 2, 3):
        for m in (0, 1):
            side_g_copy(i, m).wait_recv()
            side_n_copy(i, m).wait_recv()
    bsum[...] = jnp.zeros_like(bsum)

    def mixed_rows():
        z_copy(0, 1).wait_recv()

        @pl.loop(0, quarter // 16)
        def _(r):
            at = r * 16
            rows = pl.ds(mult(my_rows + at, 16), 16)
            place = my_rows + at + lax.broadcasted_iota(jnp.int32, (16, width), 0)
            branch = jnp.where(place < total_len, z_sum(0, at) + obias[...], 0.0)
            zout[0, rows, :] = (tok[rows, :].astype(F32) + branch).astype(BF16)

        z_copy(0, 2).start()

    def grad_rows():
        z_copy(1, 1).wait_recv()
        cot_load.wait()

        @pl.loop(0, quarter // 16)
        def _(r):
            at = r * 16
            rows = pl.ds(mult(my_rows + at, 16), 16)
            inv = stat_i[rows, 0:1]
            standard = (tok[rows, :].astype(F32) - stat_m[rows, 0:1]) * inv
            grad = z_sum(1, at) * gain[...]
            first = jnp.sum(grad, axis=1, keepdims=True) * (1.0 / width)
            second = jnp.sum(grad * standard, axis=1, keepdims=True) * (1.0 / width)
            back = inv * (grad - first - standard * second)
            raw = cot_rows[pl.ds(mult(at, 16), 16), :].astype(F32)
            zout[1, rows, :] = (raw + back).astype(BF16)

        z_copy(1, 2).start()

    def z_last(t):
        z_copy(t, 2).wait_recv()
        z_copy(t, 3).start()

    def vec_second():
        vz_copy(0).wait_recv()
        vz[1] = vz[0] + vzr[0]
        vz_copy(1).start()

    def vec_spread():
        vz_copy(1).wait_recv()
        vd[...] = vz[1] + vzr[1]
        for owner in range(n_own):
            vd[owner, 2:3, :] = gsum[0:1, owner * BLK : owner * BLK + BLK]
        for mask in range(1, GROUP):
            vd_copy(mask).start()

    ones_row = jnp.ones((8, 4 * toks), BF16)

    @pl.loop(0, n_chunks + 1)
    def _(s):
        @pl.when(s < n_chunks)
        def _():
            bn_copy(s, 0).wait_recv()
            bn_copy(s, 2).start()

        @pl.when(s < g_chunks)
        def _():
            bg_copy(s, 0).wait_recv()
            bg_copy(s, 2).start()

        @pl.when(s > 0)
        def _():
            p = s - 1
            bn_copy(p, 1).wait_recv()
            bn_copy(p, 2).wait_recv()
            rsn_s[p] = nn(side_n[1], bn[p]).astype(BF16)
            rn_copy(p).start()
            bsum[pl.ds(p, 1), :] = nn(ones_row, bn[p])[0:1, :]

        @pl.when((s > 0) & (s <= g_chunks))
        def _():
            p = s - 1
            bg_copy(p, 1).wait_recv()
            bg_copy(p, 2).wait_recv()
            rsg_s[p] = nn(bg[p], side_g[1]).astype(BF16)
            rg_copy(p).start()

        @pl.when(s == 5)
        def _():
            z_second(0)
            vec_second()

        @pl.when(s == 9)
        def _():
            z_second(1)
            mixed_rows()
            vec_spread()

    bs_copy.start()

    def out_n(s):
        return pltpu.make_async_copy(
            stage_n.at[lax.rem(s, 2)],
            gradn_h.at[:, pl.ds(mult(s * BLK, BLK), BLK)],
            on_sem.at[lax.rem(s, 2)],
        )

    def out_g(s):
        return pltpu.make_async_copy(
            stage_g.at[lax.rem(s, 2)],
            gradg_h.at[pl.ds(mult(s * BLK, BLK), BLK), :],
            og_sem.at[lax.rem(s, 2)],
        )

    @pl.loop(0, n_chunks)
    def _(s):
        @pl.when(s >= 2)
        def _():
            out_n(s - 2).wait()

        mine = nn(side_n[0], bn[s])
        rn_copy(s).wait_recv()
        stage_n[lax.rem(s, 2)] = mine + rsn_r[s].astype(F32)
        out_n(s).start()

        @pl.when(s == 0)
        def _():
            z_last(0)

        @pl.when(s == 1)
        def _():
            grad_rows()

        @pl.when(s < g_chunks)
        def _():
            @pl.when(s >= 2)
            def _():
                out_g(s - 2).wait()

            mine_g = nn(bg[s], side_g[0])
            rg_copy(s).wait_recv()
            stage_g[lax.rem(s, 2)] = mine_g + rsg_r[s].astype(F32)
            out_g(s).start()

        @pl.when(s == 6)
        def _():
            z_last(1)

    bs_copy.wait_recv()
    sums = vd[inner]
    for mask in range(1, GROUP):
        vd_copy(mask).wait_recv()
        sums = sums + vdr[mask]
    vec_o[0:8, :] = sums
    vec_o[8:, :] = bsum[...] + bsum_r[...]

    z_outs = []
    for t, out_h in enumerate((mixed_h, gtok_h)):
        z_copy(t, 3).wait_recv()
        z_outs.append(pltpu.make_async_copy(zout.at[t], out_h, oz_sem.at[t]))
        z_outs[t].start()

    for i in (1, 2, 3):
        for m in (0, 1):
            side_g_copy(i, m).wait_send()
            side_n_copy(i, m).wait_send()

    @pl.loop(0, n_chunks)
    def _(s):
        for k in range(3):
            bn_copy(s, k).wait_send()
        rn_copy(s).wait_send()

    @pl.loop(0, g_chunks)
    def _(s):
        for k in range(3):
            bg_copy(s, k).wait_send()
        rg_copy(s).wait_send()

    for t in (0, 1):
        for which in range(4):
            z_copy(t, which).wait_send()
        vz_copy(t).wait_send()
    for mask in range(1, GROUP):
        vd_copy(mask).wait_send()
    bs_copy.wait_send()
    for back in (2, 1):
        out_n(n_chunks - back).wait()
        out_g(g_chunks - back).wait()
    for out in z_outs:
        out.wait()


def layer(tokens, lengths, ln_gain, ln_bias, w_query, b_query, w_key, b_key, w_value, b_value, w_out, w_up, b_up, w_down, out_bias, cotangent):
    toks, width = tokens.shape
    heads_w = w_query.shape[1]
    hidden = w_up.shape[1]
    n_chunks = (3 * heads_w + hidden) // BLK
    g_chunks = (heads_w + hidden) // BLK
    n_own = width // BLK
    n_vec = -(-n_chunks // 8) * 8
    half, quarter = toks // 2, toks // 4
    dma = pltpu.SemaphoreType.DMA
    vmem = pltpu.VMEM
    scratch = [
        vmem((toks, width), BF16),
        vmem((toks, width), BF16),
        vmem((toks, width), BF16),
        vmem((n_own, BLK, toks), BF16),
        vmem(w_query.shape, BF16),
        vmem(w_key.shape, BF16),
        vmem(w_value.shape, BF16),
        vmem(w_out.shape, BF16),
        vmem(w_up.shape, BF16),
        vmem(w_down.shape, BF16),
        vmem((n_chunks, 4 * toks, BLK), BF16),
        vmem((g_chunks, BLK, 4 * toks), BF16),
        vmem((2, BLK, 4 * toks), BF16),
        vmem((2, 4 * toks, BLK), BF16),
        vmem((n_chunks, BLK, BLK), BF16),
        vmem((n_chunks, BLK, BLK), BF16),
        vmem((g_chunks, BLK, BLK), BF16),
        vmem((g_chunks, BLK, BLK), BF16),
        vmem((toks, hidden), BF16),
        vmem((toks, hidden), BF16),
        vmem((toks, 3 * heads_w), BF16),
        vmem((toks, heads_w), BF16),
        vmem((toks, heads_w), BF16),
        vmem((toks, heads_w), BF16),
        vmem((toks, heads_w), BF16),
        vmem((toks, heads_w), BF16),
        vmem((toks, toks), F32),
        vmem((toks, 128), F32),
        vmem((toks, 128), F32),
        vmem((toks, 128), F32),
        vmem((toks, 128), F32),
        vmem((toks, 128), F32),
        vmem((2, BLK, BLK), F32),
        vmem((2, BLK, BLK), F32),
        vmem((2, toks, width), BF16),
        vmem((2, half, width), BF16),
        vmem((2, quarter, width), BF16),
        vmem((2, quarter, width), BF16),
        vmem((2, toks, width), BF16),
        vmem((2, n_own, 8, BLK), F32),
        vmem((2, n_own, 8, BLK), F32),
        vmem((n_own, 8, BLK), F32),
        vmem((GROUP, 8, BLK), F32),
        vmem((8, width), F32),
        vmem((n_vec, BLK), F32),
        vmem((n_vec, BLK), F32),
        vmem((quarter, width), BF16),
        dma((7,)),
        dma((hidden // BLK,)),
        dma((hidden // BLK,)),
        dma((3, 2)),
        dma((3, 2)),
        dma((3, 2)),
        dma((3, 2)),
        dma((n_chunks, 3)),
        dma((n_chunks, 3)),
        dma((g_chunks, 3)),
        dma((g_chunks, 3)),
        dma((n_chunks,)),
        dma((n_chunks,)),
        dma((g_chunks,)),
        dma((g_chunks,)),
        dma((2, 4)),
        dma((2, 4)),
        dma((2,)),
        dma((2,)),
        dma((GROUP,)),
        dma((GROUP,)),
        dma,
        dma,
        dma((2,)),
        dma((2,)),
        dma((2,)),
    ]
    anyspace = pl.BlockSpec(memory_space=pl.ANY)
    local = pl.BlockSpec(memory_space=pltpu.VMEM)
    row = lambda value: value.reshape(1, -1)
    mixed, grad_tokens, grad_n, grad_g, vec = pl.pallas_call(
        functools.partial(layer_kernel, n_chunks, g_chunks),
        out_shape=(
            jax.ShapeDtypeStruct((toks, width), BF16),
            jax.ShapeDtypeStruct((toks, width), BF16),
            jax.ShapeDtypeStruct((BLK, n_chunks * BLK), F32),
            jax.ShapeDtypeStruct((g_chunks * BLK, BLK), F32),
            jax.ShapeDtypeStruct((8 + n_vec, BLK), F32),
        ),
        in_specs=[pl.BlockSpec(memory_space=pltpu.SMEM), anyspace, anyspace]
        + [local] * 7
        + [anyspace] * 6,
        out_specs=(anyspace, anyspace, anyspace, anyspace, local),
        scratch_shapes=scratch,
        compiler_params=pltpu.CompilerParams(
            collective_id=0, has_side_effects=True, vmem_limit_bytes=67043328
        ),
    )(
        lengths,
        tokens,
        cotangent,
        row(ln_gain),
        row(ln_bias),
        row(b_query),
        row(b_key),
        row(b_value),
        row(b_up),
        row(out_bias),
        w_query,
        w_key,
        w_value,
        w_out,
        w_up,
        w_down,
    )
    sent_q = grad_n[:, :heads_w]
    sent_k = grad_n[:, heads_w : 2 * heads_w]
    sent_v = grad_n[:, 2 * heads_w : 3 * heads_w]
    sent_up = grad_n[:, 3 * heads_w :]
    per = heads_w // BLK
    bias = vec[8 : 8 + n_chunks]
    return (
        mixed,
        grad_tokens,
        vec[0],
        vec[1],
        sent_q,
        bias[:per].reshape(-1),
        sent_k,
        bias[per : 2 * per].reshape(-1),
        sent_v,
        bias[2 * per : 3 * per].reshape(-1),
        grad_g[:heads_w],
        sent_up,
        bias[3 * per :].reshape(-1),
        grad_g[heads_w:],
        vec[2],
    )


def make_body(n_dp, n_mp):
    outer = n_dp // GROUP

    def order(value, axis):
        if outer == 1:
            return value
        shape = value.shape
        split = shape[:axis] + (outer, GROUP, shape[axis] // n_dp) + shape[axis + 1 :]
        return jnp.swapaxes(value.reshape(split), axis, axis + 1).reshape(shape)

    def restore(value, axis):
        if outer == 1:
            return value
        shape = value.shape
        split = shape[:axis] + (GROUP, outer, shape[axis] // n_dp) + shape[axis + 1 :]
        return jnp.swapaxes(value.reshape(split), axis, axis + 1).reshape(shape)

    groups = [[o * GROUP + i for o in range(outer)] for i in range(GROUP)]

    def scatter(value, axis):
        if outer == 1:
            return value
        return lax.psum_scatter(
            value, "dp", scatter_dimension=axis, axis_index_groups=groups, tiled=True
        )

    def total(value):
        if outer == 1:
            return value
        return lax.psum(value, "dp", axis_index_groups=groups)

    def body(tokens, lengths, ln_gain, ln_bias, w_query, b_query, w_key, b_key, w_value, b_value, w_out, w_up, b_up, w_down, out_bias, cotangent):
        found = layer(
            order(tokens, 1),
            lengths,
            order(ln_gain, 0),
            order(ln_bias, 0),
            order(w_query, 0),
            b_query,
            order(w_key, 0),
            b_key,
            order(w_value, 0),
            b_value,
            order(w_out, 1),
            order(w_up, 0),
            b_up,
            order(w_down, 1),
            order(out_bias, 0),
            order(cotangent, 1),
        )
        (mixed, grad_tokens, gain, shift, g_q, b_q, g_k, b_k, g_v, b_v, g_out, g_up, b_u, g_down, b_out) = found
        return (
            restore(mixed, 1),
            restore(grad_tokens, 1),
            scatter(gain, 0),
            scatter(shift, 0),
            scatter(g_q, 0),
            total(b_q),
            scatter(g_k, 0),
            total(b_k),
            scatter(g_v, 0),
            total(b_v),
            scatter(g_out, 1),
            scatter(g_up, 0),
            total(b_u),
            scatter(g_down, 1),
            scatter(b_out, 0),
        )

    return body


def solution(mesh):
    in_specs = (
        P("dp", None),
        P("dp", None),
        P(),
        P(),
        P(None, "mp"),
        P("mp"),
        P(None, "mp"),
        P("mp"),
        P(None, "mp"),
        P("mp"),
        P("mp", None),
        P(None, "mp"),
        P("mp"),
        P("mp", None),
        P(),
        P("dp", None),
    )
    out_specs = (
        P("dp", None),
        P("dp", None),
        P("dp"),
        P("dp"),
        P("dp", "mp"),
        P("mp"),
        P("dp", "mp"),
        P("mp"),
        P("dp", "mp"),
        P("mp"),
        P("mp", "dp"),
        P("dp", "mp"),
        P("mp"),
        P("mp", "dp"),
        P("dp"),
    )
    body = make_body(mesh.shape["dp"], mesh.shape["mp"])
    return jax.shard_map(body, mesh=mesh, in_specs=in_specs, out_specs=out_specs, check_vma=False)
```

time: 542 us -> 136 us (0.25)
  waiting for transfers between devices: 394 us -> 0 us
  Pallas kernels: 0 us -> 120 us
  matrix products: 66.6 us -> 0 us
  blocking collectives: 25.2 us -> 0 us
  between operations: 16.8 us -> 0.67 us
  other arithmetic: 15.4 us -> 0 us
  local copies, waits for them, and re-layouts: 22.9 us -> 15.6 us
    reduce_scatter x6 -> x0, waiting for transfers between devices: 273 us -> none  [the longest x1 120 us: body(): lax.psum_scatter(grad_down, 'dp', scatter_dimension=1, tiled=True)]
    psum x1 -> x0, waiting for transfers between devices: 121 us -> none  [body(): total = lax.psum(partial_out, 'mp')]
    pallas_call x0 -> x1, Pallas kernels: none -> 120 us  [layer(): pl.pallas_call(functools.partial(layer_kernel, n_chunks, g_chunks), out_s...]
    dot_general x24 -> x0, matrix products: 66.6 us -> none  [the longest x6 30 us: contract_rows(): lax.dot_general(left, right, (((0,), (0,)), ((), ())), preferred_element_...]
    unnamed x1 -> x0, blocking collectives: 25.2 us -> none
    reduce_sum x9 -> x0, other arithmetic: 9.47 us -> none  [the longest x2 3.21 us: layer_norm(): return center * lax.rsqrt(spread + EPSILON) * gain_vec + shift_vec]
    slice x2 -> x5, local copies, waits for them, and re-layouts: 1.93 us -> 9.12 us  [the longest x1 3.2 us: layer(): grad_g[heads_w:]]
    unnamed x98 -> x14, local copies, waits for them, and re-layouts: 13.6 us -> 6.46 us
  transfers between devices with their start and end apart: 7 -> 0, of which waited for: 4 -> 0; matrix products, arithmetic and copies ran while one was open for 7% -> 0% of each run, Pallas kernels for 0% -> 0%
where the time goes in v2:
time: 136 us
  Pallas kernels  120 us (88%)
  local copies, waits for them, and re-layouts  15.6 us (11%)
    pallas_call x1, Pallas kernels, layer(): pl.pallas_call(functools.partial(layer_kernel, n_chunks, g_chunks), out_s...  120 us
    unnamed x14, local copies, waits for them, and re-layouts  6.46 us
    slice x1, local copies, waits for them, and re-layouts, layer(): grad_g[heads_w:]  3.2 us

profile of v2, /device:TPU:0, one launch (start us, length us, event | category | flops | bytes accessed | tf_op | source)
XLA Modules:
  0.0 135.9 jit_solution(16766853839498170969)
XLA Ops:
  0.7 119.7 %shard_map.271 = (bf16[256,2048]{1,0:T(8,128)(2,1)}, bf16[256,2048]{1,0:T(8,128)(2,1)}, f32[256,3584]{1,0:T(8,128)}, f32[2560,256]{1,0:T(8,128)}, f32[24,256]{1,0:T(8,128)}) custom-call(s32[1,4]{1,0:T(1,128)} %lens.1, bf16[256,2048]{1,0:T(8,128)(2,1)} %tok_h.1, bf16[256,2048]{1,0:T(8,128)(2,1)} %cot_h.1, f32[1,2048]{1,0:T(1,128)} %bitcast.22, ...), custom_call_target="tpu_custom_call" | custom-call | tf_op jit(solution)/shard_map/pallas_call | solution.py:802
  120.3 1.4 %fusion.1 = (f32[1,256]{1,0:T(1,128)}, f32[1,256]{1,0:T(1,128)}, f32[1,256]{1,0:T(1,128)}) fusion(f32[24,256]{1,0:T(8,128)} %get-tuple-element.22), kind=kLoop, calls=%fused_computation.5 | loop fusion | bytes 6144 | tf_op jit(solution)/shard_map/slice | solution.py:858
  121.7 0.8 slice_bitcast_fusion.1
  122.5 0.7 slice_bitcast_fusion
  123.2 0.6 copy.34
  123.8 0.6 copy.33
  124.4 0.6 copy.32
  125.0 0.6 copy.31
  125.6 1.9 %slice.52 = f32[512,256]{1,0:T(8,128)} slice(f32[2560,256]{1,0:T(8,128)} %get-tuple-element.24), slice={[0:512], [0:256]} | slice | bytes 1048576 | tf_op jit(solution)/shard_map/slice | solution.py:854
  127.4 0.0 copy-start
  127.4 3.2 %slice.55 = f32[2048,256]{1,0:T(8,128)} slice(f32[2560,256]{1,0:T(8,128)} %get-tuple-element.24), slice={[512:2560], [0:256]} | slice | bytes 4194304 | tf_op jit(solution)/shard_map/slice | solution.py:857
  130.6 0.0 copy-done
  130.6 1.2 fusion
  131.8 0.0 copy-start.2
  131.8 1.5 %slice.53 = f32[256,2048]{1,0:T(8,128)} slice(f32[256,3584]{1,0:T(8,128)S(1)} %copy-done), slice={[0:256], [1536:3584]} | slice | bytes 4194304 | tf_op jit(solution)/shard_map/slice | solution.py:840
  133.3 0.0 copy-start.1
  133.3 0.0 copy-done.2
  133.4 1.0 copy.37
  134.3 0.6 copy-done.1
  134.9 1.0 copy.38
Async XLA Ops:
  127.4 3.2 %copy-start = (f32[256,3584]{1,0:T(8,128)S(1)}, f32[256,3584]{1,0:T(8,128)}, u32[]{:S(2)}) copy-start(f32[256,3584]{1,0:T(8,128)} %get-tuple-element.23) | copy-start | bytes 11010052
  131.8 1.5 %copy-start.2 = (bf16[256,2048]{1,0:T(8,128)(2,1)S(1)}, bf16[256,2048]{1,0:T(8,128)(2,1)}, u32[]{:S(2)}) copy-start(bf16[256,2048]{1,0:T(8,128)(2,1)} %get-tuple-element.49) | copy-start | bytes 3145732
  133.3 1.6 %copy-start.1 = (bf16[256,2048]{1,0:T(8,128)(2,1)S(1)}, bf16[256,2048]{1,0:T(8,128)(2,1)}, u32[]{:S(2)}) copy-start(bf16[256,2048]{1,0:T(8,128)(2,1)} %get-tuple-element.50) | copy-start | bytes 3145732

commit v3 on v2

--- a/solution.py
+++ b/solution.py
@@ -14,9 +14,12 @@
 GROUP = 8
 CORE, XBIT, YBIT = 1, 2, 4
 BLK = 256
+N_MP = 4
+Z_PARTS = 4
 F32 = jnp.float32
 BF16 = jnp.bfloat16
 MESH = pl.DeviceIdType.MESH
+MAIN_VMEM = 46 * 2**20
 GELU_A = math.sqrt(2.0 / math.pi)
 GELU_B = 0.044715
 
@@ -69,10 +72,11 @@
     wo_h,
     wu_h,
     wd_h,
-    mixed_h,
-    gtok_h,
-    gradn_h,
-    gradg_h,
+    bn,
+    bg,
+    rsn_r,
+    rsg_r,
+    zout,
     vec_o,
     tok,
     gout,
@@ -84,14 +88,10 @@
     wo,
     wu,
     wd,
-    bn,
-    bg,
     side_n,
     side_g,
     rsn_s,
-    rsn_r,
     rsg_s,
-    rsg_r,
     act,
     dact,
     gqkv,
@@ -106,13 +106,10 @@
     rot_b,
     stat_m,
     stat_i,
-    stage_n,
-    stage_g,
     zpart,
-    zr1,
-    zr2,
-    zs2,
-    zout,
+    zfar,
+    znear,
+    zmid,
     vz,
     vzr,
     vd,
@@ -136,17 +133,22 @@
     rn_rs,
     rg_ss,
     rg_rs,
-    z_ss,
-    z_rs,
+    zf_ss,
+    zf_rs,
+    zn_ss,
+    zn_rs,
+    zm_ss,
+    zm_rs,
+    zo_ss,
+    zo_rs,
+    zw_ss,
+    zw_rs,
     vz_ss,
     vz_rs,
     vd_ss,
     vd_rs,
     bs_ss,
     bs_rs,
-    on_sem,
-    og_sem,
-    oz_sem,
 ):
     toks, width = tok.shape
     hidden = wu.shape[1]
@@ -160,13 +162,22 @@
     inner = lax.rem(dp, GROUP)
     outer = dp - inner
     half = toks // 2
-    quarter = toks // 4
+    piece_cols = width // Z_PARTS
+    piece_rows = half // Z_PARTS
 
     def peer(mask):
         return (outer + flip(inner, mask), zed)
 
-    def zpeer(mask):
-        return (dp, zed + mask * (1 - 2 * ((zed // mask) % 2)))
+    middle = (zed == 1) | (zed == 2)
+    end_of_line = (zed == 0) | (zed == 3)
+    side_of_line = zed // 2
+    beside = (dp, zed + 1 - 2 * lax.rem(zed, 2))
+    across = (dp, 3 - zed)
+    near_rows = mult(side_of_line * half, half)
+    far_rows = mult((1 - side_of_line) * half, half)
+
+    def zpeer(step):
+        return (dp, lax.rem(zed + step, N_MP))
 
     def remote(src, dst, ssem, rsem, where):
         return pltpu.make_async_remote_copy(
@@ -203,21 +214,14 @@
     def _(c):
         wd_load(c).start()
 
-    b0 = lax.rem(zed, 2)
-    b1 = (zed // 2) % 2
-    keep_half = mult(b0 * half, half)
-    send_half = mult((1 - b0) * half, half)
-    keep_q = mult(b1 * quarter, quarter)
-    send_q = mult((1 - b1) * quarter, quarter)
-    my_rows = mult(b0 * half + b1 * quarter, quarter)
-    cot_load = pltpu.make_async_copy(cot_h.at[pl.ds(my_rows, quarter), :], cot_rows, in_sem.at[6])
+    cot_load = pltpu.make_async_copy(cot_h.at[pl.ds(near_rows, half), :], cot_rows, in_sem.at[6])
     cot_load.start()
 
     barrier = pltpu.get_barrier_semaphore()
     for mask in range(1, GROUP):
         pl.semaphore_signal(barrier, inc=1, device_id=peer(mask), device_id_type=MESH)
-    for mask in (1, 2):
-        pl.semaphore_signal(barrier, inc=1, device_id=zpeer(mask), device_id_type=MESH)
+    for step in range(1, N_MP):
+        pl.semaphore_signal(barrier, inc=1, device_id=zpeer(step), device_id_type=MESH)
 
     ends = []
     total_len = 0
@@ -255,14 +259,12 @@
         gout[rows, :] = value.astype(BF16)
         gsum[0:1, :] = gsum[0:1, :] + jnp.sum(value, axis=0, keepdims=True)
 
-    pl.semaphore_wait(barrier, GROUP + 1)
-
     def side_g_copy(i, m):
         owner = flip(inner, G_JS[i] ^ G_MS[m])
         return remote(
             gout.at[:, pl.ds(mult(owner * BLK, BLK), BLK)],
-            side_g.at[m, pl.ds(i * toks, toks), :],
-            sg_ss.at[i - 1, m],
+            side_g.at[pl.ds(i * toks, toks), pl.ds(m * BLK, BLK)],
+            sg_ss,
             sg_rs.at[i - 1, m],
             peer(G_JS[i]),
         )
@@ -272,14 +274,10 @@
         return remote(
             turned_n.at[owner],
             side_n.at[m, :, pl.ds(i * toks, toks)],
-            sn_ss.at[i - 1, m],
+            sn_ss,
             sn_rs.at[i - 1, m],
             peer(N_JS[i]),
         )
-
-    for i in (1, 3, 2):
-        for m in (0, 1):
-            side_g_copy(i, m).start()
 
     loads[1].wait()
 
@@ -295,6 +293,11 @@
         stat_m[rows, :] = jnp.broadcast_to(mean, (step_rows, 128))
         stat_i[rows, :] = jnp.broadcast_to(inv, (step_rows, 128))
 
+    pl.semaphore_wait(barrier, GROUP - 1 + N_MP - 1)
+    for i in (1, 3, 2):
+        for m in (0, 1):
+            side_g_copy(i, m).start()
+
     @pl.loop(0, n_own)
     def _(o):
         turned_n[o] = normed[:, pl.ds(mult(o * BLK, BLK), BLK)].T
@@ -304,7 +307,7 @@
             side_n_copy(i, m).start()
     for m in (0, 1):
         owner_g = mult(flip(inner, G_MS[m]) * BLK, BLK)
-        side_g[m, 0:toks, :] = gout[:, pl.ds(owner_g, BLK)]
+        side_g[0:toks, m * BLK : m * BLK + BLK] = gout[:, pl.ds(owner_g, BLK)]
         side_n[m, :, 0:toks] = turned_n[flip(inner, N_MS[m])]
 
     lane = lax.broadcasted_iota(jnp.int32, (toks, 128), 1)
@@ -346,8 +349,8 @@
         return remote(
             src,
             bn.at[s, pl.ds(slot_at * toks, toks), :],
-            bn_ss.at[s, k],
-            bn_rs.at[s, k],
+            bn_ss,
+            bn_rs.at[s, min(k, 1)],
             peer((XBIT, CORE, CORE)[k]),
         )
 
@@ -357,8 +360,8 @@
         return remote(
             src,
             bg.at[s, :, pl.ds(slot_at * toks, toks)],
-            bg_ss.at[s, k],
-            bg_rs.at[s, k],
+            bg_ss,
+            bg_rs.at[s, min(k, 1)],
             peer((YBIT, CORE, CORE)[k]),
         )
 
@@ -419,44 +422,132 @@
         for k in (0, 1):
             bg_copy(n_att + c, k).start()
 
-    def z_copy(t, which):
-        if which == 0:
-            return remote(
-                zpart.at[t, pl.ds(send_half, half), :],
-                zr1.at[t],
-                z_ss.at[t, 0],
-                z_rs.at[t, 0],
-                zpeer(1),
+    def piece(t, g, first_row):
+        if t == 0:
+            return pl.ds(first_row, half), pl.ds(mult(g * piece_cols, piece_cols), piece_cols)
+        return pl.ds(mult(first_row + g * piece_rows, piece_rows), piece_rows), pl.ds(0, width)
+
+    def z_far(t, g):
+        rows, cols = piece(t, g, far_rows)
+        to_rows, _ = piece(t, g, 0)
+        return remote(
+            zpart.at[t, rows, cols],
+            zfar.at[t, to_rows, cols],
+            zf_ss,
+            zf_rs.at[t * Z_PARTS + g],
+            beside,
+        )
+
+    def z_near(t, g):
+        rows, cols = piece(t, g, near_rows)
+        to_rows, _ = piece(t, g, 0)
+        return remote(
+            zpart.at[t, rows, cols],
+            znear.at[t, to_rows, cols],
+            zn_ss,
+            zn_rs.at[t * Z_PARTS + g],
+            beside,
+        )
+
+    def z_mid(t, g):
+        rows, cols = piece(t, g, far_rows)
+        to_rows, _ = piece(t, g, 0)
+        return remote(
+            zpart.at[t, rows, cols],
+            zmid.at[t, to_rows, cols],
+            zm_ss,
+            zm_rs.at[t * Z_PARTS + g],
+            across,
+        )
+
+    def z_done(t, g, where):
+        rows, cols = piece(t, g, near_rows)
+        return remote(
+            zout.at[t, rows, cols], zout.at[t, rows, cols], zo_ss, zo_rs.at[t * Z_PARTS + g], where
+        )
+
+    def z_pass(t, g):
+        rows, cols = piece(t, g, far_rows)
+        return remote(
+            zout.at[t, rows, cols], zout.at[t, rows, cols], zw_ss, zw_rs.at[t * Z_PARTS + g], beside
+        )
+
+    def z_send(t, g):
+        @pl.when(end_of_line)
+        def _():
+            z_far(t, g).start()
+            z_near(t, g).start()
+
+    def by_rows(t, body):
+        count = 16 if t == 0 else piece_rows // 2
+
+        @pl.loop(0, (half if t == 0 else piece_rows) // count)
+        def _(r):
+            body(r * count, count)
+
+    def z_first(t, g):
+        z_far(t, g).wait_recv()
+        cols = piece(t, g, 0)[1]
+        first = 0 if t == 0 else g * piece_rows
+
+        def add(at, count):
+            mine = pl.ds(mult(far_rows + first + at, count), count)
+            other = pl.ds(mult(first + at, count), count)
+            zpart[t, mine, cols] = (
+                zpart[t, mine, cols].astype(F32) + zfar[t, other, cols].astype(F32)
+            ).astype(BF16)
+
+        by_rows(t, add)
+        z_mid(t, g).start()
+
+    def z_second(t, g):
+        z_near(t, g).wait_recv()
+        z_mid(t, g).wait_recv()
+        if t == 1:
+            @pl.when(g == 0)
+            def _():
+                cot_load.wait()
+        cols = piece(t, g, 0)[1]
+        first = 0 if t == 0 else g * piece_rows
+
+        def finish(at, count):
+            rows = pl.ds(mult(near_rows + first + at, count), count)
+            there = pl.ds(mult(first + at, count), count)
+            total = (
+                zpart[t, rows, cols].astype(F32)
+                + znear[t, there, cols].astype(F32)
+                + zmid[t, there, cols].astype(F32)
             )
-        if which == 1:
-            return remote(zs2.at[t], zr2.at[t], z_ss.at[t, 1], z_rs.at[t, 1], zpeer(2))
-        if which == 2:
-            rows = pl.ds(my_rows, quarter)
-            where = zpeer(2)
-        else:
-            rows = pl.ds(keep_half, half)
-            where = zpeer(1)
-        return remote(
-            zout.at[t, rows, :], zout.at[t, rows, :], z_ss.at[t, which], z_rs.at[t, which], where
-        )
-
-    def z_second(t):
-        z_copy(t, 0).wait_recv()
-
-        @pl.loop(0, quarter // 16)
-        def _(r):
-            at = r * 16
-            mine = zpart[t, pl.ds(mult(keep_half + send_q + at, 16), 16), :].astype(F32)
-            other = zr1[t, pl.ds(mult(send_q + at, 16), 16), :].astype(F32)
-            zs2[t, pl.ds(mult(at, 16), 16), :] = (mine + other).astype(BF16)
-
-        z_copy(t, 1).start()
-
-    def z_sum(t, at):
-        mine = zpart[t, pl.ds(mult(my_rows + at, 16), 16), :].astype(F32)
-        other = zr1[t, pl.ds(mult(keep_q + at, 16), 16), :].astype(F32)
-        far = zr2[t, pl.ds(mult(at, 16), 16), :].astype(F32)
-        return mine + other + far
+            base = tok[rows, cols].astype(F32)
+            if t == 0:
+                place = near_rows + at + lax.broadcasted_iota(jnp.int32, total.shape, 0)
+                branch = jnp.where(place < total_len, total + obias[:, cols], 0.0)
+                zout[t, rows, cols] = (base + branch).astype(BF16)
+            else:
+                inv = stat_i[rows, 0:1]
+                standard = (base - stat_m[rows, 0:1]) * inv
+                grad = total * gain[...]
+                mean_g = jnp.sum(grad, axis=1, keepdims=True) * (1.0 / width)
+                mean_x = jnp.sum(grad * standard, axis=1, keepdims=True) * (1.0 / width)
+                back = inv * (grad - mean_g - standard * mean_x)
+                zout[t, rows, cols] = (cot_rows[there, :].astype(F32) + back).astype(BF16)
+
+        by_rows(t, finish)
+        z_done(t, g, beside).start()
+        z_done(t, g, across).start()
+
+    def z_third(t, g):
+        z_done(t, g, across).wait_recv()
+        z_pass(t, g).start()
+
+    def z_steps(first, second, third):
+        for number, step in ((first, z_first), (second, z_second), (third, z_third)):
+            for t in (0, 1):
+                low = t * Z_PARTS
+
+                @pl.when(middle & (number >= low) & (number < low + Z_PARTS))
+                def _(number=number, step=step, t=t, low=low):
+                    step(t, number - low)
 
     @pl.loop(0, n_hid)
     def _(c):
@@ -467,7 +558,9 @@
         cols = pl.ds(mult(n * BLK, BLK), BLK)
         zpart[0, :, cols] = (nn(act[...], wd[:, cols]) + nn(att[...], wo[:, cols])).astype(BF16)
 
-    z_copy(0, 0).start()
+        @pl.when(lax.rem(n, n_own // Z_PARTS) == n_own // Z_PARTS - 1)
+        def _():
+            z_send(0, n // (n_own // Z_PARTS))
 
     @pl.loop(0, n_hid)
     def _(c):
@@ -477,6 +570,8 @@
         bn[n_qkv + c, 0:toks, :] = grad
         for k in (0, 1):
             bn_copy(n_qkv + c, k).start()
+
+    z_steps(0, -1, -1)
 
     vz[...] = jnp.zeros_like(vz)
 
@@ -492,31 +587,33 @@
             at = pl.ds(mult(n * BLK + part * 128, 128), 128)
             piece = grad[:, lanes]
             standard = (tok[:, at].astype(F32) - stat_m[...]) * stat_i[...]
-            vz[0, n, 0:1, lanes] = jnp.sum(piece * standard, axis=0, keepdims=True)
-            vz[0, n, 1:2, lanes] = jnp.sum(piece, axis=0, keepdims=True)
-
-    z_copy(1, 0).start()
-
-    def vz_copy(t):
-        return remote(vz.at[t], vzr.at[t], vz_ss.at[t], vz_rs.at[t], zpeer((1, 2)[t]))
+            vz[n, 0:1, lanes] = jnp.sum(piece * standard, axis=0, keepdims=True)
+            vz[n, 1:2, lanes] = jnp.sum(piece, axis=0, keepdims=True)
+
+    def vz_copy(step):
+        return remote(vz, vzr.at[step], vz_ss, vz_rs.at[step], zpeer(step))
+
+    for step in range(1, N_MP):
+        vz_copy(step).start()
+    for g in range(Z_PARTS):
+        z_send(1, g)
 
     def vd_copy(mask):
         return remote(
             vd.at[flip(inner, mask)],
             vdr.at[mask],
-            vd_ss.at[mask],
+            vd_ss,
             vd_rs.at[mask],
             peer(mask),
         )
 
     bs_copy = remote(bsum, bsum_r, bs_ss, bs_rs, peer(YBIT))
-    vz_copy(0).start()
 
     def rn_copy(s):
-        return remote(rsn_s.at[s], rsn_r.at[s], rn_ss.at[s], rn_rs.at[s], peer(YBIT))
+        return remote(rsn_s.at[s], rsn_r.at[s], rn_ss, rn_rs.at[s], peer(YBIT))
 
     def rg_copy(s):
-        return remote(rsg_s.at[s], rsg_r.at[s], rg_ss.at[s], rg_rs.at[s], peer(XBIT))
+        return remote(rsg_s.at[s], rsg_r.at[s], rg_ss, rg_rs.at[s], peer(XBIT))
 
     for i in (1, 2, 3):
         for m in (0, 1):
@@ -524,54 +621,23 @@
             side_n_copy(i, m).wait_recv()
     bsum[...] = jnp.zeros_like(bsum)
 
-    def mixed_rows():
-        z_copy(0, 1).wait_recv()
-
-        @pl.loop(0, quarter // 16)
-        def _(r):
-            at = r * 16
-            rows = pl.ds(mult(my_rows + at, 16), 16)
-            place = my_rows + at + lax.broadcasted_iota(jnp.int32, (16, width), 0)
-            branch = jnp.where(place < total_len, z_sum(0, at) + obias[...], 0.0)
-            zout[0, rows, :] = (tok[rows, :].astype(F32) + branch).astype(BF16)
-
-        z_copy(0, 2).start()
-
-    def grad_rows():
-        z_copy(1, 1).wait_recv()
-        cot_load.wait()
-
-        @pl.loop(0, quarter // 16)
-        def _(r):
-            at = r * 16
-            rows = pl.ds(mult(my_rows + at, 16), 16)
-            inv = stat_i[rows, 0:1]
-            standard = (tok[rows, :].astype(F32) - stat_m[rows, 0:1]) * inv
-            grad = z_sum(1, at) * gain[...]
-            first = jnp.sum(grad, axis=1, keepdims=True) * (1.0 / width)
-            second = jnp.sum(grad * standard, axis=1, keepdims=True) * (1.0 / width)
-            back = inv * (grad - first - standard * second)
-            raw = cot_rows[pl.ds(mult(at, 16), 16), :].astype(F32)
-            zout[1, rows, :] = (raw + back).astype(BF16)
-
-        z_copy(1, 2).start()
-
-    def z_last(t):
-        z_copy(t, 2).wait_recv()
-        z_copy(t, 3).start()
-
-    def vec_second():
-        vz_copy(0).wait_recv()
-        vz[1] = vz[0] + vzr[0]
-        vz_copy(1).start()
-
     def vec_spread():
-        vz_copy(1).wait_recv()
-        vd[...] = vz[1] + vzr[1]
+        total = vz[...]
+        for step in range(1, N_MP):
+            vz_copy(step).wait_recv()
+            total = total + vzr[step]
+        vd[...] = total
         for owner in range(n_own):
             vd[owner, 2:3, :] = gsum[0:1, owner * BLK : owner * BLK + BLK]
         for mask in range(1, GROUP):
             vd_copy(mask).start()
+
+    z_steps(1, 0, -1)
+    def pair_n(p):
+        return bn.at[p, pl.ds(2 * toks, 2 * toks), :]
+
+    def pair_g(p):
+        return bg.at[p, :, pl.ds(2 * toks, 2 * toks)]
 
     ones_row = jnp.ones((8, 4 * toks), BF16)
 
@@ -590,80 +656,31 @@
         @pl.when(s > 0)
         def _():
             p = s - 1
-            bn_copy(p, 1).wait_recv()
-            bn_copy(p, 2).wait_recv()
-            rsn_s[p] = nn(side_n[1], bn[p]).astype(BF16)
+            pltpu.make_async_copy(pair_n(p), pair_n(p), bn_rs.at[p, 1]).wait()
+            both = nn(side_n[...].reshape(2 * BLK, 4 * toks), bn[p])
+            rsn_s[p] = both[BLK:, :].astype(BF16)
             rn_copy(p).start()
             bsum[pl.ds(p, 1), :] = nn(ones_row, bn[p])[0:1, :]
+            bn[p, 2 * toks : 3 * toks, :] = both[:BLK, :].astype(BF16)
 
         @pl.when((s > 0) & (s <= g_chunks))
         def _():
             p = s - 1
-            bg_copy(p, 1).wait_recv()
-            bg_copy(p, 2).wait_recv()
-            rsg_s[p] = nn(bg[p], side_g[1]).astype(BF16)
+            pltpu.make_async_copy(pair_g(p), pair_g(p), bg_rs.at[p, 1]).wait()
+            both = nn(bg[p], side_g[...])
+            rsg_s[p] = both[:, BLK:].astype(BF16)
             rg_copy(p).start()
-
-        @pl.when(s == 5)
+            bg[p, :, 2 * toks : 3 * toks] = both[:, :BLK].astype(BF16)
+
+        @pl.when((s >= 6) & (lax.rem(s, 2) == 0))
         def _():
-            z_second(0)
-            vec_second()
-
-        @pl.when(s == 9)
-        def _():
-            z_second(1)
-            mixed_rows()
-            vec_spread()
+            e = (s - 6) // 2
+            z_steps(2 + e, 1 + e, e - 1)
 
     bs_copy.start()
-
-    def out_n(s):
-        return pltpu.make_async_copy(
-            stage_n.at[lax.rem(s, 2)],
-            gradn_h.at[:, pl.ds(mult(s * BLK, BLK), BLK)],
-            on_sem.at[lax.rem(s, 2)],
-        )
-
-    def out_g(s):
-        return pltpu.make_async_copy(
-            stage_g.at[lax.rem(s, 2)],
-            gradg_h.at[pl.ds(mult(s * BLK, BLK), BLK), :],
-            og_sem.at[lax.rem(s, 2)],
-        )
-
-    @pl.loop(0, n_chunks)
-    def _(s):
-        @pl.when(s >= 2)
-        def _():
-            out_n(s - 2).wait()
-
-        mine = nn(side_n[0], bn[s])
-        rn_copy(s).wait_recv()
-        stage_n[lax.rem(s, 2)] = mine + rsn_r[s].astype(F32)
-        out_n(s).start()
-
-        @pl.when(s == 0)
-        def _():
-            z_last(0)
-
-        @pl.when(s == 1)
-        def _():
-            grad_rows()
-
-        @pl.when(s < g_chunks)
-        def _():
-            @pl.when(s >= 2)
-            def _():
-                out_g(s - 2).wait()
-
-            mine_g = nn(bg[s], side_g[0])
-            rg_copy(s).wait_recv()
-            stage_g[lax.rem(s, 2)] = mine_g + rsg_r[s].astype(F32)
-            out_g(s).start()
-
-        @pl.when(s == 6)
-        def _():
-            z_last(1)
+    vec_spread()
+    for numbers in ((7, 6, 4), (8, 7, 5), (8, 8, 6), (8, 8, 7)):
+        z_steps(*numbers)
 
     bs_copy.wait_recv()
     sums = vd[inner]
@@ -673,39 +690,84 @@
     vec_o[0:8, :] = sums
     vec_o[8:, :] = bsum[...] + bsum_r[...]
 
-    z_outs = []
-    for t, out_h in enumerate((mixed_h, gtok_h)):
-        z_copy(t, 3).wait_recv()
-        z_outs.append(pltpu.make_async_copy(zout.at[t], out_h, oz_sem.at[t]))
-        z_outs[t].start()
-
-    for i in (1, 2, 3):
-        for m in (0, 1):
-            side_g_copy(i, m).wait_send()
-            side_n_copy(i, m).wait_send()
-
     @pl.loop(0, n_chunks)
     def _(s):
-        for k in range(3):
-            bn_copy(s, k).wait_send()
-        rn_copy(s).wait_send()
+        rn_copy(s).wait_recv()
 
     @pl.loop(0, g_chunks)
     def _(s):
-        for k in range(3):
-            bg_copy(s, k).wait_send()
-        rg_copy(s).wait_send()
-
-    for t in (0, 1):
-        for which in range(4):
-            z_copy(t, which).wait_send()
-        vz_copy(t).wait_send()
-    for mask in range(1, GROUP):
-        vd_copy(mask).wait_send()
+        rg_copy(s).wait_recv()
+
+    def sent(ref, sem):
+        pltpu.make_async_copy(ref, ref, sem).wait()
+
+    sent(side_n.at[:, :, pl.ds(0, 3 * toks)], sn_ss)
+    sent(side_g.at[pl.ds(0, 3 * toks), :], sg_ss)
+    sent(bn.at[:, pl.ds(0, 3 * toks), :], bn_ss)
+    sent(bg.at[:, :, pl.ds(0, 3 * toks)], bg_ss)
+    sent(rsn_s, rn_ss)
+    sent(rsg_s, rg_ss)
+    sent(vzr.at[pl.ds(1, N_MP - 1)], vz_ss)
+    sent(vdr.at[pl.ds(1, GROUP - 1)], vd_ss)
     bs_copy.wait_send()
-    for back in (2, 1):
-        out_n(n_chunks - back).wait()
-        out_g(g_chunks - back).wait()
+
+    @pl.when(end_of_line)
+    def _():
+        sent(zfar, zf_ss)
+        sent(znear, zn_ss)
+        for t in (0, 1):
+            for g in range(Z_PARTS):
+                z_done(t, g, beside).wait_recv()
+                z_pass(t, g).wait_recv()
+        cot_load.wait()
+
+    @pl.when(middle)
+    def _():
+        sent(zmid, zm_ss)
+        sent(zout, zo_ss)
+        sent(zmid, zw_ss)
+
+
+def write_kernel(n_qkv, n_att, bn, bg, rsn, rsg, zout, vec, mixed_h, gtok_h, gain_o, shift_o, gq_h, bq_o, gk_h, bk_o, gv_h, bv_o, go_h, gu_h, bu_o, gd_h, ob_o, stage, sems, zsem):
+    n_chunks, n_g = bn.shape[0], bg.shape[0]
+    toks = zout.shape[1]
+    slots = stage.shape[0]
+    z_outs = [
+        pltpu.make_async_copy(zout.at[t], out, zsem.at[t]) for t, out in enumerate((mixed_h, gtok_h))
+    ]
+    for out in z_outs:
+        out.start()
+    places = []
+    for s in range(n_chunks):
+        if s < n_qkv:
+            out, at = (gq_h, gk_h, gv_h)[s // n_att], s % n_att
+        else:
+            out, at = gu_h, s - n_qkv
+        places.append((True, s, out.at[:, pl.ds(at * BLK, BLK)]))
+    for s in range(n_g):
+        out, at = (go_h, s) if s < n_att else (gd_h, s - n_att)
+        places.append((False, s, out.at[pl.ds(at * BLK, BLK), :]))
+    copies = []
+    for number, (first, s, place) in enumerate(places):
+        slot = number % slots
+        if number >= slots:
+            copies[number - slots].wait()
+        if first:
+            value = bn[s, 2 * toks : 3 * toks, :].astype(F32) + rsn[s].astype(F32)
+        else:
+            value = bg[s, :, 2 * toks : 3 * toks].astype(F32) + rsg[s].astype(F32)
+        stage[slot] = value
+        copies.append(pltpu.make_async_copy(stage.at[slot], place, sems.at[slot]))
+        copies[number].start()
+    for row, out in enumerate((gain_o, shift_o, ob_o)):
+        out[...] = vec[row]
+    row = 8
+    for out in (bq_o, bk_o, bv_o, bu_o):
+        for at in range(out.shape[0] // BLK):
+            out[at * BLK : at * BLK + BLK] = vec[row]
+            row += 1
+    for copy in copies[-slots:]:
+        copy.wait()
     for out in z_outs:
         out.wait()
 
@@ -718,7 +780,7 @@
     g_chunks = (heads_w + hidden) // BLK
     n_own = width // BLK
     n_vec = -(-n_chunks // 8) * 8
-    half, quarter = toks // 2, toks // 4
+    half = toks // 2
     dma = pltpu.SemaphoreType.DMA
     vmem = pltpu.VMEM
     scratch = [
@@ -732,13 +794,9 @@
         vmem(w_out.shape, BF16),
         vmem(w_up.shape, BF16),
         vmem(w_down.shape, BF16),
-        vmem((n_chunks, 4 * toks, BLK), BF16),
-        vmem((g_chunks, BLK, 4 * toks), BF16),
         vmem((2, BLK, 4 * toks), BF16),
-        vmem((2, 4 * toks, BLK), BF16),
+        vmem((4 * toks, 2 * BLK), BF16),
         vmem((n_chunks, BLK, BLK), BF16),
-        vmem((n_chunks, BLK, BLK), BF16),
-        vmem((g_chunks, BLK, BLK), BF16),
         vmem((g_chunks, BLK, BLK), BF16),
         vmem((toks, hidden), BF16),
         vmem((toks, hidden), BF16),
@@ -754,67 +812,70 @@
         vmem((toks, 128), F32),
         vmem((toks, 128), F32),
         vmem((toks, 128), F32),
-        vmem((2, BLK, BLK), F32),
-        vmem((2, BLK, BLK), F32),
         vmem((2, toks, width), BF16),
         vmem((2, half, width), BF16),
-        vmem((2, quarter, width), BF16),
-        vmem((2, quarter, width), BF16),
-        vmem((2, toks, width), BF16),
-        vmem((2, n_own, 8, BLK), F32),
-        vmem((2, n_own, 8, BLK), F32),
+        vmem((2, half, width), BF16),
+        vmem((2, half, width), BF16),
+        vmem((n_own, 8, BLK), F32),
+        vmem((N_MP, n_own, 8, BLK), F32),
         vmem((n_own, 8, BLK), F32),
         vmem((GROUP, 8, BLK), F32),
         vmem((8, width), F32),
         vmem((n_vec, BLK), F32),
         vmem((n_vec, BLK), F32),
-        vmem((quarter, width), BF16),
+        vmem((half, width), BF16),
         dma((7,)),
         dma((hidden // BLK,)),
         dma((hidden // BLK,)),
+        dma,
         dma((3, 2)),
+        dma,
         dma((3, 2)),
-        dma((3, 2)),
-        dma((3, 2)),
-        dma((n_chunks, 3)),
-        dma((n_chunks, 3)),
-        dma((g_chunks, 3)),
-        dma((g_chunks, 3)),
+        dma,
+        dma((n_chunks, 2)),
+        dma,
+        dma((g_chunks, 2)),
+        dma,
         dma((n_chunks,)),
-        dma((n_chunks,)),
+        dma,
         dma((g_chunks,)),
-        dma((g_chunks,)),
-        dma((2, 4)),
-        dma((2, 4)),
-        dma((2,)),
-        dma((2,)),
+        dma,
+        dma((2 * Z_PARTS,)),
+        dma,
+        dma((2 * Z_PARTS,)),
+        dma,
+        dma((2 * Z_PARTS,)),
+        dma,
+        dma((2 * Z_PARTS,)),
+        dma,
+        dma((2 * Z_PARTS,)),
+        dma,
+        dma((N_MP,)),
+        dma,
         dma((GROUP,)),
-        dma((GROUP,)),
-        dma,
-        dma,
-        dma((2,)),
-        dma((2,)),
-        dma((2,)),
+        dma,
+        dma,
     ]
     anyspace = pl.BlockSpec(memory_space=pl.ANY)
     local = pl.BlockSpec(memory_space=pltpu.VMEM)
     row = lambda value: value.reshape(1, -1)
-    mixed, grad_tokens, grad_n, grad_g, vec = pl.pallas_call(
+    kept = pl.pallas_call(
         functools.partial(layer_kernel, n_chunks, g_chunks),
         out_shape=(
-            jax.ShapeDtypeStruct((toks, width), BF16),
-            jax.ShapeDtypeStruct((toks, width), BF16),
-            jax.ShapeDtypeStruct((BLK, n_chunks * BLK), F32),
-            jax.ShapeDtypeStruct((g_chunks * BLK, BLK), F32),
-            jax.ShapeDtypeStruct((8 + n_vec, BLK), F32),
+            vmem((n_chunks, 4 * toks, BLK), BF16),
+            vmem((g_chunks, BLK, 4 * toks), BF16),
+            vmem((n_chunks, BLK, BLK), BF16),
+            vmem((g_chunks, BLK, BLK), BF16),
+            vmem((2, toks, width), BF16),
+            vmem((8 + n_vec, BLK), F32),
         ),
         in_specs=[pl.BlockSpec(memory_space=pltpu.SMEM), anyspace, anyspace]
         + [local] * 7
         + [anyspace] * 6,
-        out_specs=(anyspace, anyspace, anyspace, anyspace, local),
+        out_specs=(local,) * 6,
         scratch_shapes=scratch,
         compiler_params=pltpu.CompilerParams(
-            collective_id=0, has_side_effects=True, vmem_limit_bytes=67043328
+            collective_id=0, has_side_effects=True, vmem_limit_bytes=MAIN_VMEM
         ),
     )(
         lengths,
@@ -834,29 +895,35 @@
         w_up,
         w_down,
     )
-    sent_q = grad_n[:, :heads_w]
-    sent_k = grad_n[:, heads_w : 2 * heads_w]
-    sent_v = grad_n[:, 2 * heads_w : 3 * heads_w]
-    sent_up = grad_n[:, 3 * heads_w :]
-    per = heads_w // BLK
-    bias = vec[8 : 8 + n_chunks]
-    return (
-        mixed,
-        grad_tokens,
-        vec[0],
-        vec[1],
-        sent_q,
-        bias[:per].reshape(-1),
-        sent_k,
-        bias[per : 2 * per].reshape(-1),
-        sent_v,
-        bias[2 * per : 3 * per].reshape(-1),
-        grad_g[:heads_w],
-        sent_up,
-        bias[3 * per :].reshape(-1),
-        grad_g[heads_w:],
-        vec[2],
+    f32 = lambda *shape: jax.ShapeDtypeStruct(shape, F32)
+    low = jax.ShapeDtypeStruct((toks, width), BF16)
+    spec = lambda kind: anyspace if len(kind.shape) == 2 else local
+    outs = (
+        low,
+        low,
+        f32(BLK),
+        f32(BLK),
+        f32(BLK, heads_w),
+        f32(heads_w),
+        f32(BLK, heads_w),
+        f32(heads_w),
+        f32(BLK, heads_w),
+        f32(heads_w),
+        f32(heads_w, BLK),
+        f32(BLK, hidden),
+        f32(hidden),
+        f32(hidden, BLK),
+        f32(BLK),
     )
+    slots = 6
+    return pl.pallas_call(
+        functools.partial(write_kernel, 3 * heads_w // BLK, heads_w // BLK),
+        out_shape=outs,
+        in_specs=[local] * 6,
+        out_specs=tuple(spec(kind) for kind in outs),
+        scratch_shapes=[vmem((slots, BLK, BLK), F32), dma((slots,)), dma((2,))],
+        compiler_params=pltpu.CompilerParams(vmem_limit_bytes=4 * 2**20),
+    )(*kept)
 
 
 def make_body(n_dp, n_mp):

time: 136 us -> 101 us (0.74)
  Pallas kernels: 120 us -> 100 us
  local copies, waits for them, and re-layouts: 15.6 us -> 0 us
    pallas_call x1, Pallas kernels: 120 us -> 95.5 us  [layer(): pl.pallas_call(functools.partial(layer_kernel, n_chunks, g_chunks), out_s...]
    slice x5 -> x0, local copies, waits for them, and re-layouts: 9.12 us -> none  [the longest x1 3.2 us: layer(): grad_g[heads_w:]]
    unnamed x14 -> x0, local copies, waits for them, and re-layouts: 6.46 us -> none
    pallas_call x0 -> x1, Pallas kernels: none -> 4.73 us  [layer(): pl.pallas_call(functools.partial(write_kernel, 3 * heads_w // BLK, heads_...]
where the time goes in v3:
time: 101 us
  Pallas kernels  100 us (99%)
    pallas_call x1, Pallas kernels, layer(): pl.pallas_call(functools.partial(layer_kernel, n_chunks, g_chunks), out_s...  95.5 us
    pallas_call x1, Pallas kernels, layer(): pl.pallas_call(functools.partial(write_kernel, 3 * heads_w // BLK, heads_...  4.73 us

profile of v3, /device:TPU:0, one launch (start us, length us, event | category | flops | bytes accessed | tf_op | source)
XLA Modules:
  0.0 100.8 jit_solution(17517494301340653323)
XLA Ops:
  0.7 95.5 %shard_map.271 = (bf16[14,1024,256]{2,1,0:T(8,128)(2,1)S(1)}, bf16[10,256,1024]{2,1,0:T(8,128)(2,1)S(1)}, bf16[14,256,256]{2,1,0:T(8,128)(2,1)S(1)}, bf16[10,256...) custom-call(s32[1,4]{1,0:T(1,128)} %lens.1, bf16[256,2048]{1,0:T(8,128)(2,1)} %tok_h.1, ...), custom_call_target="tpu_custom_call" | custom-call | tf_op jit(solution)/shard_map/pallas_call | solution.py:862
  96.1 4.7 %shard_map.272 = (bf16[256,2048]{1,0:T(8,128)(2,1)}, bf16[256,2048]{1,0:T(8,128)(2,1)}, f32[256]{0:T(256)}, f32[256]{0:T(256)}, f32[256,512]{1,0:T(8,128)}, /*in...) custom-call(bf16[14,1024,256]{2,1,0:T(8,128)(2,1)S(1)} %get-tuple-el, ...), custom_call_target="tpu_custom_call" | custom-call | tf_op jit(solution)/shard_map/pallas_call | solution.py:919

commit v4 on v3

--- a/solution.py
+++ b/solution.py
@@ -14,8 +14,11 @@
 GROUP = 8
 CORE, XBIT, YBIT = 1, 2, 4
 BLK = 256
+WIDE = 512
 N_MP = 4
-Z_PARTS = 4
+Z_PARTS = 8
+Z_LAG = 2
+Z_TICKS = ((0, 2), (3, 3), (6, 4), (7, 5), (8, 6), (9, 7), (10, 8), (11, 9), (12, 10), (13, 11))
 F32 = jnp.float32
 BF16 = jnp.bfloat16
 MESH = pl.DeviceIdType.MESH
@@ -110,6 +113,7 @@
     zfar,
     znear,
     zmid,
+    vzl,
     vz,
     vzr,
     vd,
@@ -259,25 +263,45 @@
         gout[rows, :] = value.astype(BF16)
         gsum[0:1, :] = gsum[0:1, :] + jnp.sum(value, axis=0, keepdims=True)
 
-    def side_g_copy(i, m):
-        owner = flip(inner, G_JS[i] ^ G_MS[m])
-        return remote(
-            gout.at[:, pl.ds(mult(owner * BLK, BLK), BLK)],
-            side_g.at[pl.ds(i * toks, toks), pl.ds(m * BLK, BLK)],
-            sg_ss,
-            sg_rs.at[i - 1, m],
-            peer(G_JS[i]),
-        )
-
-    def side_n_copy(i, m):
-        owner = flip(inner, N_JS[i] ^ N_MS[m])
-        return remote(
-            turned_n.at[owner],
-            side_n.at[m, :, pl.ds(i * toks, toks)],
-            sn_ss,
-            sn_rs.at[i - 1, m],
-            peer(N_JS[i]),
-        )
+    parity = lax.rem(zed, 2)
+
+    def cross_core(index, times):
+        return index + times * (1 - 2 * lax.rem(index, 2))
+
+    def side_copy(to_side, ssem, rsem, chip_bit, other_bit, source, kind, m):
+        owner_bit = m * other_bit
+        if kind == 0:
+            target = flip(cross_core(inner, parity), chip_bit)
+            where = (outer + target, zed)
+            slot_at = 1 + 2 * parity
+        elif kind == 1:
+            target = flip(inner, CORE)
+            where = (outer + target, zed)
+            slot_at = 2
+        else:
+            slot_at = 1 + 2 * parity
+            where = beside
+        place = to_side(m, mult(slot_at * toks, toks))
+        src = place if kind == 2 else source(flip(target, owner_bit))
+        return remote(src, place, ssem, rsem.at[kind, m], where)
+
+    def side_g_copy(kind, m):
+        def source(owner):
+            return gout.at[:, pl.ds(mult(owner * BLK, BLK), BLK)]
+
+        def to_side(m, at):
+            return side_g.at[pl.ds(at, toks), pl.ds(m * BLK, BLK)]
+
+        return side_copy(to_side, sg_ss, sg_rs, YBIT, XBIT, source, kind, m)
+
+    def side_n_copy(kind, m):
+        def source(owner):
+            return turned_n.at[owner]
+
+        def to_side(m, at):
+            return side_n.at[pl.ds(m * BLK, BLK), pl.ds(at, toks)]
+
+        return side_copy(to_side, sn_ss, sn_rs, XBIT, YBIT, source, kind, m)
 
     loads[1].wait()
 
@@ -294,21 +318,27 @@
         stat_i[rows, :] = jnp.broadcast_to(inv, (step_rows, 128))
 
     pl.semaphore_wait(barrier, GROUP - 1 + N_MP - 1)
-    for i in (1, 3, 2):
-        for m in (0, 1):
-            side_g_copy(i, m).start()
+    for m in (0, 1):
+        side_g_copy(0, m).start()
+    first_at = flip(cross_core(inner, parity), XBIT)
+    for m in (0, 1):
+        owner = flip(first_at, N_MS[m])
+        turned_n[owner] = normed[:, pl.ds(mult(owner * BLK, BLK), BLK)].T
+        side_n_copy(0, m).start()
 
     @pl.loop(0, n_own)
     def _(o):
-        turned_n[o] = normed[:, pl.ds(mult(o * BLK, BLK), BLK)].T
-
-    for i in (1, 3, 2):
-        for m in (0, 1):
-            side_n_copy(i, m).start()
+        @pl.when((o != first_at) & (o != flip(first_at, YBIT)))
+        def _():
+            turned_n[o] = normed[:, pl.ds(mult(o * BLK, BLK), BLK)].T
+
+    for m in (0, 1):
+        side_g_copy(1, m).start()
+        side_n_copy(1, m).start()
     for m in (0, 1):
         owner_g = mult(flip(inner, G_MS[m]) * BLK, BLK)
         side_g[0:toks, m * BLK : m * BLK + BLK] = gout[:, pl.ds(owner_g, BLK)]
-        side_n[m, :, 0:toks] = turned_n[flip(inner, N_MS[m])]
+        side_n[m * BLK : m * BLK + BLK, 0:toks] = turned_n[flip(inner, N_MS[m])]
 
     lane = lax.broadcasted_iota(jnp.int32, (toks, 128), 1)
     slot = lax.broadcasted_iota(jnp.int32, (toks, 128), 0)
@@ -365,12 +395,22 @@
             peer((YBIT, CORE, CORE)[k]),
         )
 
+    def side_pass(m):
+        for copy_of in (side_g_copy, side_n_copy):
+            copy_of(0, m).wait_recv()
+            copy_of(2, m).start()
+
+    side_pass(0)
     low_lane = lax.broadcasted_iota(jnp.int32, (1, 128), 1) < HD
     head_mask = (jnp.where(low_lane, 1.0, 0.0).astype(BF16), jnp.where(low_lane, 0.0, 1.0).astype(BF16))
     low_full = lax.broadcasted_iota(jnp.int32, (toks, 128), 1) < HD
 
     @pl.loop(0, n_att)
     def _(n):
+        @pl.when(n == n_att - 1)
+        def _():
+            side_pass(1)
+
         for part in range(BLK // 128):
             at = pl.ds(mult(n * BLK + part * 128, 128), 128)
             lanes = slice(part * 128, part * 128 + 128)
@@ -405,10 +445,13 @@
             for kind in range(3):
                 bn_copy(n + kind * n_att, k).start()
 
-    @pl.loop(0, n_hid)
-    def _(c):
-        cols = pl.ds(mult(c * BLK, BLK), BLK)
-        wu_load(c).wait()
+    per_wide = WIDE // BLK
+
+    @pl.loop(0, hidden // WIDE)
+    def _(w):
+        cols = pl.ds(mult(w * WIDE, WIDE), WIDE)
+        for part in range(per_wide):
+            wu_load(w * per_wide + part).wait()
         up = nn(normed[...], wu[:, cols]) + bup[:, cols]
         square = up * up
         tanh = jnp.tanh(GELU_A * up * (1.0 + GELU_B * square))
@@ -418,9 +461,11 @@
             0.5 * (1.0 + tanh)
             + 0.5 * up * (1.0 - tanh * tanh) * (GELU_A * (1.0 + 3.0 * GELU_B * square))
         ).astype(BF16)
-        bg[n_att + c, :, 0:toks] = active.T
-        for k in (0, 1):
-            bg_copy(n_att + c, k).start()
+        for part in range(per_wide):
+            c = n_att + w * per_wide + part
+            bg[c, :, 0:toks] = active[:, part * BLK : part * BLK + BLK].T
+            for k in (0, 1):
+                bg_copy(c, k).start()
 
     def piece(t, g, first_row):
         if t == 0:
@@ -472,131 +517,125 @@
             zout.at[t, rows, cols], zout.at[t, rows, cols], zw_ss, zw_rs.at[t * Z_PARTS + g], beside
         )
 
-    def z_send(t, g):
+    def z_send(copies):
         @pl.when(end_of_line)
         def _():
-            z_far(t, g).start()
-            z_near(t, g).start()
-
-    def by_rows(t, body):
-        count = 16 if t == 0 else piece_rows // 2
-
-        @pl.loop(0, (half if t == 0 else piece_rows) // count)
-        def _(r):
-            body(r * count, count)
+            for copy in copies:
+                copy.start()
 
     def z_first(t, g):
         z_far(t, g).wait_recv()
-        cols = piece(t, g, 0)[1]
-        first = 0 if t == 0 else g * piece_rows
-
-        def add(at, count):
-            mine = pl.ds(mult(far_rows + first + at, count), count)
-            other = pl.ds(mult(first + at, count), count)
-            zpart[t, mine, cols] = (
-                zpart[t, mine, cols].astype(F32) + zfar[t, other, cols].astype(F32)
-            ).astype(BF16)
-
-        by_rows(t, add)
+        rows, cols = piece(t, g, far_rows)
+        there, _ = piece(t, g, 0)
+        zpart[t, rows, cols] = (
+            zpart[t, rows, cols].astype(F32) + zfar[t, there, cols].astype(F32)
+        ).astype(BF16)
         z_mid(t, g).start()
 
     def z_second(t, g):
         z_near(t, g).wait_recv()
         z_mid(t, g).wait_recv()
-        if t == 1:
+        rows, cols = piece(t, g, near_rows)
+        there, _ = piece(t, g, 0)
+        total = (
+            zpart[t, rows, cols].astype(F32)
+            + znear[t, there, cols].astype(F32)
+            + zmid[t, there, cols].astype(F32)
+        )
+        base = tok[rows, cols].astype(F32)
+        if t == 0:
+            place = near_rows + lax.broadcasted_iota(jnp.int32, total.shape, 0)
+            branch = jnp.where(place < total_len, total + obias[:, cols], 0.0)
+            zout[t, rows, cols] = (base + branch).astype(BF16)
+        else:
             @pl.when(g == 0)
             def _():
                 cot_load.wait()
-        cols = piece(t, g, 0)[1]
-        first = 0 if t == 0 else g * piece_rows
-
-        def finish(at, count):
-            rows = pl.ds(mult(near_rows + first + at, count), count)
-            there = pl.ds(mult(first + at, count), count)
-            total = (
-                zpart[t, rows, cols].astype(F32)
-                + znear[t, there, cols].astype(F32)
-                + zmid[t, there, cols].astype(F32)
-            )
-            base = tok[rows, cols].astype(F32)
-            if t == 0:
-                place = near_rows + at + lax.broadcasted_iota(jnp.int32, total.shape, 0)
-                branch = jnp.where(place < total_len, total + obias[:, cols], 0.0)
-                zout[t, rows, cols] = (base + branch).astype(BF16)
-            else:
-                inv = stat_i[rows, 0:1]
-                standard = (base - stat_m[rows, 0:1]) * inv
-                grad = total * gain[...]
-                mean_g = jnp.sum(grad, axis=1, keepdims=True) * (1.0 / width)
-                mean_x = jnp.sum(grad * standard, axis=1, keepdims=True) * (1.0 / width)
-                back = inv * (grad - mean_g - standard * mean_x)
-                zout[t, rows, cols] = (cot_rows[there, :].astype(F32) + back).astype(BF16)
-
-        by_rows(t, finish)
+
+            inv = stat_i[rows, 0:1]
+            standard = (base - stat_m[rows, 0:1]) * inv
+            grad = total * gain[...]
+            mean_g = jnp.sum(grad, axis=1, keepdims=True) * (1.0 / width)
+            mean_x = jnp.sum(grad * standard, axis=1, keepdims=True) * (1.0 / width)
+            back = inv * (grad - mean_g - standard * mean_x)
+            zout[t, rows, cols] = (cot_rows[there, :].astype(F32) + back).astype(BF16)
+        z_done(t, g, across).start()
         z_done(t, g, beside).start()
-        z_done(t, g, across).start()
 
     def z_third(t, g):
         z_done(t, g, across).wait_recv()
         z_pass(t, g).start()
 
-    def z_steps(first, second, third):
-        for number, step in ((first, z_first), (second, z_second), (third, z_third)):
-            for t in (0, 1):
+    def z_tick(number, kinds=(0, 1)):
+        for step, lag in ((z_first, 0), (z_second, Z_LAG), (z_third, 2 * Z_LAG)):
+            at = number - lag
+            for t in kinds:
                 low = t * Z_PARTS
-
-                @pl.when(middle & (number >= low) & (number < low + Z_PARTS))
-                def _(number=number, step=step, t=t, low=low):
-                    step(t, number - low)
+                if isinstance(number, int):
+                    if low <= at < low + Z_PARTS:
+                        pl.when(middle)(functools.partial(step, t, at - low))
+                else:
+                    inside = (at >= low) & (at < low + Z_PARTS)
+                    pl.when(middle & inside)(functools.partial(step, t, at - low))
 
     @pl.loop(0, n_hid)
     def _(c):
         wd_load(c).wait()
 
-    @pl.loop(0, n_own)
+    @pl.loop(0, width // WIDE)
     def _(n):
-        cols = pl.ds(mult(n * BLK, BLK), BLK)
+        cols = pl.ds(mult(n * WIDE, WIDE), WIDE)
         zpart[0, :, cols] = (nn(act[...], wd[:, cols]) + nn(att[...], wo[:, cols])).astype(BF16)
-
-        @pl.when(lax.rem(n, n_own // Z_PARTS) == n_own // Z_PARTS - 1)
-        def _():
-            z_send(0, n // (n_own // Z_PARTS))
-
-    @pl.loop(0, n_hid)
-    def _(c):
-        cols = pl.ds(mult(c * BLK, BLK), BLK)
+        for part in range(WIDE // piece_cols):
+            g = n * (WIDE // piece_cols) + part
+            z_send([z_far(0, g), z_near(0, g)])
+
+    @pl.loop(0, hidden // WIDE)
+    def _(w):
+        cols = pl.ds(mult(w * WIDE, WIDE), WIDE)
         grad = (nt(gout[...], wd[cols, :]) * dact[:, cols].astype(F32)).astype(BF16)
         dact[:, cols] = grad
-        bn[n_qkv + c, 0:toks, :] = grad
-        for k in (0, 1):
-            bn_copy(n_qkv + c, k).start()
-
-    z_steps(0, -1, -1)
-
-    vz[...] = jnp.zeros_like(vz)
-
-    @pl.loop(0, n_own)
+        for part in range(per_wide):
+            c = n_qkv + w * per_wide + part
+            bn[c, 0:toks, :] = grad[:, part * BLK : part * BLK + BLK]
+            for k in (0, 1):
+                bn_copy(c, k).start()
+
+    z_tick(0)
+
+
+    @pl.loop(0, width // WIDE)
     def _(n):
-        cols = pl.ds(mult(n * BLK, BLK), BLK)
+        cols = pl.ds(mult(n * WIDE, WIDE), WIDE)
         grad = nt(dact[...], wu[cols, :])
         for kind, weight in enumerate((wq, wk, wv)):
             grad = grad + nt(gqkv[:, kind * heads_w : (kind + 1) * heads_w], weight[cols, :])
         zpart[1, :, cols] = grad.astype(BF16)
-        for part in range(BLK // 128):
+
+        @pl.when(n == 2)
+        def _():
+            z_tick(1)
+
+        for part in range(WIDE // 128):
             lanes = slice(part * 128, part * 128 + 128)
-            at = pl.ds(mult(n * BLK + part * 128, 128), 128)
-            piece = grad[:, lanes]
+            at = pl.ds(mult(n * WIDE + part * 128, 128), 128)
+            owner = n * per_wide + part * 128 // BLK
+            into = slice(part * 128 % BLK, part * 128 % BLK + 128)
+            piece_of = grad[:, lanes]
             standard = (tok[:, at].astype(F32) - stat_m[...]) * stat_i[...]
-            vz[n, 0:1, lanes] = jnp.sum(piece * standard, axis=0, keepdims=True)
-            vz[n, 1:2, lanes] = jnp.sum(piece, axis=0, keepdims=True)
+            vzl[owner, 0:1, into] = jnp.sum(piece_of * standard, axis=0, keepdims=True)
+            vzl[owner, 1:2, into] = jnp.sum(piece_of, axis=0, keepdims=True)
 
     def vz_copy(step):
         return remote(vz, vzr.at[step], vz_ss, vz_rs.at[step], zpeer(step))
 
+    for owner in range(n_own):
+        vz[owner : owner + 1, :] = vzl[owner, 0:1, :]
+        vz[n_own + owner : n_own + owner + 1, :] = vzl[owner, 1:2, :]
     for step in range(1, N_MP):
         vz_copy(step).start()
     for g in range(Z_PARTS):
-        z_send(1, g)
+        z_send([z_far(1, g), z_near(1, g)])
 
     def vd_copy(mask):
         return remote(
@@ -615,10 +654,10 @@
     def rg_copy(s):
         return remote(rsg_s.at[s], rsg_r.at[s], rg_ss, rg_rs.at[s], peer(XBIT))
 
-    for i in (1, 2, 3):
+    for kind in (1, 2):
         for m in (0, 1):
-            side_g_copy(i, m).wait_recv()
-            side_n_copy(i, m).wait_recv()
+            side_g_copy(kind, m).wait_recv()
+            side_n_copy(kind, m).wait_recv()
     bsum[...] = jnp.zeros_like(bsum)
 
     def vec_spread():
@@ -626,20 +665,21 @@
         for step in range(1, N_MP):
             vz_copy(step).wait_recv()
             total = total + vzr[step]
-        vd[...] = total
+        vd[...] = jnp.zeros_like(vd)
         for owner in range(n_own):
+            vd[owner, 0:1, :] = total[owner : owner + 1, :]
+            vd[owner, 1:2, :] = total[n_own + owner : n_own + owner + 1, :]
             vd[owner, 2:3, :] = gsum[0:1, owner * BLK : owner * BLK + BLK]
         for mask in range(1, GROUP):
             vd_copy(mask).start()
 
-    z_steps(1, 0, -1)
     def pair_n(p):
         return bn.at[p, pl.ds(2 * toks, 2 * toks), :]
 
     def pair_g(p):
         return bg.at[p, :, pl.ds(2 * toks, 2 * toks)]
 
-    ones_row = jnp.ones((8, 4 * toks), BF16)
+    side_n[2 * BLK :, :] = jnp.ones((16, 4 * toks), BF16)
 
     @pl.loop(0, n_chunks + 1)
     def _(s):
@@ -657,10 +697,10 @@
         def _():
             p = s - 1
             pltpu.make_async_copy(pair_n(p), pair_n(p), bn_rs.at[p, 1]).wait()
-            both = nn(side_n[...].reshape(2 * BLK, 4 * toks), bn[p])
-            rsn_s[p] = both[BLK:, :].astype(BF16)
+            both = nn(side_n[...], bn[p])
+            rsn_s[p] = both[BLK : 2 * BLK, :].astype(BF16)
             rn_copy(p).start()
-            bsum[pl.ds(p, 1), :] = nn(ones_row, bn[p])[0:1, :]
+            bsum[pl.ds(p, 1), :] = both[2 * BLK : 2 * BLK + 1, :]
             bn[p, 2 * toks : 3 * toks, :] = both[:BLK, :].astype(BF16)
 
         @pl.when((s > 0) & (s <= g_chunks))
@@ -672,15 +712,16 @@
             rg_copy(p).start()
             bg[p, :, 2 * toks : 3 * toks] = both[:, :BLK].astype(BF16)
 
-        @pl.when((s >= 6) & (lax.rem(s, 2) == 0))
-        def _():
-            e = (s - 6) // 2
-            z_steps(2 + e, 1 + e, e - 1)
+        tick = -1
+        for turn, number in Z_TICKS:
+            tick = jnp.where(s == turn, number, tick)
+        z_tick(tick)
 
     bs_copy.start()
     vec_spread()
-    for numbers in ((7, 6, 4), (8, 7, 5), (8, 8, 6), (8, 8, 7)):
-        z_steps(*numbers)
+    @pl.loop(Z_TICKS[-1][1] + 1, 2 * Z_PARTS + 2 * Z_LAG)
+    def _(number):
+        z_tick(number)
 
     bs_copy.wait_recv()
     sums = vd[inner]
@@ -701,7 +742,7 @@
     def sent(ref, sem):
         pltpu.make_async_copy(ref, ref, sem).wait()
 
-    sent(side_n.at[:, :, pl.ds(0, 3 * toks)], sn_ss)
+    sent(side_n.at[pl.ds(0, 2 * BLK), pl.ds(0, 3 * toks)], sn_ss)
     sent(side_g.at[pl.ds(0, 3 * toks), :], sg_ss)
     sent(bn.at[:, pl.ds(0, 3 * toks), :], bn_ss)
     sent(bg.at[:, :, pl.ds(0, 3 * toks)], bg_ss)
@@ -794,7 +835,7 @@
         vmem(w_out.shape, BF16),
         vmem(w_up.shape, BF16),
         vmem(w_down.shape, BF16),
-        vmem((2, BLK, 4 * toks), BF16),
+        vmem((2 * BLK + 16, 4 * toks), BF16),
         vmem((4 * toks, 2 * BLK), BF16),
         vmem((n_chunks, BLK, BLK), BF16),
         vmem((g_chunks, BLK, BLK), BF16),
@@ -817,7 +858,8 @@
         vmem((2, half, width), BF16),
         vmem((2, half, width), BF16),
         vmem((n_own, 8, BLK), F32),
-        vmem((N_MP, n_own, 8, BLK), F32),
+        vmem((2 * n_own, BLK), F32),
+        vmem((N_MP, 2 * n_own, BLK), F32),
         vmem((n_own, 8, BLK), F32),
         vmem((GROUP, 8, BLK), F32),
         vmem((8, width), F32),
@@ -915,14 +957,14 @@
         f32(hidden, BLK),
         f32(BLK),
     )
-    slots = 6
+    slots = n_chunks + g_chunks
     return pl.pallas_call(
         functools.partial(write_kernel, 3 * heads_w // BLK, heads_w // BLK),
         out_shape=outs,
         in_specs=[local] * 6,
         out_specs=tuple(spec(kind) for kind in outs),
         scratch_shapes=[vmem((slots, BLK, BLK), F32), dma((slots,)), dma((2,))],
-        compiler_params=pltpu.CompilerParams(vmem_limit_bytes=4 * 2**20),
+        compiler_params=pltpu.CompilerParams(vmem_limit_bytes=12 * 2**20),
     )(*kept)
 
 

time: 101 us -> 93 us (0.921)
  Pallas kernels: 100 us -> 92.1 us
    pallas_call x1, Pallas kernels: 95.5 us -> 88 us  [layer(): pl.pallas_call(functools.partial(layer_kernel, n_chunks, g_chunks), out_s...]
where the time goes in v4:
time: 93 us; the launch traced here: 92.8 us
  Pallas kernels  92.1 us (99%)
    pallas_call x1, Pallas kernels, layer(): pl.pallas_call(functools.partial(layer_kernel, n_chunks, g_chunks), out_s...  88 us
    pallas_call x1, Pallas kernels, layer(): pl.pallas_call(functools.partial(write_kernel, 3 * heads_w // BLK, heads_...  4.14 us

profile of v4, /device:TPU:0, one launch (start us, length us, event | category | flops | bytes accessed | tf_op | source)
XLA Modules:
  0.0 92.8 jit_solution(8521061243825545059)
XLA Ops:
  0.7 88.0 %shard_map.271 = (bf16[14,1024,256]{2,1,0:T(8,128)(2,1)S(1)}, bf16[10,256,1024]{2,1,0:T(8,128)(2,1)S(1)}, bf16[14,256,256]{2,1,0:T(8,128)(2,1)S(1)}, bf16[10,256...) custom-call(s32[1,4]{1,0:T(1,128)} %lens.1, bf16[256,2048]{1,0:T(8,128)(2,1)} %tok_h.1, ...), custom_call_target="tpu_custom_call" | custom-call | tf_op jit(solution)/shard_map/pallas_call | solution.py:904
  88.6 4.1 %shard_map.272 = (bf16[256,2048]{1,0:T(8,128)(2,1)}, bf16[256,2048]{1,0:T(8,128)(2,1)}, f32[256]{0:T(256)}, f32[256]{0:T(256)}, f32[256,512]{1,0:T(8,128)}, /*in...) custom-call(bf16[14,1024,256]{2,1,0:T(8,128)(2,1)S(1)} %get-tuple-el, ...), custom_call_target="tpu_custom_call" | custom-call | tf_op jit(solution)/shard_map/pallas_call | solution.py:961

commit v5 on v4

v5 whole, which is shorter than its diff:
```python
import functools
import math

import jax
import jax.numpy as jnp
from jax import lax
from jax.experimental import pallas as pl
from jax.experimental.pallas import tpu as pltpu
from jax.sharding import PartitionSpec as P

HD = 64
ROT = 32
EPSILON = 1e-05
GROUP = 8
CORE, XBIT, YBIT = 1, 2, 4
BLK = 256
WIDE = 512
N_MP = 4
Z_PARTS = 8
Z_LAG = 2
Z_TICKS = ((1, 2), (4, 3), (7, 4), (8, 5), (9, 6), (10, 7), (11, 8), (12, 9), (13, 10))
F32 = jnp.float32
BF16 = jnp.bfloat16
MESH = pl.DeviceIdType.MESH
MAIN_VMEM = 93 * 2**19
GELU_A = math.sqrt(2.0 / math.pi)
GELU_B = 0.044715


def nn(left, right):
    return lax.dot_general(left, right, (((1,), (0,)), ((), ())), preferred_element_type=F32)


def nt(left, right):
    return lax.dot_general(left, right, (((1,), (1,)), ((), ())), preferred_element_type=F32)


def tn(left, right):
    return lax.dot_general(left, right, (((0,), (0,)), ((), ())), preferred_element_type=F32)


def flip(index, mask):
    for bit in (1, 2, 4):
        if mask & bit:
            index = index + bit * (1 - 2 * ((index // bit) % 2))
    return index


def mult(value, by):
    return pl.multiple_of(value, by)


N_JS = (0, XBIT, CORE, XBIT | CORE)
N_MS = (0, YBIT)
G_JS = (0, YBIT, CORE, YBIT | CORE)
G_MS = (0, XBIT)


def layer_kernel(
    n_chunks,
    g_chunks,
    lens_h,
    tok_h,
    cot_h,
    gain_h,
    shift_h,
    bq_h,
    bk_h,
    bv_h,
    bup_h,
    obias_h,
    wq_h,
    wk_h,
    wv_h,
    wo_h,
    wu_h,
    wd_h,
    bn,
    bg,
    rsn_r,
    rsg_r,
    zout,
    vec_o,
    lens,
    gain,
    shift,
    bq,
    bk,
    bv,
    bup,
    obias,
    tok,
    gout,
    normed,
    turned_n,
    wq,
    wk,
    wv,
    wo,
    wu,
    wd,
    side_n,
    side_g,
    rsn_s,
    rsg_s,
    act,
    dact,
    gqkv,
    att,
    q_s,
    k_s,
    v_s,
    ga_s,
    amask,
    rot_c,
    rot_a,
    rot_b,
    stat_m,
    stat_i,
    zpart,
    zfar,
    znear,
    zmid,
    vzl,
    vz,
    vzr,
    vdr,
    gsum,
    bsum,
    bsum_r,
    cot_rows,
    in_sem,
    sn_ss,
    sg_ss,
    side_rs,
    bn_ss,
    bg_ss,
    blk_rs,
    rn_ss,
    rn_rs,
    rg_ss,
    rg_rs,
    zf_ss,
    zf_rs,
    zn_ss,
    zm_ss,
    zm_rs,
    zo_ss,
    zo_rs,
    zw_ss,
    ze_rs,
    vz_ss,
    vz_rs,
    vd_ss,
    vd_rs,
    bs_ss,
    bs_rs,
):
    toks, width = tok.shape
    hidden = wu.shape[1]
    heads_w = wq.shape[1]
    n_att = heads_w // BLK
    n_hid = hidden // BLK
    n_own = width // BLK
    dp = lax.axis_index("dp")
    zed = lax.axis_index("mp")
    inner = lax.rem(dp, GROUP)
    outer = dp - inner
    half = toks // 2
    piece_cols = width // Z_PARTS
    piece_rows = half // Z_PARTS

    def peer(mask):
        return (outer + flip(inner, mask), zed)

    def came(ref, sem):
        pltpu.make_async_copy(ref, ref, sem).wait()

    middle = (zed == 1) | (zed == 2)
    end_of_line = (zed == 0) | (zed == 3)
    side_of_line = zed // 2
    beside = (dp, zed + 1 - 2 * lax.rem(zed, 2))
    across = (dp, 3 - zed)
    near_rows = mult(side_of_line * half, half)
    far_rows = mult((1 - side_of_line) * half, half)

    def zpeer(step):
        return (dp, lax.rem(zed + step, N_MP))

    def remote(src, dst, ssem, rsem, where):
        return pltpu.make_async_remote_copy(
            src_ref=src,
            dst_ref=dst,
            send_sem=ssem,
            recv_sem=rsem,
            device_id=where,
            device_id_type=MESH,
        )

    def load(src, dst, number):
        copy = pltpu.make_async_copy(src, dst, in_sem.at[number])
        copy.start()
        return copy

    tok_load = load(tok_h, tok, 0)
    gain_load = load(gain_h, gain, 1)
    shift_load = load(shift_h, shift, 2)
    lens_load = load(lens_h, lens, 3)

    barrier = pltpu.get_barrier_semaphore()
    for mask in range(1, GROUP):
        pl.semaphore_signal(barrier, inc=1, device_id=peer(mask), device_id_type=MESH)
    for step in range(1, N_MP):
        pl.semaphore_signal(barrier, inc=1, device_id=zpeer(step), device_id_type=MESH)

    gout_load = load(cot_h, gout, 4)
    bias_loads = [
        load(src, dst, 5 + i)
        for i, (src, dst) in enumerate(
            ((bup_h, bup), (bq_h, bq), (bk_h, bk), (bv_h, bv), (obias_h, obias))
        )
    ]
    wu_load = load(wu_h, wu, 10)
    wd_load = load(wd_h, wd, 11)
    for src, dst in ((wq_h, wq), (wk_h, wk), (wv_h, wv), (wo_h, wo)):
        load(src, dst, 12)
    attn_load = pltpu.make_async_copy(wu_h, wu, in_sem.at[12])
    cot_load = load(cot_h.at[pl.ds(near_rows, half), :], cot_rows, 13)

    def segment_of(place):
        number = jnp.zeros_like(place)
        start_of = jnp.zeros_like(place)
        for j, end in enumerate(ends):
            start = end - lens[0, j]
            inside = ((place >= start) & (place < end)).astype(jnp.int32)
            number = number + inside * (j + 1)
            start_of = start_of + inside * start
        return number, start_of

    parity = lax.rem(zed, 2)

    def cross_core(index, times):
        return index + times * (1 - 2 * lax.rem(index, 2))

    def side_copy(to_side, ssem, chip_bit, other_bit, source, kind, m):
        owner_bit = m * other_bit
        if kind == 0:
            target = flip(cross_core(inner, parity), chip_bit)
            where = (outer + target, zed)
            slot_at = 1 + 2 * parity
        elif kind == 1:
            target = flip(inner, CORE)
            where = (outer + target, zed)
            slot_at = 2
        else:
            slot_at = 1 + 2 * parity
            where = beside
        place = to_side(m, mult(slot_at * toks, toks))
        src = place if kind == 2 else source(flip(target, owner_bit))
        return remote(src, place, ssem, side_rs.at[m if kind == 0 else 2], where)

    def side_g_copy(kind, m):
        def source(owner):
            return cot_h.at[:, pl.ds(mult(owner * BLK, BLK), BLK)]

        def to_side(m, at):
            return side_g.at[pl.ds(at, toks), pl.ds(m * BLK, BLK)]

        return side_copy(to_side, sg_ss, YBIT, XBIT, source, kind, m)

    def side_n_copy(kind, m):
        def source(owner):
            return turned_n.at[owner]

        def to_side(m, at):
            return side_n.at[pl.ds(m * BLK, BLK), pl.ds(at, toks)]

        return side_copy(to_side, sn_ss, XBIT, YBIT, source, kind, m)

    for copy in (tok_load, gain_load, shift_load):
        copy.wait()
    step_rows = 32

    @pl.loop(0, toks // step_rows, unroll=2)
    def _(r):
        rows = pl.ds(mult(r * step_rows, step_rows), step_rows)
        value = tok[rows, :].astype(F32)
        mean = jnp.sum(value, axis=1, keepdims=True) * (1.0 / width)
        center = value - mean
        spread = jnp.sum(center * center, axis=1, keepdims=True) * (1.0 / width)
        inv = lax.rsqrt(spread + EPSILON)
        normed[rows, :] = (center * inv * gain[...] + shift[...]).astype(BF16)
        stat_m[rows, :] = jnp.broadcast_to(mean, (step_rows, 128))
        stat_i[rows, :] = jnp.broadcast_to(inv, (step_rows, 128))

    pl.semaphore_wait(barrier, GROUP - 1 + N_MP - 1)
    for m in (0, 1):
        side_g_copy(0, m).start()
    first_at = flip(cross_core(inner, parity), XBIT)
    for m in (0, 1):
        owner = flip(first_at, N_MS[m])
        turned_n[owner] = normed[:, pl.ds(mult(owner * BLK, BLK), BLK)].T
        side_n_copy(0, m).start()

    @pl.loop(0, n_own)
    def _(o):
        @pl.when((o != first_at) & (o != flip(first_at, YBIT)))
        def _():
            turned_n[o] = normed[:, pl.ds(mult(o * BLK, BLK), BLK)].T

    for m in (0, 1):
        side_g_copy(1, m).start()
        side_n_copy(1, m).start()
    for copy in (lens_load, gout_load, *bias_loads):
        copy.wait()

    ends = []
    total_len = 0
    for j in range(lens.shape[1]):
        total_len = total_len + lens[0, j]
        ends.append(total_len)

    gsum[...] = jnp.zeros_like(gsum)

    @pl.loop(0, toks // step_rows)
    def _(r):
        first = r * step_rows
        rows = pl.ds(mult(first, step_rows), step_rows)
        place = first + lax.broadcasted_iota(jnp.int32, (step_rows, width), 0)
        value = jnp.where(place < total_len, gout[rows, :].astype(F32), 0.0)
        gout[rows, :] = value.astype(BF16)
        gsum[0:1, :] = gsum[0:1, :] + jnp.sum(value, axis=0, keepdims=True)

    for m in (0, 1):
        owner_g = mult(flip(inner, G_MS[m]) * BLK, BLK)
        side_g[0:toks, m * BLK : m * BLK + BLK] = gout[:, pl.ds(owner_g, BLK)]
        side_n[m * BLK : m * BLK + BLK, 0:toks] = turned_n[flip(inner, N_MS[m])]

    def bn_copy(s, k):
        src = bn.at[s, pl.ds(toks if k == 2 else 0, toks), :]
        slot_at = (1, 2, 3)[k]
        return remote(
            src,
            bn.at[s, pl.ds(slot_at * toks, toks), :],
            bn_ss,
            blk_rs.at[s, min(k, 1)],
            peer((XBIT, CORE, CORE)[k]),
        )

    def bg_copy(s, k):
        src = bg.at[s, :, pl.ds(toks if k == 2 else 0, toks)]
        slot_at = (1, 2, 3)[k]
        return remote(
            src,
            bg.at[s, :, pl.ds(slot_at * toks, toks)],
            bg_ss,
            blk_rs.at[s, min(k, 1)],
            peer((YBIT, CORE, CORE)[k]),
        )

    def piece(t, g, first_row):
        if t == 0:
            return pl.ds(first_row, half), pl.ds(mult(g * piece_cols, piece_cols), piece_cols)
        return pl.ds(mult(first_row + g * piece_rows, piece_rows), piece_rows), pl.ds(0, width)

    def z_far(t, g):
        rows, cols = piece(t, g, far_rows)
        to_rows, _ = piece(t, g, 0)
        return remote(
            zpart.at[t, rows, cols],
            zfar.at[t, to_rows, cols],
            zf_ss,
            zf_rs.at[t * Z_PARTS + g],
            beside,
        )

    def z_near(t, g):
        rows, cols = piece(t, g, near_rows)
        to_rows, _ = piece(t, g, 0)
        return remote(
            zpart.at[t, rows, cols],
            znear.at[t, to_rows, cols],
            zn_ss,
            zm_rs.at[t * Z_PARTS + g],
            beside,
        )

    def z_mid(t, g):
        rows, cols = piece(t, g, far_rows)
        to_rows, _ = piece(t, g, 0)
        return remote(
            zpart.at[t, rows, cols],
            zmid.at[t, to_rows, cols],
            zm_ss,
            zm_rs.at[t * Z_PARTS + g],
            across,
        )

    def z_done(t, g, to_end):
        rows, cols = piece(t, g, near_rows)
        place = zout.at[t, rows, cols]
        if to_end:
            return remote(place, place, zo_ss, ze_rs, beside)
        return remote(place, place, zo_ss, zo_rs.at[t * Z_PARTS + g], across)

    def z_pass(t, g):
        rows, cols = piece(t, g, far_rows)
        return remote(zout.at[t, rows, cols], zout.at[t, rows, cols], zw_ss, ze_rs, beside)

    def z_send(copies):
        @pl.when(end_of_line)
        def _():
            for copy in copies:
                copy.start()

    def z_first(t, g):
        z_far(t, g).wait_recv()
        rows, cols = piece(t, g, far_rows)
        there, _ = piece(t, g, 0)
        zpart[t, rows, cols] = (
            zpart[t, rows, cols].astype(F32) + zfar[t, there, cols].astype(F32)
        ).astype(BF16)
        z_mid(t, g).start()

    def z_second(t, g):
        came(znear.at[0, :, pl.ds(0, 2 * piece_cols)], zm_rs.at[t * Z_PARTS + g])
        rows, cols = piece(t, g, near_rows)
        there, _ = piece(t, g, 0)
        total = (
            zpart[t, rows, cols].astype(F32)
            + znear[t, there, cols].astype(F32)
            + zmid[t, there, cols].astype(F32)
        )
        base = tok[rows, cols].astype(F32)
        if t == 0:
            place = near_rows + lax.broadcasted_iota(jnp.int32, total.shape, 0)
            branch = jnp.where(place < total_len, total + obias[:, cols], 0.0)
            zout[t, rows, cols] = (base + branch).astype(BF16)
        else:
            @pl.when(g == 0)
            def _():
                cot_load.wait()

            inv = stat_i[rows, 0:1]
            standard = (base - stat_m[rows, 0:1]) * inv
            grad = total * gain[...]
            mean_g = jnp.sum(grad, axis=1, keepdims=True) * (1.0 / width)
            mean_x = jnp.sum(grad * standard, axis=1, keepdims=True) * (1.0 / width)
            back = inv * (grad - mean_g - standard * mean_x)
            zout[t, rows, cols] = (cot_rows[there, :].astype(F32) + back).astype(BF16)
        z_done(t, g, False).start()
        z_done(t, g, True).start()

    def z_third(t, g):
        z_done(t, g, False).wait_recv()
        z_pass(t, g).start()

    def z_tick(number, kinds=(0, 1)):
        for step, lag in ((z_first, 0), (z_second, Z_LAG), (z_third, 2 * Z_LAG)):
            at = number - lag
            for t in kinds:
                low = t * Z_PARTS
                if isinstance(number, int):
                    if low <= at < low + Z_PARTS:
                        pl.when(middle)(functools.partial(step, t, at - low))
                else:
                    inside = (at >= low) & (at < low + Z_PARTS)
                    pl.when(middle & inside)(functools.partial(step, t, at - low))

    per_wide = WIDE // BLK

    wu_load.wait()

    @pl.loop(0, hidden // (2 * WIDE))
    def _(w):
        blocks = [pl.ds(mult((2 * w + side) * WIDE, WIDE), WIDE) for side in (0, 1)]
        ups = [nn(normed[...], wu[:, cols]) + bup[:, cols] for cols in blocks]
        for side, (up, cols) in enumerate(zip(ups, blocks)):
            square = up * up
            tanh = jnp.tanh(GELU_A * up * (1.0 + GELU_B * square))
            row = lax.broadcasted_iota(jnp.int32, up.shape, 0)
            active = jnp.where(row < total_len, 0.5 * up * (1.0 + tanh), 0.0).astype(BF16)
            act[:, cols] = active
            dact[:, cols] = (
                0.5 * (1.0 + tanh)
                + 0.5 * up * (1.0 - tanh * tanh) * (GELU_A * (1.0 + 3.0 * GELU_B * square))
            ).astype(BF16)
            for part in range(per_wide):
                c = (2 * w + side) * per_wide + part
                bg[c, :, 0:toks] = active[:, part * BLK : part * BLK + BLK].T
        for part in range(2 * per_wide):
            for k in (0, 1):
                bg_copy(2 * w * per_wide + part, k).start()

    def side_pass(m):
        came(bn.at[0, pl.ds(0, 2 * toks), :], side_rs.at[m])
        for copy_of in (side_g_copy, side_n_copy):
            copy_of(2, m).start()

    side_pass(0)

    def hidden_grad(first, past, shift):
        @pl.loop(first, past)
        def _(w):
            cols = pl.ds(mult(w * WIDE, WIDE), WIDE)
            grad = (nt(gout[...], wd[cols, :]) * dact[:, cols].astype(F32)).astype(BF16)
            dact[:, cols] = grad
            for part in range(per_wide):
                c = shift + w * per_wide + part
                bn[c, 0:toks, :] = grad[:, part * BLK : part * BLK + BLK]
                for k in (0, 1):
                    bn_copy(c, k).start()

    n_wide = hidden // WIDE
    wd_load.wait()
    hidden_grad(0, n_wide // 2, 0)
    side_pass(1)

    place_r = lax.broadcasted_iota(jnp.int32, (toks, toks), 0)
    place_c = lax.broadcasted_iota(jnp.int32, (toks, toks), 1)
    seg_r, _ = segment_of(place_r)
    seg_c, _ = segment_of(place_c)
    allowed = (seg_r == seg_c) & (place_c <= place_r)
    for h in (0, 1):
        amask[h * toks : h * toks + toks, :] = jnp.where(allowed, 0.0, -1e30)

    lane = lax.broadcasted_iota(jnp.int32, (toks, 128), 1)
    slot = lax.broadcasted_iota(jnp.int32, (toks, 128), 0)
    _, start_of = segment_of(slot)
    in_head = lane % HD
    order = (in_head % (ROT // 2)).astype(F32)
    freq = jnp.exp(order * (-2.0 / ROT * math.log(10000.0)))
    angle = (slot - start_of).astype(F32) * freq
    cosine, sine = jnp.cos(angle), jnp.sin(angle)
    rot_c[...] = jnp.where(in_head < ROT, cosine, 1.0)
    rot_a[...] = jnp.where(in_head < ROT // 2, -sine, 0.0)
    rot_b[...] = jnp.where((in_head >= ROT // 2) & (in_head < ROT), sine, 0.0)

    def rotate(value, sign):
        left = pltpu.roll(value, 128 - ROT // 2, 1)
        right = pltpu.roll(value, ROT // 2, 1)
        return value * rot_c[...] + sign * (left * rot_a[...] + right * rot_b[...])

    attn_load.wait()

    @pl.loop(0, heads_w // BLK)
    def _(n):
        cols = pl.ds(mult(n * BLK, BLK), BLK)
        query = nn(normed[...], wq[:, cols]) + bq[:, cols]
        keys = nn(normed[...], wk[:, cols]) + bk[:, cols]
        for part in range(BLK // 128):
            at = pl.ds(mult(n * BLK + part * 128, 128), 128)
            lanes = slice(part * 128, part * 128 + 128)
            q_s[:, at] = (rotate(query[:, lanes], 1.0) * 0.125).astype(BF16)
            k_s[:, at] = rotate(keys[:, lanes], 1.0).astype(BF16)
        v_s[:, cols] = (nn(normed[...], wv[:, cols]) + bv[:, cols]).astype(BF16)
        ga_s[:, cols] = nt(gout[...], wo[cols, :]).astype(BF16)

    low_lane = lax.broadcasted_iota(jnp.int32, (1, 128), 1) < HD
    first_head = jnp.where(low_lane, 1.0, 0.0).astype(BF16)
    second_head = jnp.where(low_lane, 0.0, 1.0).astype(BF16)
    low_full = lax.broadcasted_iota(jnp.int32, (toks, 128), 1) < HD

    def apart(value):
        return jnp.concatenate([value * first_head, value * second_head], axis=0)

    def together(value):
        return jnp.where(low_full, value[:toks], value[toks:])

    @pl.loop(0, n_att)
    def _(n):
        base_n = n_hid // 2 + 3 * n
        for part in range(BLK // 128):
            at = pl.ds(mult(n * BLK + part * 128, 128), 128)
            lanes = slice(part * 128, part * 128 + 128)
            kp, vp = k_s[:, at], v_s[:, at]
            q2, g2 = apart(q_s[:, at]), apart(ga_s[:, at])
            scores = nt(q2, kp) + amask[...]
            top = jnp.max(scores, axis=1, keepdims=True)
            expo = jnp.exp(scores - top)
            probs = expo * (1.0 / jnp.sum(expo, axis=1, keepdims=True))
            probs_low = probs.astype(BF16)
            prob_grad = nt(g2, vp)
            delta = jnp.sum(probs * prob_grad, axis=1, keepdims=True)
            score_grad = (probs * (prob_grad - delta)).astype(BF16)
            out = jnp.where(slot < total_len, together(nn(probs_low, vp)), 0.0).astype(BF16)
            att[:, at] = out
            bg[n_hid + n, lanes, 0:toks] = out.T
            dq = rotate(together(nn(score_grad, kp)) * 0.125, -1.0).astype(BF16)
            dk = rotate(tn(score_grad, q2), -1.0).astype(BF16)
            dv = tn(probs_low, g2).astype(BF16)
            for kind, value in enumerate((dq, dk, dv)):
                bn[base_n + kind, 0:toks, lanes] = value
                gqkv[:, pl.ds(mult(kind * heads_w + n * BLK + part * 128, 128), 128)] = value
        for k in (0, 1):
            bg_copy(n_hid + n, k).start()
            for kind in range(3):
                bn_copy(base_n + kind, k).start()

    @pl.loop(0, width // WIDE)
    def _(n):
        cols = pl.ds(mult(n * WIDE, WIDE), WIDE)
        zpart[0, :, cols] = (nn(act[...], wd[:, cols]) + nn(att[...], wo[:, cols])).astype(BF16)
        for part in range(WIDE // piece_cols):
            g = n * (WIDE // piece_cols) + part
            z_send([z_far(0, g), z_near(0, g)])

    hidden_grad(n_wide // 2, n_wide, 3 * n_att)

    vzl[...] = jnp.zeros_like(vzl)

    @pl.loop(0, width // WIDE)
    def _(n):
        cols = pl.ds(mult(n * WIDE, WIDE), WIDE)
        grad = nt(dact[...], wu[cols, :])
        for kind, weight in enumerate((wq, wk, wv)):
            grad = grad + nt(gqkv[:, kind * heads_w : (kind + 1) * heads_w], weight[cols, :])
        zpart[1, :, cols] = grad.astype(BF16)

        for turn, number in ((1, 0), (3, 1)):
            @pl.when(n == turn)
            def _(number=number):
                z_tick(number)

        for part in range(WIDE // 128):
            lanes = slice(part * 128, part * 128 + 128)
            at = pl.ds(mult(n * WIDE + part * 128, 128), 128)
            owner = n * per_wide + part * 128 // BLK
            into = slice(part * 128 % BLK, part * 128 % BLK + 128)
            piece_of = grad[:, lanes]
            standard = (tok[:, at].astype(F32) - stat_m[...]) * stat_i[...]
            vzl[owner, 0:1, into] = jnp.sum(piece_of * standard, axis=0, keepdims=True)
            vzl[owner, 1:2, into] = jnp.sum(piece_of, axis=0, keepdims=True)

    def vd_copy(mask):
        return remote(
            vzl.at[flip(inner, mask)], vdr.at[mask - 1], vd_ss, vd_rs, peer(mask)
        )

    for owner in range(n_own):
        vzl[owner, 2:3, :] = gsum[0:1, owner * BLK : owner * BLK + BLK]
    for mask in range(1, GROUP):
        vd_copy(mask).start()
    for g in range(Z_PARTS):
        z_send([z_far(1, g), z_near(1, g)])

    bs_copy = remote(bsum, bsum_r, bs_ss, bs_rs, peer(YBIT))

    def rn_copy(s):
        return remote(rsn_s.at[s], rsn_r.at[s], rn_ss, rn_rs, peer(YBIT))

    def rg_copy(s):
        return remote(rsg_s.at[s], rsg_r.at[s], rg_ss, rg_rs, peer(XBIT))

    came(bn.at[pl.ds(0, 2), :, :], side_rs.at[2])
    bsum[...] = jnp.zeros_like(bsum)

    def vz_copy(step):
        return remote(vz, vzr.at[step - 1], vz_ss, vz_rs, zpeer(step))

    def vec_spread():
        came(vdr, vd_rs)
        vz[...] = vzl[inner] + jnp.sum(vdr[...], axis=0)
        for step in range(1, N_MP):
            vz_copy(step).start()

    side_n[2 * BLK :, :] = jnp.ones((16, 4 * toks), BF16)

    @pl.loop(0, n_chunks + 1)
    def _(s):
        @pl.when(s < g_chunks)
        def _():
            came(bn.at[s, pl.ds(0, 2 * toks), :], blk_rs.at[s, 0])
            bn_copy(s, 2).start()
            bg_copy(s, 2).start()

        @pl.when((s >= g_chunks) & (s < n_chunks))
        def _():
            came(bn.at[s, pl.ds(0, toks), :], blk_rs.at[s, 0])
            bn_copy(s, 2).start()

        @pl.when((s > 0) & (s <= g_chunks))
        def _():
            came(bn.at[s - 1], blk_rs.at[s - 1, 1])

        @pl.when(s > g_chunks)
        def _():
            came(bn.at[s - 1, pl.ds(0, 2 * toks), :], blk_rs.at[s - 1, 1])

        @pl.when(s > 0)
        def _():
            p = s - 1
            both = nn(side_n[...], bn[p])
            rsn_s[p] = both[BLK : 2 * BLK, :].astype(BF16)
            rn_copy(p).start()
            bsum[pl.ds(p, 1), :] = both[2 * BLK : 2 * BLK + 1, :]
            bn[p, 2 * toks : 3 * toks, :] = both[:BLK, :].astype(BF16)

        @pl.when((s > 0) & (s <= g_chunks))
        def _():
            p = s - 1
            both = nn(bg[p], side_g[...])
            rsg_s[p] = both[:, BLK:].astype(BF16)
            rg_copy(p).start()
            bg[p, :, 2 * toks : 3 * toks] = both[:, :BLK].astype(BF16)

        tick = -1
        for turn, number in Z_TICKS:
            tick = jnp.where(s == turn, number, tick)
        z_tick(tick)

    bs_copy.start()
    vec_spread()
    @pl.loop(Z_TICKS[-1][1] + 1, 2 * Z_PARTS + 2 * Z_LAG)
    def _(number):
        z_tick(number)

    bs_copy.wait_recv()
    came(vzr, vz_rs)
    vec_o[0:8, :] = vz[...] + jnp.sum(vzr[...], axis=0)
    vec_o[2:3, :] = vz[2:3, :]
    vec_o[8:, :] = bsum[...] + bsum_r[...]

    came(rsn_r, rn_rs)
    came(rsg_r, rg_rs)

    came(side_n.at[pl.ds(0, 2 * BLK), pl.ds(0, 3 * toks)], sn_ss)
    came(side_g.at[pl.ds(0, 3 * toks), :], sg_ss)
    came(bn.at[:, pl.ds(0, 3 * toks), :], bn_ss)
    came(bg.at[:, :, pl.ds(0, 3 * toks)], bg_ss)
    came(rsn_s, rn_ss)
    came(rsg_s, rg_ss)
    came(vzr, vz_ss)
    came(vdr, vd_ss)
    bs_copy.wait_send()

    @pl.when(end_of_line)
    def _():
        came(zfar, zf_ss)
        came(znear, zn_ss)
        came(zout, ze_rs)
        cot_load.wait()

    @pl.when(middle)
    def _():
        came(zmid, zm_ss)
        came(zout, zo_ss)
        came(zmid, zw_ss)


def write_kernel(n_hid, n_att, bn, bg, rsn, rsg, zout, vec, mixed_h, gtok_h, gain_o, shift_o, gq_h, bq_o, gk_h, bk_o, gv_h, bv_o, go_h, gu_h, bu_o, gd_h, ob_o, stage, sem, zsem):
    n_chunks, n_g = bn.shape[0], bg.shape[0]
    toks = zout.shape[1]
    z_outs = [
        pltpu.make_async_copy(zout.at[t], out, zsem) for t, out in enumerate((mixed_h, gtok_h))
    ]
    for out in z_outs:
        out.start()
    places, biases = [], []
    for s in range(n_chunks):
        inside = s - n_hid // 2
        if 0 <= inside < 3 * n_att:
            (out, bias), at = ((gq_h, bq_o), (gk_h, bk_o), (gv_h, bv_o))[inside % 3], inside // 3
        else:
            (out, bias), at = (gu_h, bu_o), s if inside < 0 else s - 3 * n_att
        biases.append((bias, at))
        places.append((True, s, out.at[:, pl.ds(at * BLK, BLK)]))
    for s in range(n_g):
        out, at = (gd_h, s) if s < n_hid else (go_h, s - n_hid)
        places.append((False, s, out.at[pl.ds(at * BLK, BLK), :]))
    copies = []
    for number, (first, s, place) in enumerate(places):
        slot = number
        if first:
            value = bn[s, 2 * toks : 3 * toks, :].astype(F32) + rsn[s].astype(F32)
        else:
            value = bg[s, :, 2 * toks : 3 * toks].astype(F32) + rsg[s].astype(F32)
        stage[slot] = value
        copies.append(pltpu.make_async_copy(stage.at[slot], place, sem))
        copies[number].start()
    for row, out in enumerate((gain_o, shift_o, ob_o)):
        out[...] = vec[row]
    for s, (out, at) in enumerate(biases):
        out[at * BLK : at * BLK + BLK] = vec[8 + s]
    pltpu.make_async_copy(stage, stage, sem).wait()
    pltpu.make_async_copy(zout, zout, zsem).wait()


def layer(tokens, lengths, ln_gain, ln_bias, w_query, b_query, w_key, b_key, w_value, b_value, w_out, w_up, b_up, w_down, out_bias, cotangent):
    toks, width = tokens.shape
    heads_w = w_query.shape[1]
    hidden = w_up.shape[1]
    n_chunks = (3 * heads_w + hidden) // BLK
    g_chunks = (heads_w + hidden) // BLK
    n_own = width // BLK
    n_vec = -(-n_chunks // 8) * 8
    half = toks // 2
    dma = pltpu.SemaphoreType.DMA
    vmem = pltpu.VMEM
    scratch = [
        pltpu.SMEM(lengths.shape, jnp.int32),
        vmem((1, width), F32),
        vmem((1, width), F32),
        vmem((1, heads_w), F32),
        vmem((1, heads_w), F32),
        vmem((1, heads_w), F32),
        vmem((1, hidden), F32),
        vmem((1, width), F32),
        vmem((toks, width), BF16),
        vmem((toks, width), BF16),
        vmem((toks, width), BF16),
        vmem((n_own, BLK, toks), BF16),
        vmem(w_query.shape, BF16),
        vmem(w_key.shape, BF16),
        vmem(w_value.shape, BF16),
        vmem(w_out.shape, BF16),
        vmem(w_up.shape, BF16),
        vmem(w_down.shape, BF16),
        vmem((2 * BLK + 16, 4 * toks), BF16),
        vmem((4 * toks, 2 * BLK), BF16),
        vmem((n_chunks, BLK, BLK), BF16),
        vmem((g_chunks, BLK, BLK), BF16),
        vmem((toks, hidden), BF16),
        vmem((toks, hidden), BF16),
        vmem((toks, 3 * heads_w), BF16),
        vmem((toks, heads_w), BF16),
        vmem((toks, heads_w), BF16),
        vmem((toks, heads_w), BF16),
        vmem((toks, heads_w), BF16),
        vmem((toks, heads_w), BF16),
        vmem((2 * toks, toks), F32),
        vmem((toks, 128), F32),
        vmem((toks, 128), F32),
        vmem((toks, 128), F32),
        vmem((toks, 128), F32),
        vmem((toks, 128), F32),
        vmem((2, toks, width), BF16),
        vmem((2, half, width), BF16),
        vmem((2, half, width), BF16),
        vmem((2, half, width), BF16),
        vmem((n_own, 8, BLK), F32),
        vmem((8, BLK), F32),
        vmem((N_MP - 1, 8, BLK), F32),
        vmem((GROUP - 1, 8, BLK), F32),
        vmem((8, width), F32),
        vmem((n_vec, BLK), F32),
        vmem((n_vec, BLK), F32),
        vmem((half, width), BF16),
        dma((14,)),
        dma,
        dma,
        dma((3,)),
        dma,
        dma,
        dma((n_chunks, 2)),
        dma,
        dma,
        dma,
        dma,
        dma,
        dma((2 * Z_PARTS,)),
        dma,
        dma,
        dma((2 * Z_PARTS,)),
        dma,
        dma((2 * Z_PARTS,)),
        dma,
        dma,
        dma,
        dma,
        dma,
        dma,
        dma,
        dma,
    ]
    anyspace = pl.BlockSpec(memory_space=pl.ANY)
    local = pl.BlockSpec(memory_space=pltpu.VMEM)
    row = lambda value: value.reshape(1, -1)
    kept = pl.pallas_call(
        functools.partial(layer_kernel, n_chunks, g_chunks),
        out_shape=(
            vmem((n_chunks, 4 * toks, BLK), BF16),
            vmem((g_chunks, BLK, 4 * toks), BF16),
            vmem((n_chunks, BLK, BLK), BF16),
            vmem((g_chunks, BLK, BLK), BF16),
            vmem((2, toks, width), BF16),
            vmem((8 + n_vec, BLK), F32),
        ),
        in_specs=[anyspace] * 16,
        out_specs=(local,) * 6,
        scratch_shapes=scratch,
        compiler_params=pltpu.CompilerParams(
            collective_id=0, has_side_effects=True, vmem_limit_bytes=MAIN_VMEM
        ),
    )(
        lengths,
        tokens,
        cotangent,
        row(ln_gain),
        row(ln_bias),
        row(b_query),
        row(b_key),
        row(b_value),
        row(b_up),
        row(out_bias),
        w_query,
        w_key,
        w_value,
        w_out,
        w_up,
        w_down,
    )
    f32 = lambda *shape: jax.ShapeDtypeStruct(shape, F32)
    low = jax.ShapeDtypeStruct((toks, width), BF16)
    spec = lambda kind: anyspace if len(kind.shape) == 2 else local
    outs = (
        low,
        low,
        f32(BLK),
        f32(BLK),
        f32(BLK, heads_w),
        f32(heads_w),
        f32(BLK, heads_w),
        f32(heads_w),
        f32(BLK, heads_w),
        f32(heads_w),
        f32(heads_w, BLK),
        f32(BLK, hidden),
        f32(hidden),
        f32(hidden, BLK),
        f32(BLK),
    )
    slots = n_chunks + g_chunks
    return pl.pallas_call(
        functools.partial(write_kernel, hidden // BLK, heads_w // BLK),
        out_shape=outs,
        in_specs=[local] * 6,
        out_specs=tuple(spec(kind) for kind in outs),
        scratch_shapes=[vmem((slots, BLK, BLK), F32), dma, dma],
        compiler_params=pltpu.CompilerParams(vmem_limit_bytes=12 * 2**20),
    )(*kept)


def make_body(n_dp, n_mp):
    outer = n_dp // GROUP

    def order(value, axis):
        if outer == 1:
            return value
        shape = value.shape
        split = shape[:axis] + (outer, GROUP, shape[axis] // n_dp) + shape[axis + 1 :]
        return jnp.swapaxes(value.reshape(split), axis, axis + 1).reshape(shape)

    def restore(value, axis):
        if outer == 1:
            return value
        shape = value.shape
        split = shape[:axis] + (GROUP, outer, shape[axis] // n_dp) + shape[axis + 1 :]
        return jnp.swapaxes(value.reshape(split), axis, axis + 1).reshape(shape)

    groups = [[o * GROUP + i for o in range(outer)] for i in range(GROUP)]

    def scatter(value, axis):
        if outer == 1:
            return value
        return lax.psum_scatter(
            value, "dp", scatter_dimension=axis, axis_index_groups=groups, tiled=True
        )

    def total(value):
        if outer == 1:
            return value
        return lax.psum(value, "dp", axis_index_groups=groups)

    def body(tokens, lengths, ln_gain, ln_bias, w_query, b_query, w_key, b_key, w_value, b_value, w_out, w_up, b_up, w_down, out_bias, cotangent):
        found = layer(
            order(tokens, 1),
            lengths,
            order(ln_gain, 0),
            order(ln_bias, 0),
            order(w_query, 0),
            b_query,
            order(w_key, 0),
            b_key,
            order(w_value, 0),
            b_value,
            order(w_out, 1),
            order(w_up, 0),
            b_up,
            order(w_down, 1),
            order(out_bias, 0),
            order(cotangent, 1),
        )
        (mixed, grad_tokens, gain, shift, g_q, b_q, g_k, b_k, g_v, b_v, g_out, g_up, b_u, g_down, b_out) = found
        return (
            restore(mixed, 1),
            restore(grad_tokens, 1),
            scatter(gain, 0),
            scatter(shift, 0),
            scatter(g_q, 0),
            total(b_q),
            scatter(g_k, 0),
            total(b_k),
            scatter(g_v, 0),
            total(b_v),
            scatter(g_out, 1),
            scatter(g_up, 0),
            total(b_u),
            scatter(g_down, 1),
            scatter(b_out, 0),
        )

    return body


def solution(mesh):
    in_specs = (
        P("dp", None),
        P("dp", None),
        P(),
        P(),
        P(None, "mp"),
        P("mp"),
        P(None, "mp"),
        P("mp"),
        P(None, "mp"),
        P("mp"),
        P("mp", None),
        P(None, "mp"),
        P("mp"),
        P("mp", None),
        P(),
        P("dp", None),
    )
    out_specs = (
        P("dp", None),
        P("dp", None),
        P("dp"),
        P("dp"),
        P("dp", "mp"),
        P("mp"),
        P("dp", "mp"),
        P("mp"),
        P("dp", "mp"),
        P("mp"),
        P("mp", "dp"),
        P("dp", "mp"),
        P("mp"),
        P("mp", "dp"),
        P("dp"),
    )
    body = make_body(mesh.shape["dp"], mesh.shape["mp"])
    return jax.shard_map(body, mesh=mesh, in_specs=in_specs, out_specs=out_specs, check_vma=False)
```

time: 93 us -> 90.3 us (0.971)
  Pallas kernels: 92.1 us -> 89.5 us
    pallas_call x1, Pallas kernels: 88 us -> 85.6 us  [layer(): pl.pallas_call(functools.partial(layer_kernel, n_chunks, g_chunks), out_s...]
where the time goes in v5:
time: 90.3 us; the launch traced here: 90.2 us
  Pallas kernels  89.5 us (99%)
    pallas_call x1, Pallas kernels, layer(): pl.pallas_call(functools.partial(layer_kernel, n_chunks, g_chunks), out_s...  85.6 us
    pallas_call x1, Pallas kernels, layer(): pl.pallas_call(functools.partial(write_kernel, hidden // BLK, heads_w //...  3.92 us

profile of v5, /device:TPU:0, one launch (start us, length us, event | category | flops | bytes accessed | tf_op | source)
XLA Modules:
  0.0 90.2 jit_solution(2524830414360115240)
XLA Ops:
  0.7 85.6 %shard_map.271 = (bf16[14,1024,256]{2,1,0:T(8,128)(2,1)S(1)}, bf16[10,256,1024]{2,1,0:T(8,128)(2,1)S(1)}, bf16[14,256,256]{2,1,0:T(8,128)(2,1)S(1)}, bf16[10,256...) custom-call(s32[1,4]{1,0:T(1,128)} %lens_h.1, bf16[256,2048]{1,0:T(8,128)(2,1)} %tok_h.1, ...), custom_call_target="tpu_custom_call" | custom-call | tf_op jit(solution)/shard_map/pallas_call | solution.py:879
  86.3 3.9 %shard_map.272 = (bf16[256,2048]{1,0:T(8,128)(2,1)}, bf16[256,2048]{1,0:T(8,128)(2,1)}, f32[256]{0:T(256)}, f32[256]{0:T(256)}, f32[256,512]{1,0:T(8,128)}, /*in...) custom-call(bf16[14,1024,256]{2,1,0:T(8,128)(2,1)S(1)} %get-tuple-el, ...), custom_call_target="tpu_custom_call" | custom-call | tf_op jit(solution)/shard_map/pallas_call | solution.py:934

commit v6 on v5

--- a/solution.py
+++ b/solution.py
@@ -17,8 +17,9 @@
 WIDE = 512
 N_MP = 4
 Z_PARTS = 8
-Z_LAG = 2
-Z_TICKS = ((1, 2), (4, 3), (7, 4), (8, 5), (9, 6), (10, 7), (11, 8), (12, 9), (13, 10))
+Z_LEAD = 2
+Z_LAG = (0, 2, 4)
+Z_TICKS = ((1, 4), (4, 5), (6, 6), (9, 7), (10, 8), (11, 9), (12, 10), (13, 11))
 F32 = jnp.float32
 BF16 = jnp.bfloat16
 MESH = pl.DeviceIdType.MESH
@@ -104,7 +105,7 @@
     rsn_s,
     rsg_s,
     act,
-    dact,
+    gup,
     gqkv,
     att,
     q_s,
@@ -130,8 +131,8 @@
     bsum_r,
     cot_rows,
     in_sem,
-    sn_ss,
-    sg_ss,
+    wide_sem,
+    side_ss,
     side_rs,
     bn_ss,
     bg_ss,
@@ -220,8 +221,18 @@
             ((bup_h, bup), (bq_h, bq), (bk_h, bk), (bv_h, bv), (obias_h, obias))
         )
     ]
-    wu_load = load(wu_h, wu, 10)
-    wd_load = load(wd_h, wd, 11)
+    def wide_loads(w):
+        part = pl.ds(mult(w * WIDE, WIDE), WIDE)
+        return (
+            pltpu.make_async_copy(wu_h.at[:, part], wu.at[:, part], wide_sem.at[w, 0]),
+            pltpu.make_async_copy(wd_h.at[part, :], wd.at[part, :], wide_sem.at[w, 1]),
+        )
+
+    @pl.loop(0, hidden // WIDE)
+    def _(w):
+        for copy in wide_loads(w):
+            copy.start()
+
     for src, dst in ((wq_h, wq), (wk_h, wk), (wv_h, wv), (wo_h, wo)):
         load(src, dst, 12)
     attn_load = pltpu.make_async_copy(wu_h, wu, in_sem.at[12])
@@ -237,45 +248,71 @@
             start_of = start_of + inside * start
         return number, start_of
 
-    parity = lax.rem(zed, 2)
-
     def cross_core(index, times):
         return index + times * (1 - 2 * lax.rem(index, 2))
 
-    def side_copy(to_side, ssem, chip_bit, other_bit, source, kind, m):
-        owner_bit = m * other_bit
-        if kind == 0:
-            target = flip(cross_core(inner, parity), chip_bit)
-            where = (outer + target, zed)
-            slot_at = 1 + 2 * parity
-        elif kind == 1:
-            target = flip(inner, CORE)
-            where = (outer + target, zed)
-            slot_at = 2
+    def flip_by(index, bit, times):
+        return index + times * (bit * (1 - 2 * ((index // bit) % 2)))
+
+    own_part = lax.rem(zed, 2)
+    own_slot = 1 + 2 * side_of_line
+    other_slot = 3 - 2 * side_of_line
+
+    def side_places(slot_at, m):
+        at = pl.ds(mult(slot_at * toks, toks), toks)
+        rows = pl.ds(mult(m * BLK, BLK), BLK)
+        return side_n.at[rows, at], side_g.at[at, rows]
+
+    def side_direct():
+        at_n = flip(cross_core(inner, side_of_line), XBIT)
+        at_g = flip(cross_core(inner, side_of_line), YBIT)
+        owner_n = flip_by(at_n, YBIT, own_part)
+        owner_g = flip_by(at_g, XBIT, own_part)
+        place_n, place_g = side_places(own_slot, own_part)
+        source_g = cot_h.at[:, pl.ds(mult(owner_g * BLK, BLK), BLK)]
+        return (
+            remote(turned_n.at[owner_n], place_n, side_ss, side_rs.at[0], (outer + at_n, zed)),
+            remote(source_g, place_g, side_ss, side_rs.at[0], (outer + at_g, zed)),
+            owner_n,
+        )
+
+    def side_core(m):
+        place_n, place_g = side_places(2, m)
+        owner_n = flip(inner, CORE ^ N_MS[m])
+        owner_g = flip(inner, CORE ^ G_MS[m])
+        source_g = cot_h.at[:, pl.ds(mult(owner_g * BLK, BLK), BLK)]
+        return (
+            remote(turned_n.at[owner_n], place_n, side_ss, side_rs.at[4], peer(CORE)),
+            remote(source_g, place_g, side_ss, side_rs.at[4], peer(CORE)),
+        )
+
+    def side_send(slot_at, m, number, where):
+        for place in side_places(slot_at, m):
+            remote(place, place, side_ss, side_rs.at[number], where).start()
+
+    def side_came(number, blocks=2):
+        came(bn.at[0, pl.ds(0, blocks * toks), :], side_rs.at[number])
+
+    def side_pass(stage):
+        if stage == 0:
+            side_came(0)
+            side_send(own_slot, own_part, 1, beside)
+
+            @pl.when(middle)
+            def _():
+                side_send(own_slot, own_part, 2, across)
+        elif stage == 1:
+            @pl.when(middle)
+            def _():
+                side_came(1)
+                side_send(own_slot, 1 - own_part, 3, across)
+                side_came(2)
+                side_send(other_slot, 1 - own_part, 2, beside)
         else:
-            slot_at = 1 + 2 * parity
-            where = beside
-        place = to_side(m, mult(slot_at * toks, toks))
-        src = place if kind == 2 else source(flip(target, owner_bit))
-        return remote(src, place, ssem, side_rs.at[m if kind == 0 else 2], where)
-
-    def side_g_copy(kind, m):
-        def source(owner):
-            return cot_h.at[:, pl.ds(mult(owner * BLK, BLK), BLK)]
-
-        def to_side(m, at):
-            return side_g.at[pl.ds(at, toks), pl.ds(m * BLK, BLK)]
-
-        return side_copy(to_side, sg_ss, YBIT, XBIT, source, kind, m)
-
-    def side_n_copy(kind, m):
-        def source(owner):
-            return turned_n.at[owner]
-
-        def to_side(m, at):
-            return side_n.at[pl.ds(m * BLK, BLK), pl.ds(at, toks)]
-
-        return side_copy(to_side, sn_ss, XBIT, YBIT, source, kind, m)
+            @pl.when(middle)
+            def _():
+                side_came(3)
+                side_send(other_slot, own_part, 3, beside)
 
     for copy in (tok_load, gain_load, shift_load):
         copy.wait()
@@ -294,23 +331,11 @@
         stat_i[rows, :] = jnp.broadcast_to(inv, (step_rows, 128))
 
     pl.semaphore_wait(barrier, GROUP - 1 + N_MP - 1)
-    for m in (0, 1):
-        side_g_copy(0, m).start()
-    first_at = flip(cross_core(inner, parity), XBIT)
-    for m in (0, 1):
-        owner = flip(first_at, N_MS[m])
-        turned_n[owner] = normed[:, pl.ds(mult(owner * BLK, BLK), BLK)].T
-        side_n_copy(0, m).start()
-
-    @pl.loop(0, n_own)
-    def _(o):
-        @pl.when((o != first_at) & (o != flip(first_at, YBIT)))
-        def _():
-            turned_n[o] = normed[:, pl.ds(mult(o * BLK, BLK), BLK)].T
-
-    for m in (0, 1):
-        side_g_copy(1, m).start()
-        side_n_copy(1, m).start()
+    direct_n, direct_g, first_owner = side_direct()
+    direct_g.start()
+    turned_n[first_owner] = normed[:, pl.ds(mult(first_owner * BLK, BLK), BLK)].T
+    direct_n.start()
+
     for copy in (lens_load, gout_load, *bias_loads):
         copy.wait()
 
@@ -330,11 +355,6 @@
         value = jnp.where(place < total_len, gout[rows, :].astype(F32), 0.0)
         gout[rows, :] = value.astype(BF16)
         gsum[0:1, :] = gsum[0:1, :] + jnp.sum(value, axis=0, keepdims=True)
-
-    for m in (0, 1):
-        owner_g = mult(flip(inner, G_MS[m]) * BLK, BLK)
-        side_g[0:toks, m * BLK : m * BLK + BLK] = gout[:, pl.ds(owner_g, BLK)]
-        side_n[m * BLK : m * BLK + BLK, 0:toks] = turned_n[flip(inner, N_MS[m])]
 
     def bn_copy(s, k):
         src = bn.at[s, pl.ds(toks if k == 2 else 0, toks), :]
@@ -455,66 +475,77 @@
         z_done(t, g, False).wait_recv()
         z_pass(t, g).start()
 
-    def z_tick(number, kinds=(0, 1)):
-        for step, lag in ((z_first, 0), (z_second, Z_LAG), (z_third, 2 * Z_LAG)):
-            at = number - lag
-            for t in kinds:
-                low = t * Z_PARTS
-                if isinstance(number, int):
-                    if low <= at < low + Z_PARTS:
-                        pl.when(middle)(functools.partial(step, t, at - low))
-                else:
-                    inside = (at >= low) & (at < low + Z_PARTS)
-                    pl.when(middle & inside)(functools.partial(step, t, at - low))
+    def z_move(step, number):
+        for t in (0, 1):
+            at = number - t * Z_PARTS
+            if isinstance(number, int):
+                if 0 <= at < Z_PARTS:
+                    pl.when(middle)(functools.partial(step, t, at))
+            else:
+                pl.when(middle & (at >= 0) & (at < Z_PARTS))(functools.partial(step, t, at))
+
+    def z_tick(number):
+        for step, lag in zip((z_first, z_second, z_third), Z_LAG):
+            z_move(step, number - lag)
 
     per_wide = WIDE // BLK
-
-    wu_load.wait()
-
-    @pl.loop(0, hidden // (2 * WIDE))
+    n_wide = hidden // WIDE
+
+    def hidden_block(w, with_grad):
+        cols = pl.ds(mult(w * WIDE, WIDE), WIDE)
+        for copy in wide_loads(w):
+            copy.wait()
+        up = nn(normed[...], wu[:, cols]) + bup[:, cols]
+        square = up * up
+        tanh = jnp.tanh(GELU_A * up * (1.0 + GELU_B * square))
+        row = lax.broadcasted_iota(jnp.int32, up.shape, 0)
+        active = jnp.where(row < total_len, 0.5 * up * (1.0 + tanh), 0.0).astype(BF16)
+        act[:, cols] = active
+        slope = 0.5 * (1.0 + tanh) + 0.5 * up * (1.0 - tanh * tanh) * (
+            GELU_A * (1.0 + 3.0 * GELU_B * square)
+        )
+        if with_grad:
+            grad = (nt(gout[...], wd[cols, :]) * slope).astype(BF16)
+            gup[:, cols] = grad
+        else:
+            gup[:, cols] = slope.astype(BF16)
+        for part in range(per_wide):
+            c = w * per_wide + part
+            inside = slice(part * BLK, part * BLK + BLK)
+            bg[c, :, 0:toks] = active[:, inside].T
+            if with_grad:
+                bn[c, 0:toks, :] = grad[:, inside]
+        for part in range(per_wide):
+            c = w * per_wide + part
+            for k in (0, 1):
+                bg_copy(c, k).start()
+                if with_grad:
+                    bn_copy(c, k).start()
+
+    @pl.loop(0, n_wide // 2)
     def _(w):
-        blocks = [pl.ds(mult((2 * w + side) * WIDE, WIDE), WIDE) for side in (0, 1)]
-        ups = [nn(normed[...], wu[:, cols]) + bup[:, cols] for cols in blocks]
-        for side, (up, cols) in enumerate(zip(ups, blocks)):
-            square = up * up
-            tanh = jnp.tanh(GELU_A * up * (1.0 + GELU_B * square))
-            row = lax.broadcasted_iota(jnp.int32, up.shape, 0)
-            active = jnp.where(row < total_len, 0.5 * up * (1.0 + tanh), 0.0).astype(BF16)
-            act[:, cols] = active
-            dact[:, cols] = (
-                0.5 * (1.0 + tanh)
-                + 0.5 * up * (1.0 - tanh * tanh) * (GELU_A * (1.0 + 3.0 * GELU_B * square))
-            ).astype(BF16)
-            for part in range(per_wide):
-                c = (2 * w + side) * per_wide + part
-                bg[c, :, 0:toks] = active[:, part * BLK : part * BLK + BLK].T
-        for part in range(2 * per_wide):
-            for k in (0, 1):
-                bg_copy(2 * w * per_wide + part, k).start()
-
-    def side_pass(m):
-        came(bn.at[0, pl.ds(0, 2 * toks), :], side_rs.at[m])
-        for copy_of in (side_g_copy, side_n_copy):
-            copy_of(2, m).start()
-
-    side_pass(0)
+        hidden_block(w, True)
+
+    @pl.loop(n_wide // 2, n_wide)
+    def _(w):
+        hidden_block(w, False)
+
+        @pl.when(w == n_wide // 2)
+        def _():
+            side_pass(0)
 
     def hidden_grad(first, past, shift):
         @pl.loop(first, past)
         def _(w):
+            z_tick(w - first)
             cols = pl.ds(mult(w * WIDE, WIDE), WIDE)
-            grad = (nt(gout[...], wd[cols, :]) * dact[:, cols].astype(F32)).astype(BF16)
-            dact[:, cols] = grad
+            grad = (nt(gout[...], wd[cols, :]) * gup[:, cols].astype(F32)).astype(BF16)
+            gup[:, cols] = grad
             for part in range(per_wide):
                 c = shift + w * per_wide + part
                 bn[c, 0:toks, :] = grad[:, part * BLK : part * BLK + BLK]
                 for k in (0, 1):
                     bn_copy(c, k).start()
-
-    n_wide = hidden // WIDE
-    wd_load.wait()
-    hidden_grad(0, n_wide // 2, 0)
-    side_pass(1)
 
     place_r = lax.broadcasted_iota(jnp.int32, (toks, toks), 0)
     place_c = lax.broadcasted_iota(jnp.int32, (toks, toks), 1)
@@ -570,6 +601,7 @@
     @pl.loop(0, n_att)
     def _(n):
         base_n = n_hid // 2 + 3 * n
+
         for part in range(BLK // 128):
             at = pl.ds(mult(n * BLK + part * 128, 128), 128)
             lanes = slice(part * 128, part * 128 + 128)
@@ -597,14 +629,28 @@
             for kind in range(3):
                 bn_copy(base_n + kind, k).start()
 
+    side_pass(1)
+
     @pl.loop(0, width // WIDE)
     def _(n):
         cols = pl.ds(mult(n * WIDE, WIDE), WIDE)
         zpart[0, :, cols] = (nn(act[...], wd[:, cols]) + nn(att[...], wo[:, cols])).astype(BF16)
-        for part in range(WIDE // piece_cols):
-            g = n * (WIDE // piece_cols) + part
-            z_send([z_far(0, g), z_near(0, g)])
-
+        for part in range(Z_LEAD):
+            g = n * Z_LEAD + part
+            z_send([z_far(0, g)])
+
+            @pl.when(n > 0)
+            def _(g=g):
+                z_send([z_near(0, g - Z_LEAD)])
+
+    for m in (0, 1):
+        for owner in (flip(inner, CORE ^ N_MS[m]), flip(inner, N_MS[m])):
+            turned_n[owner] = normed[:, pl.ds(mult(owner * BLK, BLK), BLK)].T
+        for copy in side_core(m):
+            copy.start()
+        owner_g = mult(flip(inner, G_MS[m]) * BLK, BLK)
+        side_g[0:toks, m * BLK : m * BLK + BLK] = gout[:, pl.ds(owner_g, BLK)]
+        side_n[m * BLK : m * BLK + BLK, 0:toks] = turned_n[flip(inner, N_MS[m])]
     hidden_grad(n_wide // 2, n_wide, 3 * n_att)
 
     vzl[...] = jnp.zeros_like(vzl)
@@ -612,15 +658,22 @@
     @pl.loop(0, width // WIDE)
     def _(n):
         cols = pl.ds(mult(n * WIDE, WIDE), WIDE)
-        grad = nt(dact[...], wu[cols, :])
+        grad = nt(gup[...], wu[cols, :])
         for kind, weight in enumerate((wq, wk, wv)):
             grad = grad + nt(gqkv[:, kind * heads_w : (kind + 1) * heads_w], weight[cols, :])
         zpart[1, :, cols] = grad.astype(BF16)
 
-        for turn, number in ((1, 0), (3, 1)):
-            @pl.when(n == turn)
-            def _(number=number):
-                z_tick(number)
+        @pl.when(n == 0)
+        def _():
+            side_pass(2)
+
+        @pl.when(n == 1)
+        def _():
+            z_tick(2)
+
+        @pl.when(n == 3)
+        def _():
+            z_tick(3)
 
         for part in range(WIDE // 128):
             lanes = slice(part * 128, part * 128 + 128)
@@ -642,7 +695,10 @@
     for mask in range(1, GROUP):
         vd_copy(mask).start()
     for g in range(Z_PARTS):
-        z_send([z_far(1, g), z_near(1, g)])
+        late = Z_PARTS - Z_LEAD + g
+        z_send([z_far(1, g), z_near(late // Z_PARTS, late % Z_PARTS)])
+    for g in range(Z_PARTS - Z_LEAD, Z_PARTS):
+        z_send([z_near(1, g)])
 
     bs_copy = remote(bsum, bsum_r, bs_ss, bs_rs, peer(YBIT))
 
@@ -652,7 +708,13 @@
     def rg_copy(s):
         return remote(rsg_s.at[s], rsg_r.at[s], rg_ss, rg_rs, peer(XBIT))
 
-    came(bn.at[pl.ds(0, 2), :, :], side_rs.at[2])
+    side_came(4, 4)
+
+    @pl.when(end_of_line)
+    def _():
+        for number in (1, 2, 3):
+            side_came(number)
+
     bsum[...] = jnp.zeros_like(bsum)
 
     def vz_copy(step):
@@ -711,7 +773,7 @@
 
     bs_copy.start()
     vec_spread()
-    @pl.loop(Z_TICKS[-1][1] + 1, 2 * Z_PARTS + 2 * Z_LAG)
+    @pl.loop(Z_TICKS[-1][1] + 1, 2 * Z_PARTS + Z_LAG[-1])
     def _(number):
         z_tick(number)
 
@@ -724,8 +786,6 @@
     came(rsn_r, rn_rs)
     came(rsg_r, rg_rs)
 
-    came(side_n.at[pl.ds(0, 2 * BLK), pl.ds(0, 3 * toks)], sn_ss)
-    came(side_g.at[pl.ds(0, 3 * toks), :], sg_ss)
     came(bn.at[:, pl.ds(0, 3 * toks), :], bn_ss)
     came(bg.at[:, :, pl.ds(0, 3 * toks)], bg_ss)
     came(rsn_s, rn_ss)
@@ -736,6 +796,7 @@
 
     @pl.when(end_of_line)
     def _():
+        came(bn.at[pl.ds(0, 2)], side_ss)
         came(zfar, zf_ss)
         came(znear, zn_ss)
         came(zout, ze_rs)
@@ -743,6 +804,7 @@
 
     @pl.when(middle)
     def _():
+        came(bn.at[pl.ds(0, 4)], side_ss)
         came(zmid, zm_ss)
         came(zout, zo_ss)
         came(zmid, zw_ss)
@@ -847,9 +909,9 @@
         vmem((n_vec, BLK), F32),
         vmem((half, width), BF16),
         dma((14,)),
-        dma,
-        dma,
-        dma((3,)),
+        dma((hidden // WIDE, 2)),
+        dma,
+        dma((5,)),
         dma,
         dma,
         dma((n_chunks, 2)),

time: 90.3 us -> 85.6 us (0.948)
  Pallas kernels: 89.5 us -> 84.8 us
    pallas_call x1, Pallas kernels: 85.6 us -> 80.9 us  [layer(): pl.pallas_call(functools.partial(layer_kernel, n_chunks, g_chunks), out_s...]
where the time goes in v6:
time: 85.6 us; the launch traced here: 85.4 us
  Pallas kernels  84.8 us (99%)
    pallas_call x1, Pallas kernels, layer(): pl.pallas_call(functools.partial(layer_kernel, n_chunks, g_chunks), out_s...  80.9 us
    pallas_call x1, Pallas kernels, layer(): pl.pallas_call(functools.partial(write_kernel, hidden // BLK, heads_w //...  3.92 us

profile of v6, /device:TPU:0, one launch (start us, length us, event | category | flops | bytes accessed | tf_op | source)
XLA Modules:
  0.0 85.4 jit_solution(282789283979992506)
XLA Ops:
  0.7 80.9 %shard_map.271 = (bf16[14,1024,256]{2,1,0:T(8,128)(2,1)S(1)}, bf16[10,256,1024]{2,1,0:T(8,128)(2,1)S(1)}, bf16[14,256,256]{2,1,0:T(8,128)(2,1)S(1)}, bf16[10,256...) custom-call(s32[1,4]{1,0:T(1,128)} %lens_h.1, bf16[256,2048]{1,0:T(8,128)(2,1)} %tok_h.1, ...), custom_call_target="tpu_custom_call" | custom-call | tf_op jit(solution)/shard_map/pallas_call | solution.py:941
  81.5 3.9 %shard_map.272 = (bf16[256,2048]{1,0:T(8,128)(2,1)}, bf16[256,2048]{1,0:T(8,128)(2,1)}, f32[256]{0:T(256)}, f32[256]{0:T(256)}, f32[256,512]{1,0:T(8,128)}, /*in...) custom-call(bf16[14,1024,256]{2,1,0:T(8,128)(2,1)S(1)} %get-tuple-el, ...), custom_call_target="tpu_custom_call" | custom-call | tf_op jit(solution)/shard_map/pallas_call | solution.py:996

commit v7 on v6

--- a/solution.py
+++ b/solution.py
@@ -83,13 +83,8 @@
     zout,
     vec_o,
     lens,
-    gain,
-    shift,
-    bq,
-    bk,
-    bv,
-    bup,
-    obias,
+    norm_in,
+    bias_in,
     tok,
     gout,
     normed,
@@ -131,6 +126,7 @@
     bsum_r,
     cot_rows,
     in_sem,
+    tok_sem,
     wide_sem,
     side_ss,
     side_rs,
@@ -203,10 +199,17 @@
         copy.start()
         return copy
 
-    tok_load = load(tok_h, tok, 0)
-    gain_load = load(gain_h, gain, 1)
-    shift_load = load(shift_h, shift, 2)
-    lens_load = load(lens_h, lens, 3)
+    tok_parts = 4
+
+    def tok_load(c):
+        rows = pl.ds(mult(c * (toks // tok_parts), toks // tok_parts), toks // tok_parts)
+        return pltpu.make_async_copy(tok_h.at[rows, :], tok.at[rows, :], tok_sem.at[c])
+
+    for c in range(tok_parts):
+        tok_load(c).start()
+    for at, src in enumerate((gain_h, shift_h)):
+        load(src, norm_in.at[:, pl.ds(at * width, width)], 0)
+    lens_load = load(lens_h, lens, 1)
 
     barrier = pltpu.get_barrier_semaphore()
     for mask in range(1, GROUP):
@@ -214,18 +217,21 @@
     for step in range(1, N_MP):
         pl.semaphore_signal(barrier, inc=1, device_id=zpeer(step), device_id_type=MESH)
 
-    gout_load = load(cot_h, gout, 4)
-    bias_loads = [
-        load(src, dst, 5 + i)
-        for i, (src, dst) in enumerate(
-            ((bup_h, bup), (bq_h, bq), (bk_h, bk), (bv_h, bv), (obias_h, obias))
-        )
-    ]
+    gout_load = load(cot_h, gout, 2)
+    at = 0
+    biases = []
+    for src in (bup_h, bq_h, bk_h, bv_h, obias_h):
+        biases.append(bias_in.at[:, pl.ds(at, src.shape[1])])
+        load(src, biases[-1], 3)
+        at += src.shape[1]
+    bup, bq, bk, bv, obias = biases
+    gain, shift = norm_in.at[:, pl.ds(0, width)], norm_in.at[:, pl.ds(width, width)]
+
     def wide_loads(w):
         part = pl.ds(mult(w * WIDE, WIDE), WIDE)
         return (
-            pltpu.make_async_copy(wu_h.at[:, part], wu.at[:, part], wide_sem.at[w, 0]),
-            pltpu.make_async_copy(wd_h.at[part, :], wd.at[part, :], wide_sem.at[w, 1]),
+            pltpu.make_async_copy(wu_h.at[:, part], wu.at[:, part], wide_sem.at[w]),
+            pltpu.make_async_copy(wd_h.at[part, :], wd.at[part, :], wide_sem.at[w]),
         )
 
     @pl.loop(0, hidden // WIDE)
@@ -234,9 +240,9 @@
             copy.start()
 
     for src, dst in ((wq_h, wq), (wk_h, wk), (wv_h, wv), (wo_h, wo)):
-        load(src, dst, 12)
-    attn_load = pltpu.make_async_copy(wu_h, wu, in_sem.at[12])
-    cot_load = load(cot_h.at[pl.ds(near_rows, half), :], cot_rows, 13)
+        load(src, dst, 4)
+    attn_load = pltpu.make_async_copy(wu_h, wu, in_sem.at[4])
+    cot_load = load(cot_h.at[pl.ds(near_rows, half), :], cot_rows, 5)
 
     def segment_of(place):
         number = jnp.zeros_like(place)
@@ -314,21 +320,31 @@
                 side_came(3)
                 side_send(other_slot, own_part, 3, beside)
 
-    for copy in (tok_load, gain_load, shift_load):
-        copy.wait()
+    lane = lax.broadcasted_iota(jnp.int32, (toks, 128), 1)
+    slot = lax.broadcasted_iota(jnp.int32, (toks, 128), 0)
+    in_head = lane % HD
+    order = (in_head % (ROT // 2)).astype(F32)
+    freq = jnp.exp(order * (-2.0 / ROT * math.log(10000.0)))
+    angle = slot.astype(F32) * freq
+    rot_c[...] = jnp.cos(angle)
+    rot_a[...] = jnp.sin(angle)
+
+    came(norm_in, in_sem.at[0])
     step_rows = 32
 
-    @pl.loop(0, toks // step_rows, unroll=2)
-    def _(r):
-        rows = pl.ds(mult(r * step_rows, step_rows), step_rows)
-        value = tok[rows, :].astype(F32)
-        mean = jnp.sum(value, axis=1, keepdims=True) * (1.0 / width)
-        center = value - mean
-        spread = jnp.sum(center * center, axis=1, keepdims=True) * (1.0 / width)
-        inv = lax.rsqrt(spread + EPSILON)
-        normed[rows, :] = (center * inv * gain[...] + shift[...]).astype(BF16)
-        stat_m[rows, :] = jnp.broadcast_to(mean, (step_rows, 128))
-        stat_i[rows, :] = jnp.broadcast_to(inv, (step_rows, 128))
+    @pl.loop(0, tok_parts)
+    def _(c):
+        tok_load(c).wait()
+        for part in range(toks // tok_parts // step_rows):
+            rows = pl.ds(mult(c * (toks // tok_parts) + part * step_rows, step_rows), step_rows)
+            value = tok[rows, :].astype(F32)
+            mean = jnp.sum(value, axis=1, keepdims=True) * (1.0 / width)
+            center = value - mean
+            spread = jnp.sum(center * center, axis=1, keepdims=True) * (1.0 / width)
+            inv = lax.rsqrt(spread + EPSILON)
+            normed[rows, :] = (center * inv * gain[...] + shift[...]).astype(BF16)
+            stat_m[rows, :] = jnp.broadcast_to(mean, (step_rows, 128))
+            stat_i[rows, :] = jnp.broadcast_to(inv, (step_rows, 128))
 
     pl.semaphore_wait(barrier, GROUP - 1 + N_MP - 1)
     direct_n, direct_g, first_owner = side_direct()
@@ -336,8 +352,9 @@
     turned_n[first_owner] = normed[:, pl.ds(mult(first_owner * BLK, BLK), BLK)].T
     direct_n.start()
 
-    for copy in (lens_load, gout_load, *bias_loads):
-        copy.wait()
+    lens_load.wait()
+    gout_load.wait()
+    came(bias_in, in_sem.at[3])
 
     ends = []
     total_len = 0
@@ -356,6 +373,14 @@
         gout[rows, :] = value.astype(BF16)
         gsum[0:1, :] = gsum[0:1, :] + jnp.sum(value, axis=0, keepdims=True)
 
+    for m in (0, 1):
+        for owner in (flip(inner, CORE ^ N_MS[m]), flip(inner, N_MS[m])):
+            turned_n[owner] = normed[:, pl.ds(mult(owner * BLK, BLK), BLK)].T
+        for copy in side_core(m):
+            copy.start()
+        owner_g = mult(flip(inner, G_MS[m]) * BLK, BLK)
+        side_g[0:toks, m * BLK : m * BLK + BLK] = gout[:, pl.ds(owner_g, BLK)]
+        side_n[m * BLK : m * BLK + BLK, 0:toks] = turned_n[flip(inner, N_MS[m])]
     def bn_copy(s, k):
         src = bn.at[s, pl.ds(toks if k == 2 else 0, toks), :]
         slot_at = (1, 2, 3)[k]
@@ -493,8 +518,7 @@
 
     def hidden_block(w, with_grad):
         cols = pl.ds(mult(w * WIDE, WIDE), WIDE)
-        for copy in wide_loads(w):
-            copy.wait()
+        came(wu.at[:, pl.ds(0, 2 * WIDE)], wide_sem.at[w])
         up = nn(normed[...], wu[:, cols]) + bup[:, cols]
         square = up * up
         tanh = jnp.tanh(GELU_A * up * (1.0 + GELU_B * square))
@@ -547,22 +571,29 @@
                 for k in (0, 1):
                     bn_copy(c, k).start()
 
+    seg_r, _ = segment_of(slot)
+    seg_c, _ = segment_of(lax.broadcasted_iota(jnp.int32, (8, toks), 1))
     place_r = lax.broadcasted_iota(jnp.int32, (toks, toks), 0)
     place_c = lax.broadcasted_iota(jnp.int32, (toks, toks), 1)
-    seg_r, _ = segment_of(place_r)
-    seg_c, _ = segment_of(place_c)
-    allowed = (seg_r == seg_c) & (place_c <= place_r)
+    same = jnp.concatenate([seg_r] * (toks // 128), axis=1) == seg_c[0:1, :]
+    mask = jnp.where(same & (place_c <= place_r), 0.0, -1e30)
     for h in (0, 1):
-        amask[h * toks : h * toks + toks, :] = jnp.where(allowed, 0.0, -1e30)
-
-    lane = lax.broadcasted_iota(jnp.int32, (toks, 128), 1)
-    slot = lax.broadcasted_iota(jnp.int32, (toks, 128), 0)
-    _, start_of = segment_of(slot)
-    in_head = lane % HD
-    order = (in_head % (ROT // 2)).astype(F32)
-    freq = jnp.exp(order * (-2.0 / ROT * math.log(10000.0)))
-    angle = (slot - start_of).astype(F32) * freq
-    cosine, sine = jnp.cos(angle), jnp.sin(angle)
+        amask[h * toks : h * toks + toks, :] = mask
+
+    which = lax.broadcasted_iota(jnp.int32, (8, 128), 0)
+    starts = jnp.zeros((8, 128), jnp.int32)
+    for j, end in enumerate(ends):
+        starts = jnp.where(which == j, end - lens[0, j], starts)
+    turn = starts.astype(F32) * freq[0:8, :]
+    turn_c, turn_s = jnp.cos(turn), jnp.sin(turn)
+    back_c, back_s = jnp.ones((toks, 128), F32), jnp.zeros((toks, 128), F32)
+    for j in range(len(ends)):
+        inside = seg_r == j + 1
+        back_c = jnp.where(inside, turn_c[j : j + 1, :], back_c)
+        back_s = jnp.where(inside, turn_s[j : j + 1, :], back_s)
+    slot_c, slot_s = rot_c[...], rot_a[...]
+    cosine = slot_c * back_c + slot_s * back_s
+    sine = slot_s * back_c - slot_c * back_s
     rot_c[...] = jnp.where(in_head < ROT, cosine, 1.0)
     rot_a[...] = jnp.where(in_head < ROT // 2, -sine, 0.0)
     rot_b[...] = jnp.where((in_head >= ROT // 2) & (in_head < ROT), sine, 0.0)
@@ -643,14 +674,6 @@
             def _(g=g):
                 z_send([z_near(0, g - Z_LEAD)])
 
-    for m in (0, 1):
-        for owner in (flip(inner, CORE ^ N_MS[m]), flip(inner, N_MS[m])):
-            turned_n[owner] = normed[:, pl.ds(mult(owner * BLK, BLK), BLK)].T
-        for copy in side_core(m):
-            copy.start()
-        owner_g = mult(flip(inner, G_MS[m]) * BLK, BLK)
-        side_g[0:toks, m * BLK : m * BLK + BLK] = gout[:, pl.ds(owner_g, BLK)]
-        side_n[m * BLK : m * BLK + BLK, 0:toks] = turned_n[flip(inner, N_MS[m])]
     hidden_grad(n_wide // 2, n_wide, 3 * n_att)
 
     vzl[...] = jnp.zeros_like(vzl)
@@ -679,11 +702,11 @@
             lanes = slice(part * 128, part * 128 + 128)
             at = pl.ds(mult(n * WIDE + part * 128, 128), 128)
             owner = n * per_wide + part * 128 // BLK
-            into = slice(part * 128 % BLK, part * 128 % BLK + 128)
+            half_row = part * 128 % BLK // 128
             piece_of = grad[:, lanes]
             standard = (tok[:, at].astype(F32) - stat_m[...]) * stat_i[...]
-            vzl[owner, 0:1, into] = jnp.sum(piece_of * standard, axis=0, keepdims=True)
-            vzl[owner, 1:2, into] = jnp.sum(piece_of, axis=0, keepdims=True)
+            vzl[owner, half_row : half_row + 1, :] = jnp.sum(piece_of * standard, axis=0, keepdims=True)
+            vzl[owner, 2 + half_row : 3 + half_row, :] = jnp.sum(piece_of, axis=0, keepdims=True)
 
     def vd_copy(mask):
         return remote(
@@ -691,7 +714,9 @@
         )
 
     for owner in range(n_own):
-        vzl[owner, 2:3, :] = gsum[0:1, owner * BLK : owner * BLK + BLK]
+        for half_row in (0, 1):
+            first = owner * BLK + half_row * 128
+            vzl[owner, 4 + half_row : 5 + half_row, :] = gsum[0:1, first : first + 128]
     for mask in range(1, GROUP):
         vd_copy(mask).start()
     for g in range(Z_PARTS):
@@ -779,8 +804,12 @@
 
     bs_copy.wait_recv()
     came(vzr, vz_rs)
-    vec_o[0:8, :] = vz[...] + jnp.sum(vzr[...], axis=0)
-    vec_o[2:3, :] = vz[2:3, :]
+    norm_sums = vz[...] + jnp.sum(vzr[...], axis=0)
+    for half_row in (0, 1):
+        lanes = slice(half_row * 128, half_row * 128 + 128)
+        vec_o[0:1, lanes] = norm_sums[half_row : half_row + 1, :]
+        vec_o[1:2, lanes] = norm_sums[2 + half_row : 3 + half_row, :]
+        vec_o[2:3, lanes] = vz[4 + half_row : 5 + half_row, :]
     vec_o[8:, :] = bsum[...] + bsum_r[...]
 
     came(rsn_r, rn_rs)
@@ -810,7 +839,7 @@
         came(zmid, zw_ss)
 
 
-def write_kernel(n_hid, n_att, bn, bg, rsn, rsg, zout, vec, mixed_h, gtok_h, gain_o, shift_o, gq_h, bq_o, gk_h, bk_o, gv_h, bv_o, go_h, gu_h, bu_o, gd_h, ob_o, stage, sem, zsem):
+def write_kernel(n_hid, n_att, bn, bg, rsn, rsg, zout, vec, mixed_h, gtok_h, gain_o, shift_o, gq_h, bq_o, gk_h, bk_o, gv_h, bv_o, go_h, gu_h, bu_o, gd_h, ob_o, stage, small, sem, zsem, small_sem):
     n_chunks, n_g = bn.shape[0], bg.shape[0]
     toks = zout.shape[1]
     z_outs = [
@@ -830,6 +859,15 @@
     for s in range(n_g):
         out, at = (gd_h, s) if s < n_hid else (go_h, s - n_hid)
         places.append((False, s, out.at[pl.ds(at * BLK, BLK), :]))
+    smalls = [(gain_o, (0,)), (shift_o, (1,)), (ob_o, (2,))]
+    for bias in (bq_o, bk_o, bv_o, bu_o):
+        smalls.append((bias, tuple(8 + s for at, s in sorted((at, s) for s, (b, at) in enumerate(biases) if b is bias))))
+    at = 0
+    for out, rows in smalls:
+        for part, row in enumerate(rows):
+            small[at + part * BLK : at + part * BLK + BLK] = vec[row]
+        pltpu.make_async_copy(small.at[pl.ds(at, len(rows) * BLK)], out, small_sem).start()
+        at += len(rows) * BLK
     copies = []
     for number, (first, s, place) in enumerate(places):
         slot = number
@@ -840,12 +878,9 @@
         stage[slot] = value
         copies.append(pltpu.make_async_copy(stage.at[slot], place, sem))
         copies[number].start()
-    for row, out in enumerate((gain_o, shift_o, ob_o)):
-        out[...] = vec[row]
-    for s, (out, at) in enumerate(biases):
-        out[at * BLK : at * BLK + BLK] = vec[8 + s]
     pltpu.make_async_copy(stage, stage, sem).wait()
     pltpu.make_async_copy(zout, zout, zsem).wait()
+    pltpu.make_async_copy(small, small, small_sem).wait()
 
 
 def layer(tokens, lengths, ln_gain, ln_bias, w_query, b_query, w_key, b_key, w_value, b_value, w_out, w_up, b_up, w_down, out_bias, cotangent):
@@ -861,13 +896,8 @@
     vmem = pltpu.VMEM
     scratch = [
         pltpu.SMEM(lengths.shape, jnp.int32),
-        vmem((1, width), F32),
-        vmem((1, width), F32),
-        vmem((1, heads_w), F32),
-        vmem((1, heads_w), F32),
-        vmem((1, heads_w), F32),
-        vmem((1, hidden), F32),
-        vmem((1, width), F32),
+        vmem((1, 2 * width), F32),
+        vmem((1, hidden + 3 * heads_w + width), F32),
         vmem((toks, width), BF16),
         vmem((toks, width), BF16),
         vmem((toks, width), BF16),
@@ -900,16 +930,17 @@
         vmem((2, half, width), BF16),
         vmem((2, half, width), BF16),
         vmem((2, half, width), BF16),
-        vmem((n_own, 8, BLK), F32),
-        vmem((8, BLK), F32),
-        vmem((N_MP - 1, 8, BLK), F32),
-        vmem((GROUP - 1, 8, BLK), F32),
+        vmem((n_own, 8, 128), F32),
+        vmem((8, 128), F32),
+        vmem((N_MP - 1, 8, 128), F32),
+        vmem((GROUP - 1, 8, 128), F32),
         vmem((8, width), F32),
         vmem((n_vec, BLK), F32),
         vmem((n_vec, BLK), F32),
         vmem((half, width), BF16),
-        dma((14,)),
-        dma((hidden // WIDE, 2)),
+        dma((6,)),
+        dma((4,)),
+        dma((hidden // WIDE,)),
         dma,
         dma((5,)),
         dma,
@@ -974,7 +1005,6 @@
     )
     f32 = lambda *shape: jax.ShapeDtypeStruct(shape, F32)
     low = jax.ShapeDtypeStruct((toks, width), BF16)
-    spec = lambda kind: anyspace if len(kind.shape) == 2 else local
     outs = (
         low,
         low,
@@ -997,8 +1027,14 @@
         functools.partial(write_kernel, hidden // BLK, heads_w // BLK),
         out_shape=outs,
         in_specs=[local] * 6,
-        out_specs=tuple(spec(kind) for kind in outs),
-        scratch_shapes=[vmem((slots, BLK, BLK), F32), dma, dma],
+        out_specs=(anyspace,) * len(outs),
+        scratch_shapes=[
+            vmem((slots, BLK, BLK), F32),
+            vmem((3 * BLK + 3 * heads_w + hidden,), F32),
+            dma,
+            dma,
+            dma,
+        ],
         compiler_params=pltpu.CompilerParams(vmem_limit_bytes=12 * 2**20),
     )(*kept)
 

time: 85.6 us -> 84 us (0.981)
  Pallas kernels: 84.8 us -> 83.2 us
    pallas_call x1, Pallas kernels: 80.9 us -> 79.8 us  [layer(): pl.pallas_call(functools.partial(layer_kernel, n_chunks, g_chunks), out_s...]
where the time goes in v7:
time: 84 us; the launch traced here: 83.8 us
  Pallas kernels  83.2 us (99%)
    pallas_call x1, Pallas kernels, layer(): pl.pallas_call(functools.partial(layer_kernel, n_chunks, g_chunks), out_s...  79.8 us
    pallas_call x1, Pallas kernels, layer(): pl.pallas_call(functools.partial(write_kernel, hidden // BLK, heads_w //...  3.35 us

profile of v7, /device:TPU:0, one launch (start us, length us, event | category | flops | bytes accessed | tf_op | source)
XLA Modules:
  0.0 83.8 jit_solution(5788391608512860792)
XLA Ops:
  0.7 79.8 %shard_map.271 = (bf16[14,1024,256]{2,1,0:T(8,128)(2,1)S(1)}, bf16[10,256,1024]{2,1,0:T(8,128)(2,1)S(1)}, bf16[14,256,256]{2,1,0:T(8,128)(2,1)S(1)}, bf16[10,256...) custom-call(s32[1,4]{1,0:T(1,128)} %lens_h.1, bf16[256,2048]{1,0:T(8,128)(2,1)} %tok_h.1, ...), custom_call_target="tpu_custom_call" | custom-call | tf_op jit(solution)/shard_map/pallas_call | solution.py:972
  80.5 3.3 %shard_map.272 = (bf16[256,2048]{1,0:T(8,128)(2,1)}, bf16[256,2048]{1,0:T(8,128)(2,1)}, f32[256]{0:T(256)}, f32[256]{0:T(256)}, f32[256,512]{1,0:T(8,128)}, /*in...) custom-call(bf16[14,1024,256]{2,1,0:T(8,128)(2,1)S(1)} %get-tuple-el, ...), custom_call_target="tpu_custom_call" | custom-call | tf_op jit(solution)/shard_map/pallas_call | solution.py:1026

commit v8 on v7

--- a/solution.py
+++ b/solution.py
@@ -19,7 +19,7 @@
 Z_PARTS = 8
 Z_LEAD = 2
 Z_LAG = (0, 2, 4)
-Z_TICKS = ((1, 4), (4, 5), (6, 6), (9, 7), (10, 8), (11, 9), (12, 10), (13, 11))
+Z_TICKS = ((1, 4), (3, 5), (6, 6), (8, 7), (9, 8), (10, 9), (11, 10), (12, 11), (13, 12))
 F32 = jnp.float32
 BF16 = jnp.bfloat16
 MESH = pl.DeviceIdType.MESH
@@ -123,6 +123,7 @@
     vdr,
     gsum,
     bsum,
+    bsum_s,
     bsum_r,
     cot_rows,
     in_sem,
@@ -288,37 +289,39 @@
         owner_g = flip(inner, CORE ^ G_MS[m])
         source_g = cot_h.at[:, pl.ds(mult(owner_g * BLK, BLK), BLK)]
         return (
-            remote(turned_n.at[owner_n], place_n, side_ss, side_rs.at[4], peer(CORE)),
-            remote(source_g, place_g, side_ss, side_rs.at[4], peer(CORE)),
-        )
-
-    def side_send(slot_at, m, number, where):
-        for place in side_places(slot_at, m):
-            remote(place, place, side_ss, side_rs.at[number], where).start()
-
-    def side_came(number, blocks=2):
-        came(bn.at[0, pl.ds(0, blocks * toks), :], side_rs.at[number])
-
-    def side_pass(stage):
-        if stage == 0:
-            side_came(0)
-            side_send(own_slot, own_part, 1, beside)
+            remote(turned_n.at[owner_n], place_n, side_ss, side_rs.at[1], peer(CORE)),
+            remote(source_g, place_g, side_ss, side_rs.at[1], peer(CORE)),
+        )
+
+    def side_send(kind, slot_at, m, number, where):
+        place = side_places(slot_at, m)[kind]
+        remote(place, place, side_ss, side_rs.at[2 * number + kind], where).start()
+
+    def side_came(kind, number):
+        came(bn.at[0, pl.ds(0, toks), :], side_rs.at[2 * number + kind])
+
+    def side_first():
+        came(bn.at[0, pl.ds(0, 2 * toks), :], side_rs.at[0])
+        for kind in (0, 1):
+            side_send(kind, own_slot, own_part, 1, beside)
 
             @pl.when(middle)
             def _():
-                side_send(own_slot, own_part, 2, across)
-        elif stage == 1:
-            @pl.when(middle)
-            def _():
-                side_came(1)
-                side_send(own_slot, 1 - own_part, 3, across)
-                side_came(2)
-                side_send(other_slot, 1 - own_part, 2, beside)
-        else:
-            @pl.when(middle)
-            def _():
-                side_came(3)
-                side_send(other_slot, own_part, 3, beside)
+                side_send(kind, own_slot, own_part, 2, across)
+
+    def side_relay(kind):
+        @pl.when(middle)
+        def _():
+            side_came(kind, 1)
+            side_send(kind, own_slot, 1 - own_part, 3, across)
+            side_came(kind, 2)
+            side_send(kind, other_slot, 1 - own_part, 2, beside)
+
+    def side_out(kind):
+        @pl.when(middle)
+        def _():
+            side_came(kind, 3)
+            side_send(kind, other_slot, own_part, 3, beside)
 
     lane = lax.broadcasted_iota(jnp.int32, (toks, 128), 1)
     slot = lax.broadcasted_iota(jnp.int32, (toks, 128), 0)
@@ -556,11 +559,19 @@
 
         @pl.when(w == n_wide // 2)
         def _():
-            side_pass(0)
+            side_first()
 
     def hidden_grad(first, past, shift):
         @pl.loop(first, past)
         def _(w):
+            @pl.when(w == first)
+            def _():
+                side_out(0)
+
+            @pl.when(w == first + 1)
+            def _():
+                side_out(1)
+
             z_tick(w - first)
             cols = pl.ds(mult(w * WIDE, WIDE), WIDE)
             grad = (nt(gout[...], wd[cols, :]) * gup[:, cols].astype(F32)).astype(BF16)
@@ -632,6 +643,10 @@
     @pl.loop(0, n_att)
     def _(n):
         base_n = n_hid // 2 + 3 * n
+
+        @pl.when(n == n_att - 1)
+        def _():
+            side_relay(0)
 
         for part in range(BLK // 128):
             at = pl.ds(mult(n * BLK + part * 128, 128), 128)
@@ -660,7 +675,7 @@
             for kind in range(3):
                 bn_copy(base_n + kind, k).start()
 
-    side_pass(1)
+    side_relay(1)
 
     @pl.loop(0, width // WIDE)
     def _(n):
@@ -685,10 +700,6 @@
         for kind, weight in enumerate((wq, wk, wv)):
             grad = grad + nt(gqkv[:, kind * heads_w : (kind + 1) * heads_w], weight[cols, :])
         zpart[1, :, cols] = grad.astype(BF16)
-
-        @pl.when(n == 0)
-        def _():
-            side_pass(2)
 
         @pl.when(n == 1)
         def _():
@@ -725,7 +736,7 @@
     for g in range(Z_PARTS - Z_LEAD, Z_PARTS):
         z_send([z_near(1, g)])
 
-    bs_copy = remote(bsum, bsum_r, bs_ss, bs_rs, peer(YBIT))
+    bs_copy = remote(bsum_s, bsum_r, bs_ss, bs_rs, peer(YBIT))
 
     def rn_copy(s):
         return remote(rsn_s.at[s], rsn_r.at[s], rn_ss, rn_rs, peer(YBIT))
@@ -733,12 +744,13 @@
     def rg_copy(s):
         return remote(rsg_s.at[s], rsg_r.at[s], rg_ss, rg_rs, peer(XBIT))
 
-    side_came(4, 4)
+    came(bn.at[0], side_rs.at[1])
 
     @pl.when(end_of_line)
     def _():
         for number in (1, 2, 3):
-            side_came(number)
+            for kind in (0, 1):
+                side_came(kind, number)
 
     bsum[...] = jnp.zeros_like(bsum)
 
@@ -796,6 +808,7 @@
             tick = jnp.where(s == turn, number, tick)
         z_tick(tick)
 
+    bsum_s[...] = bsum[...].astype(BF16)
     bs_copy.start()
     vec_spread()
     @pl.loop(Z_TICKS[-1][1] + 1, 2 * Z_PARTS + Z_LAG[-1])
@@ -810,7 +823,7 @@
         vec_o[0:1, lanes] = norm_sums[half_row : half_row + 1, :]
         vec_o[1:2, lanes] = norm_sums[2 + half_row : 3 + half_row, :]
         vec_o[2:3, lanes] = vz[4 + half_row : 5 + half_row, :]
-    vec_o[8:, :] = bsum[...] + bsum_r[...]
+    vec_o[8:, :] = bsum[...] + bsum_r[...].astype(F32)
 
     came(rsn_r, rn_rs)
     came(rsg_r, rg_rs)
@@ -936,13 +949,14 @@
         vmem((GROUP - 1, 8, 128), F32),
         vmem((8, width), F32),
         vmem((n_vec, BLK), F32),
-        vmem((n_vec, BLK), F32),
+        vmem((n_vec, BLK), BF16),
+        vmem((n_vec, BLK), BF16),
         vmem((half, width), BF16),
         dma((6,)),
         dma((4,)),
         dma((hidden // WIDE,)),
         dma,
-        dma((5,)),
+        dma((8,)),
         dma,
         dma,
         dma((n_chunks, 2)),

time: 84 us -> 83.6 us (level)
  no operation moved by 1% of the time
where the time goes in v8:
time: 83.6 us; the launch traced here: 83.5 us
  Pallas kernels  82.8 us (99%)
    pallas_call x1, Pallas kernels, layer(): pl.pallas_call(functools.partial(layer_kernel, n_chunks, g_chunks), out_s...  79.5 us
    pallas_call x1, Pallas kernels, layer(): pl.pallas_call(functools.partial(write_kernel, hidden // BLK, heads_w //...  3.35 us

profile of v8, /device:TPU:0, one launch (start us, length us, event | category | flops | bytes accessed | tf_op | source)
XLA Modules:
  0.0 83.5 jit_solution(6577491291542192315)
XLA Ops:
  0.7 79.5 %shard_map.271 = (bf16[14,1024,256]{2,1,0:T(8,128)(2,1)S(1)}, bf16[10,256,1024]{2,1,0:T(8,128)(2,1)S(1)}, bf16[14,256,256]{2,1,0:T(8,128)(2,1)S(1)}, bf16[10,256...) custom-call(s32[1,4]{1,0:T(1,128)} %lens_h.1, bf16[256,2048]{1,0:T(8,128)(2,1)} %tok_h.1, ...), custom_call_target="tpu_custom_call" | custom-call | tf_op jit(solution)/shard_map/pallas_call | solution.py:986
  80.1 3.3 %shard_map.272 = (bf16[256,2048]{1,0:T(8,128)(2,1)}, bf16[256,2048]{1,0:T(8,128)(2,1)}, f32[256]{0:T(256)}, f32[256]{0:T(256)}, f32[256,512]{1,0:T(8,128)}, /*in...) custom-call(bf16[14,1024,256]{2,1,0:T(8,128)(2,1)S(1)} %get-tuple-el, ...), custom_call_target="tpu_custom_call" | custom-call | tf_op jit(solution)/shard_map/pallas_call | solution.py:1040

commit v9 on v8

--- a/solution.py
+++ b/solution.py
@@ -15,7 +15,6 @@
 CORE, XBIT, YBIT = 1, 2, 4
 BLK = 256
 WIDE = 512
-N_MP = 4
 Z_PARTS = 8
 Z_LEAD = 2
 Z_LAG = (0, 2, 4)
@@ -119,6 +118,8 @@
     zmid,
     vzl,
     vz,
+    vz_pair,
+    norm_sums,
     vzr,
     vdr,
     gsum,
@@ -182,9 +183,6 @@
     near_rows = mult(side_of_line * half, half)
     far_rows = mult((1 - side_of_line) * half, half)
 
-    def zpeer(step):
-        return (dp, lax.rem(zed + step, N_MP))
-
     def remote(src, dst, ssem, rsem, where):
         return pltpu.make_async_remote_copy(
             src_ref=src,
@@ -215,8 +213,11 @@
     barrier = pltpu.get_barrier_semaphore()
     for mask in range(1, GROUP):
         pl.semaphore_signal(barrier, inc=1, device_id=peer(mask), device_id_type=MESH)
-    for step in range(1, N_MP):
-        pl.semaphore_signal(barrier, inc=1, device_id=zpeer(step), device_id_type=MESH)
+    pl.semaphore_signal(barrier, inc=1, device_id=beside, device_id_type=MESH)
+
+    @pl.when(middle)
+    def _():
+        pl.semaphore_signal(barrier, inc=1, device_id=across, device_id_type=MESH)
 
     gout_load = load(cot_h, gout, 2)
     at = 0
@@ -349,7 +350,14 @@
             stat_m[rows, :] = jnp.broadcast_to(mean, (step_rows, 128))
             stat_i[rows, :] = jnp.broadcast_to(inv, (step_rows, 128))
 
-    pl.semaphore_wait(barrier, GROUP - 1 + N_MP - 1)
+    @pl.when(end_of_line)
+    def _():
+        pl.semaphore_wait(barrier, GROUP)
+
+    @pl.when(middle)
+    def _():
+        pl.semaphore_wait(barrier, GROUP + 1)
+
     direct_n, direct_g, first_owner = side_direct()
     direct_g.start()
     turned_n[first_owner] = normed[:, pl.ds(mult(first_owner * BLK, BLK), BLK)].T
@@ -677,17 +685,19 @@
 
     side_relay(1)
 
-    @pl.loop(0, width // WIDE)
+    def branches(cols):
+        zpart[0, :, cols] = (nn(act[...], wd[:, cols]) + nn(att[...], wo[:, cols])).astype(BF16)
+
+    for g in range(Z_LEAD):
+        branches(pl.ds(g * piece_cols, piece_cols))
+        z_send([z_far(0, g)])
+
+    @pl.loop(1, width // WIDE)
     def _(n):
-        cols = pl.ds(mult(n * WIDE, WIDE), WIDE)
-        zpart[0, :, cols] = (nn(act[...], wd[:, cols]) + nn(att[...], wo[:, cols])).astype(BF16)
+        branches(pl.ds(mult(n * WIDE, WIDE), WIDE))
         for part in range(Z_LEAD):
             g = n * Z_LEAD + part
-            z_send([z_far(0, g)])
-
-            @pl.when(n > 0)
-            def _(g=g):
-                z_send([z_near(0, g - Z_LEAD)])
+            z_send([z_far(0, g), z_near(0, g - Z_LEAD)])
 
     hidden_grad(n_wide // 2, n_wide, 3 * n_att)
 
@@ -754,14 +764,30 @@
 
     bsum[...] = jnp.zeros_like(bsum)
 
-    def vz_copy(step):
-        return remote(vz, vzr.at[step - 1], vz_ss, vz_rs, zpeer(step))
+    def vz_copy(src, i, where):
+        return remote(src, vzr.at[i], vz_ss, vz_rs.at[i], where)
 
     def vec_spread():
         came(vdr, vd_rs)
         vz[...] = vzl[inner] + jnp.sum(vdr[...], axis=0)
-        for step in range(1, N_MP):
-            vz_copy(step).start()
+
+        @pl.when(end_of_line)
+        def _():
+            vz_copy(vz, 0, beside).start()
+
+    def vec_pair():
+        @pl.when(middle)
+        def _():
+            came(vz, vz_rs.at[0])
+            vz_pair[...] = vz[...] + vzr[0]
+            vz_copy(vz_pair, 1, across).start()
+
+    def vec_back():
+        @pl.when(middle)
+        def _():
+            came(vz, vz_rs.at[1])
+            norm_sums[...] = vz_pair[...] + vzr[1]
+            vz_copy(norm_sums, 0, beside).start()
 
     side_n[2 * BLK :, :] = jnp.ones((16, 4 * toks), BF16)
 
@@ -813,11 +839,21 @@
     vec_spread()
     @pl.loop(Z_TICKS[-1][1] + 1, 2 * Z_PARTS + Z_LAG[-1])
     def _(number):
+        @pl.when(number == 2 * Z_PARTS)
+        def _():
+            vec_pair()
+
         z_tick(number)
 
+    vec_back()
+
     bs_copy.wait_recv()
-    came(vzr, vz_rs)
-    norm_sums = vz[...] + jnp.sum(vzr[...], axis=0)
+
+    @pl.when(end_of_line)
+    def _():
+        came(vz, vz_rs.at[0])
+        norm_sums[...] = vzr[0]
+
     for half_row in (0, 1):
         lanes = slice(half_row * 128, half_row * 128 + 128)
         vec_o[0:1, lanes] = norm_sums[half_row : half_row + 1, :]
@@ -832,13 +868,13 @@
     came(bg.at[:, :, pl.ds(0, 3 * toks)], bg_ss)
     came(rsn_s, rn_ss)
     came(rsg_s, rg_ss)
-    came(vzr, vz_ss)
     came(vdr, vd_ss)
     bs_copy.wait_send()
 
     @pl.when(end_of_line)
     def _():
         came(bn.at[pl.ds(0, 2)], side_ss)
+        came(vz, vz_ss)
         came(zfar, zf_ss)
         came(znear, zn_ss)
         came(zout, ze_rs)
@@ -847,6 +883,7 @@
     @pl.when(middle)
     def _():
         came(bn.at[pl.ds(0, 4)], side_ss)
+        came(vzr, vz_ss)
         came(zmid, zm_ss)
         came(zout, zo_ss)
         came(zmid, zw_ss)
@@ -945,7 +982,9 @@
         vmem((2, half, width), BF16),
         vmem((n_own, 8, 128), F32),
         vmem((8, 128), F32),
-        vmem((N_MP - 1, 8, 128), F32),
+        vmem((8, 128), F32),
+        vmem((8, 128), F32),
+        vmem((2, 8, 128), F32),
         vmem((GROUP - 1, 8, 128), F32),
         vmem((8, width), F32),
         vmem((n_vec, BLK), F32),
@@ -974,7 +1013,7 @@
         dma,
         dma,
         dma,
-        dma,
+        dma((2,)),
         dma,
         dma,
         dma,

time: 83.6 us -> 82.5 us (0.987)
  Pallas kernels: 82.8 us -> 81.7 us
    pallas_call x1, Pallas kernels: 79.5 us -> 78.3 us  [layer(): pl.pallas_call(functools.partial(layer_kernel, n_chunks, g_chunks), out_s...]
where the time goes in v9:
time: 82.5 us; the launch traced here: 82.3 us
  Pallas kernels  81.7 us (99%)
    pallas_call x1, Pallas kernels, layer(): pl.pallas_call(functools.partial(layer_kernel, n_chunks, g_chunks), out_s...  78.3 us
    pallas_call x1, Pallas kernels, layer(): pl.pallas_call(functools.partial(write_kernel, hidden // BLK, heads_w //...  3.35 us

profile of v9, /device:TPU:0, one launch (start us, length us, event | category | flops | bytes accessed | tf_op | source)
XLA Modules:
  0.0 82.3 jit_solution(620381987489432854)
XLA Ops:
  0.7 78.3 %shard_map.271 = (bf16[14,1024,256]{2,1,0:T(8,128)(2,1)S(1)}, bf16[10,256,1024]{2,1,0:T(8,128)(2,1)S(1)}, bf16[14,256,256]{2,1,0:T(8,128)(2,1)S(1)}, bf16[10,256...) custom-call(s32[1,4]{1,0:T(1,128)} %lens_h.1, bf16[256,2048]{1,0:T(8,128)(2,1)} %tok_h.1, ...), custom_call_target="tpu_custom_call" | custom-call | tf_op jit(solution)/shard_map/pallas_call | solution.py:1025
  79.0 3.3 %shard_map.272 = (bf16[256,2048]{1,0:T(8,128)(2,1)}, bf16[256,2048]{1,0:T(8,128)(2,1)}, f32[256]{0:T(256)}, f32[256]{0:T(256)}, f32[256,512]{1,0:T(8,128)}, /*in...) custom-call(bf16[14,1024,256]{2,1,0:T(8,128)(2,1)S(1)} %get-tuple-el, ...), custom_call_target="tpu_custom_call" | custom-call | tf_op jit(solution)/shard_map/pallas_call | solution.py:1079

commit v10 on v9

--- a/solution.py
+++ b/solution.py
@@ -18,7 +18,7 @@
 Z_PARTS = 8
 Z_LEAD = 2
 Z_LAG = (0, 2, 4)
-Z_TICKS = ((1, 4), (3, 5), (6, 6), (8, 7), (9, 8), (10, 9), (11, 10), (12, 11), (13, 12))
+Z_TICKS = ((1, 4), (3, 5), (5, 6), (7, 7), (8, 8), (9, 9), (10, 10), (11, 11), (12, 12), (13, 13))
 F32 = jnp.float32
 BF16 = jnp.bfloat16
 MESH = pl.DeviceIdType.MESH

time: 82.5 us -> 82.4 us (level)
  no operation moved by 1% of the time
where the time goes in v10:
time: 82.4 us; the launch traced here: 82.3 us
  Pallas kernels  81.6 us (99%)
    pallas_call x1, Pallas kernels, layer(): pl.pallas_call(functools.partial(layer_kernel, n_chunks, g_chunks), out_s...  78.3 us
    pallas_call x1, Pallas kernels, layer(): pl.pallas_call(functools.partial(write_kernel, hidden // BLK, heads_w //...  3.35 us

profile of v10, /device:TPU:0, one launch (start us, length us, event | category | flops | bytes accessed | tf_op | source)
XLA Modules:
  0.0 82.3 jit_solution(11487574370067778247)
XLA Ops:
  0.7 78.3 %shard_map.271 = (bf16[14,1024,256]{2,1,0:T(8,128)(2,1)S(1)}, bf16[10,256,1024]{2,1,0:T(8,128)(2,1)S(1)}, bf16[14,256,256]{2,1,0:T(8,128)(2,1)S(1)}, bf16[10,256...) custom-call(s32[1,4]{1,0:T(1,128)} %lens_h.1, bf16[256,2048]{1,0:T(8,128)(2,1)} %tok_h.1, ...), custom_call_target="tpu_custom_call" | custom-call | tf_op jit(solution)/shard_map/pallas_call | solution.py:1025
  78.9 3.3 %shard_map.272 = (bf16[256,2048]{1,0:T(8,128)(2,1)}, bf16[256,2048]{1,0:T(8,128)(2,1)}, f32[256]{0:T(256)}, f32[256]{0:T(256)}, f32[256,512]{1,0:T(8,128)}, /*in...) custom-call(bf16[14,1024,256]{2,1,0:T(8,128)(2,1)S(1)} %get-tuple-el, ...), custom_call_target="tpu_custom_call" | custom-call | tf_op jit(solution)/shard_map/pallas_call | solution.py:1079

commit v11 on v10

--- a/solution.py
+++ b/solution.py
@@ -375,7 +375,7 @@
 
     gsum[...] = jnp.zeros_like(gsum)
 
-    @pl.loop(0, toks // step_rows)
+    @pl.loop(0, toks // step_rows, unroll=2)
     def _(r):
         first = r * step_rows
         rows = pl.ds(mult(first, step_rows), step_rows)

time: 82.4 us -> 82.4 us (level)
  no operation moved by 1% of the time
where the time goes in v11:
time: 82.4 us; the launch traced here: 82.3 us
  Pallas kernels  81.6 us (99%)
    pallas_call x1, Pallas kernels, layer(): pl.pallas_call(functools.partial(layer_kernel, n_chunks, g_chunks), out_s...  78.3 us
    pallas_call x1, Pallas kernels, layer(): pl.pallas_call(functools.partial(write_kernel, hidden // BLK, heads_w //...  3.35 us

profile of v11, /device:TPU:0, one launch (start us, length us, event | category | flops | bytes accessed | tf_op | source)
XLA Modules:
  0.0 82.3 jit_solution(11115142268737011076)
XLA Ops:
  0.7 78.3 %shard_map.271 = (bf16[14,1024,256]{2,1,0:T(8,128)(2,1)S(1)}, bf16[10,256,1024]{2,1,0:T(8,128)(2,1)S(1)}, bf16[14,256,256]{2,1,0:T(8,128)(2,1)S(1)}, bf16[10,256...) custom-call(s32[1,4]{1,0:T(1,128)} %lens_h.1, bf16[256,2048]{1,0:T(8,128)(2,1)} %tok_h.1, ...), custom_call_target="tpu_custom_call" | custom-call | tf_op jit(solution)/shard_map/pallas_call | solution.py:1025
  78.9 3.3 %shard_map.272 = (bf16[256,2048]{1,0:T(8,128)(2,1)}, bf16[256,2048]{1,0:T(8,128)(2,1)}, f32[256]{0:T(256)}, f32[256]{0:T(256)}, f32[256,512]{1,0:T(8,128)}, /*in...) custom-call(bf16[14,1024,256]{2,1,0:T(8,128)(2,1)S(1)} %get-tuple-el, ...), custom_call_target="tpu_custom_call" | custom-call | tf_op jit(solution)/shard_map/pallas_call | solution.py:1079
